TPU v7x, 32 devices: a whole 2x2x4 slice. The times are simulated.
32 devices in a mesh: grp: 2 (over x), res: 16 (over z, y, core).
Axes of the slice: x: 2, y: 2, z: 4, core: 2. Of those that a mesh axis runs over, the one named last changes fastest.
Arguments:
- alignment_embedding: bfloat16 [256, 128, 256], P('grp', 'res'), parts along dimension 0, may hold values from -6 to 6
- coupling_embedding: bfloat16 [128, 256, 128], P('res', 'grp'), parts along dimension 1, may hold values from -6 to 6
- query_key_matrix: bfloat16 [256, 1024], replicated, may hold values from -0.375 to 0.375
- coupling_logit_matrix: bfloat16 [128, 8], replicated, may hold values from -8 to 8
- focus_final_matrix: bfloat16 [256, 256], replicated, may hold values from -3 to 3
- tensor_average_matrix: bfloat16 [256, 64], replicated, may hold values from -0.375 to 0.375
- tensor_average_final: bfloat16 [1024, 128], replicated, may hold values from -2 to 2
- trilateral_entry_matrix: bfloat16 [2, 128, 640], replicated, may hold values from -0.5 to 0.5
- trilateral_exit_matrix: bfloat16 [2, 128, 128], replicated, may hold values from -0.5 to 0.5
Outputs:
- alignment_mixed: bfloat16 [256, 128, 256], P('grp', 'res'), parts along dimension 0
- coupling_refreshed: bfloat16 [128, 256, 128], P('res', 'grp'), parts along dimension 1
There are 2 independent parts, one for each index of `grp`. A program takes and returns all parts, laid end to end along the dimension named above; an argument that names none is the same for every part. Nothing has to cross between parts.
All inputs are finite; a program needn't handle non-finite values.
Results may differ from a plain program's by a relative error of at most 0.018.
The roundings to bfloat16 on the way count: a program that leaves them out, or rounds other values in their place, can miss the bound.
Values may be sent and summed in bfloat16 or wider, within the bound.
No kernel may reach another device: no remote copies, remote signals or barrier semaphores. Data moves between devices by JAX's collectives and lax.ppermute only.
A program may use at most 128 MiB of HBM per device.

v0:
```python
import jax
import jax.numpy as jnp
from jax import lax
from jax.sharding import PartitionSpec as P


def standardise_entries(values_in, axis_num):
    values_in = values_in.astype(jnp.float32)
    centred = values_in - jnp.mean(values_in, axis=axis_num, keepdims=True)
    spread = jnp.mean(centred * centred, axis=axis_num, keepdims=True)
    return centred * lax.rsqrt(spread + 1e-05)


def attend(queries, key_rows, value_rows, bias_terms, score_scale):
    scores = (
        jnp.einsum("bid,bjd->bij", queries, key_rows, preferred_element_type=jnp.float32)
        * score_scale
        + bias_terms
    )
    row_max = jnp.max(scores, axis=-1, keepdims=True)
    weights = jnp.exp(scores - row_max)
    weights = (weights / jnp.sum(weights, axis=-1, keepdims=True)).astype(jnp.bfloat16)
    return jnp.einsum(
        "bij,bjd->bid", weights, value_rows, preferred_element_type=jnp.float32
    ).astype(jnp.bfloat16)


def triangle(pair_prev, weight_in, weight_out, contraction):
    local_strands, total_res, pair_width = pair_prev.shape
    res_count = lax.axis_size("res")
    channel_share = pair_width // res_count
    normed = standardise_entries(pair_prev, -1).astype(jnp.bfloat16)
    weight_five = weight_in.reshape(pair_width, 5, pair_width)
    mapped_strands = jnp.einsum(
        "rnc,ctf->tfrn", normed, weight_five[:, :4], preferred_element_type=jnp.float32
    )
    left_edge = (jax.nn.sigmoid(mapped_strands[0]) * mapped_strands[1]).astype(jnp.bfloat16)
    right_edge = (jax.nn.sigmoid(mapped_strands[2]) * mapped_strands[3]).astype(jnp.bfloat16)
    gate_pair = jax.nn.sigmoid(
        jnp.einsum("rnc,cf->rnf", normed, weight_five[:, 4], preferred_element_type=jnp.float32)
    )
    sending = (
        left_edge.reshape(res_count, channel_share, local_strands, total_res),
        right_edge.reshape(res_count, channel_share, local_strands, total_res),
    )
    product = jnp.einsum(
        contraction,
        lax.all_to_all(sending[0], "res", split_axis=0, concat_axis=2, tiled=True),
        lax.all_to_all(sending[1], "res", split_axis=0, concat_axis=2, tiled=True),
        preferred_element_type=jnp.float32,
    ).astype(jnp.bfloat16)
    item_count = product.shape[1]
    split_rows = product.reshape(1, item_count, res_count, local_strands, total_res)
    gathered_edges = lax.all_to_all(split_rows, "res", split_axis=2, concat_axis=0, tiled=True)
    gathered_edges = gathered_edges.reshape(pair_width, local_strands, total_res)
    edge_norm = standardise_entries(gathered_edges, 0).astype(jnp.bfloat16)
    update = jnp.einsum("crn,cf->rnf", edge_norm, weight_out, preferred_element_type=jnp.float32)
    return (pair_prev.astype(jnp.float32) + gate_pair * update).astype(jnp.bfloat16)


def body(
    alignment_embedding,
    coupling_embedding,
    query_key_matrix,
    coupling_logit_matrix,
    focus_final_matrix,
    tensor_average_matrix,
    tensor_average_final,
    trilateral_entry_matrix,
    trilateral_exit_matrix,
):
    chain_tally, local_strands, alignment_depth = alignment_embedding.shape
    res_count = lax.axis_size("res")
    focus_group_tally = coupling_logit_matrix.shape[1]
    subspace_width = query_key_matrix.shape[1] // (4 * focus_group_tally)
    score_scale = subspace_width ** (-0.5)
    focus_probabilities = query_key_matrix.reshape(
        alignment_depth, 4, focus_group_tally, subspace_width
    )
    alignment_standardised = standardise_entries(alignment_embedding, -1).astype(jnp.bfloat16)
    pair_norm = standardise_entries(coupling_embedding, -1).astype(jnp.bfloat16)
    bias_rows = jnp.einsum(
        "rnc,ch->hrn", pair_norm, coupling_logit_matrix, preferred_element_type=jnp.float32
    )
    aligned_strands = lax.all_to_all(
        alignment_standardised, "res", split_axis=0, concat_axis=1, tiled=True
    )
    mapped_strands = jnp.einsum(
        "snc,cthd->tshnd",
        aligned_strands,
        focus_probabilities[:, :3],
        preferred_element_type=jnp.float32,
    ).astype(jnp.bfloat16)
    full_bias = lax.all_gather(bias_rows, "res", axis=1, tiled=True)

    def one_sequence(operands):
        return attend(operands[0], operands[1], operands[2], full_bias, score_scale)

    mixed_signals = lax.map(one_sequence, (mapped_strands[0], mapped_strands[1], mapped_strands[2]))
    per_device = mixed_signals.shape[0]
    returned = lax.all_to_all(
        mixed_signals.reshape(
            per_device, focus_group_tally, res_count, local_strands, subspace_width
        ),
        "res",
        split_axis=2,
        concat_axis=0,
        tiled=True,
    )
    subspace_results = returned.reshape(
        chain_tally, focus_group_tally, local_strands, subspace_width
    )
    array_layout = "shrd"
    alignment_sigmoid_factors = jax.nn.sigmoid(
        jnp.einsum(
            "src,chd->" + array_layout,
            alignment_standardised,
            focus_probabilities[:, 3],
            preferred_element_type=jnp.float32,
        )
    )
    sigmoid_scaled_result = (
        subspace_results.astype(jnp.float32) * alignment_sigmoid_factors
    ).astype(jnp.bfloat16)
    alignment_increment = jnp.einsum(
        array_layout + ",hdc->src",
        sigmoid_scaled_result,
        focus_final_matrix.reshape(focus_group_tally, subspace_width, alignment_depth),
        preferred_element_type=jnp.float32,
    )
    alignment_mixed = (alignment_embedding.astype(jnp.float32) + alignment_increment).astype(
        jnp.bfloat16
    )
    tensor_depth = tensor_average_matrix.shape[1] // 2
    tensor_average_scaled = standardise_entries(alignment_mixed, -1).astype(jnp.bfloat16)
    flank_mapping = jnp.einsum(
        "src,ctk->trsk",
        tensor_average_scaled,
        tensor_average_matrix.reshape(alignment_depth, 2, tensor_depth),
        preferred_element_type=jnp.float32,
    ).astype(jnp.bfloat16)
    left_side = flank_mapping[0]
    right_flat = flank_mapping[1].reshape(local_strands, chain_tally * tensor_depth)
    piece = lax.all_gather(right_flat, "res", axis=0, tiled=True)
    col_count = piece.shape[0]
    right_piece = piece.reshape(col_count, chain_tally, tensor_depth)

    def one_row(source_embedding_line):
        tensor_accumulated = jnp.einsum(
            "sc,jse->jce", source_embedding_line, right_piece, preferred_element_type=jnp.float32
        ) * (1.0 / chain_tally)
        tensor_accumulated = tensor_accumulated.astype(jnp.bfloat16).reshape(
            col_count, tensor_depth * tensor_depth
        )
        return jnp.dot(tensor_accumulated, tensor_average_final, preferred_element_type=jnp.float32)

    opm_update = lax.map(one_row, left_side)
    pair_mid = (coupling_embedding.astype(jnp.float32) + opm_update).astype(jnp.bfloat16)
    pair_tri = triangle(
        pair_mid, trilateral_entry_matrix[0], trilateral_exit_matrix[0], "zcik,zcjk->zcij"
    )
    coupling_refreshed = triangle(
        pair_tri, trilateral_entry_matrix[1], trilateral_exit_matrix[1], "zcki,zckj->zcij"
    )
    return (alignment_mixed, coupling_refreshed)


def solution(mesh):
    return jax.shard_map(
        body,
        mesh=mesh,
        in_specs=(P("grp", "res", None), P("res", "grp", None), P(), P(), P(), P(), P(), P(), P()),
        out_specs=(P("grp", "res", None), P("res", "grp", None)),
        check_vma=False,
    )
```

profile of v0, /device:TPU:0, one launch (start us, length us, event | category | flops | bytes accessed | tf_op | source)
XLA Modules:
  0.0 238.3 jit_solution(7442636782129231384)
XLA Ops:
  7.2 1.3 convert_reduce_fusion
  8.5 1.4 fusion.53
  10.0 1.4 fusion.54
  11.3 1.1 copy.75
  12.4 7.5 %all-to-all-start = ((bf16[128,8,256]{2,1,0:T(8,128)(2,1)}), bf16[128,8,256]{2,1,0:T(8,128)(2,1)S(1)}, u32[]{:S(2)}, u32[]{:S(2)}) async-start(bf16[128,8,256]{2,1,0:T(8,128)(2,1)} %copy.75), calls=%async_computation | async-start | bytes 1048576 | tf_op jit(solution)/shard_map/all_to_all | solution.py:85
  20.6 26.3 %all_gather.6 = f32[8,128,128]{2,0,1:T(8,128)S(1)} all-gather(f32[8,8,128]{2,0,1:T(8,128)S(1)} %convolution_bitcast_fusion.4), channel_id=1, replica_groups=mesh['grp'=2,'res'=16] {'res'}, dimensions={1}, use_global_device_ids=true | all-gather | bytes 557056 | tf_op jit(solution)/shard_map/all_gather | solution.py:94
  47.4 0.6 fusion.27
  48.3 7.5 %while.20 = (s32[]{:T(128)}, bf16[8,8,128,32]{2,3,1,0:T(8,128)(2,1)S(1)}, bf16[8,8,128,32]{2,3,1,0:T(8,128)(2,1)S(1)}, bf16[8,8,128,32]{2,3,1,0:T(8,128)(2,1)S(1...) while((s32[]{:T(128)}, bf16[8,8,128,32]{2,3,1,0:T(8,128)(2,1)S(1)}, ...), condition=%wide.region_7.8_spmd, body=%wide.region_4.7_spmd.sunk | while | flops 26379520 | bytes 3025997 | solution.py:99
  48.6 0.4 fusion.171
  49.5 0.4 fusion.171
  50.4 0.4 fusion.171
  52.3 0.4 fusion.171
  53.2 0.4 fusion.171
  54.2 0.4 fusion.171
  55.8 1.0 copy.81
  56.8 2.0 copy_bitcast_fusion
  58.8 3.8 %reshape.229 = bf16[16,2,8192]{2,1,0:T(2,128)(2,1)S(1)} reshape(bf16[16,8,8,8,32]{4,3,2,1,0:T(8,128)(2,1)} %copy_bitcast_fusion) | data formatting | bytes 1048576
  62.6 17.2 %all_to_all.105 = bf16[16,2,8192]{2,1,0:T(2,128)(2,1)S(1)} all-to-all(bf16[16,2,8192]{2,1,0:T(2,128)(2,1)S(1)} %reshape.229), channel_id=1, replica_groups=mesh['grp'=2,'res'=16] {'res'}, dimensions={0} | all-to-all | bytes 1048576 | tf_op jit(solution)/shard_map/all_to_all | solution.py:101
  79.7 1.0 reshape.230
  80.8 2.4 %bitcast_convert_fusion = f32[8,8,16,1,8,32]{5,4,1,0,2,3:T(8,128)} fusion(bf16[16,8,8,8,32]{4,3,2,1,0:T(8,128)(2,1)S(1)} %reshape.230), kind=kLoop, calls=%fused_computation.28 | loop fusion | flops 262144 | bytes 1572864 | tf_op jit(solution)/shard_map/convert_element_type | solution.py:123
  83.2 3.8 %copy.83 = f32[128,8,8,32]{0,3,1,2:T(8,128)S(1)} copy(f32[128,8,8,32]{3,2,1,0:T(8,128)} %bitcast.280) | data formatting | bytes 2097152 | tf_op jit(solution)/shard_map/convert_element_type | solution.py:123
  87.0 1.9 convert_reduce_fusion.1
  89.3 0.5 fusion.52
  90.0 0.9 reshape_squeeze.9
  91.0 0.8 copy.88
  91.8 36.6 %all-gather.2.cloned.1.call-done = bf16[128,4096]{1,0:T(8,128)(2,1)} async-done(((bf16[8,4096]{1,0:T(8,128)(2,1)}), bf16[128,4096]{1,0:T(8,128)(2,1)}) %all-gather.2.cloned.1.call-update) | async-done | bytes 1048592 | tf_op jit(solution)/shard_map/all_gather | solution.py:144
  128.4 1.6 copy.85
  130.1 1.0 copy.86
  131.1 11.9 %while.21 = (s32[]{:T(128)}, f32[8,128,128]{1,2,0:T(8,128)}, bf16[8,128,32]{1,2,0:T(8,128)(2,1)S(1)}, bf16[128,128,32]{1,0,2:T(8,128)(2,1)S(1)}, bf16[1024,128]{1,0:T(8,128)(2,1)S(1)}, /*index=5*/s32[]{:T(128)}) while((s32[]{:T(128)}, f32[8,128,128]{1,2,0:T(8,128)}, bf16[8,128,32]{1,2,0:T(8,128)(2,1)S(1)}, ...), condition=%wide.region_11.12_spmd, body=%wide.region_10.11_spmd.sunk | while | flops 67371008 | bytes 2433609 | solution.py:157
  131.1 0.5 fusion.178
  131.7 0.9 fusion.179
  132.6 0.5 fusion.178
  133.2 0.9 fusion.179
  134.1 0.5 fusion.178
  134.6 0.9 fusion.179
  135.6 0.5 fusion.178
  136.1 0.9 fusion.179
  137.1 0.5 fusion.178
  137.6 0.9 fusion.179
  138.5 0.5 fusion.178
  139.1 0.9 fusion.179
  140.0 0.5 fusion.178
  140.6 0.9 fusion.179
  141.5 0.5 fusion.178
  142.1 0.9 fusion.179
  143.0 1.1 convert_reduce_fusion.2
  144.3 0.4 convolution_bitcast_fusion.2
  145.0 0.8 copy.91
  145.8 3.7 %all-to-all-start.2 = ((bf16[16,8,8,128]{3,1,2,0:T(8,128)(2,1)}), bf16[16,8,8,128]{3,1,2,0:T(8,128)(2,1)S(1)}, u32[]{:S(2)}, u32[]{:S(2)}) async-start(bf16[16,8,8,128]{3,1,2,0:T(8,128)(2,1)} %copy.91), calls=%async_computation.2 | async-start | bytes 524288 | tf_op jit(solution)/shard_map/all_to_all | solution.py:48
  149.5 9.9 %all-to-all-done.2 = bf16[16,8,8,128]{3,1,2,0:T(8,128)(2,1)S(1)} async-done(((bf16[16,8,8,128]{3,1,2,0:T(8,128)(2,1)}), bf16[16,8,8,128]{3,1,2,0:T(8,128)(2,1)S(1)}, u32[]{:S(2)}, u32[]{:S(2)}) %all-to-all-start.2) | async-done | bytes 262176 | tf_op jit(solution)/shard_map/all_to_all | solution.py:48
  159.5 12.7 %all_to_all.106 = bf16[16,8,8,128]{3,1,2,0:T(8,128)(2,1)S(1)} all-to-all(bf16[16,8,8,128]{3,1,2,0:T(8,128)(2,1)S(1)} %copy.93), channel_id=1, replica_groups=mesh['grp'=2,'res'=16] {'res'}, dimensions={0} | all-to-all | bytes 524288 | tf_op jit(solution)/shard_map/all_to_all | solution.py:49
  172.5 0.8 copy.95
  173.2 3.5 %all-to-all-start.4 = ((bf16[1,8,16,8,128]{4,3,1,0,2:T(8,128)(2,1)}), bf16[1,8,16,8,128]{4,3,1,0,2:T(8,128)(2,1)S(1)}, u32[]{:S(2)}, u32[]{:S(2)}) async-start(bf16[1,8,16,8,128]{4,3,1,0,2:T(8,128)(2,1)} %copy.95), calls=%async_computation.4 | async-start | bytes 524288 | tf_op jit(solution)/shard_map/all_to_all | solution.py:54
  177.3 9.5 %all-to-all-done.4 = bf16[1,8,16,8,128]{4,3,1,0,2:T(8,128)(2,1)S(1)} async-done(((bf16[1,8,16,8,128]{4,3,1,0,2:T(8,128)(2,1)}), bf16[1,8,16,8,128]{4,3,1,0,2:T(8,128)(2,1)S(1)}, u32[]{:S(2)}, u32[]{:S(2)}) %all-to-all-start.4) | async-done | bytes 262176 | tf_op jit(solution)/shard_map/all_to_all | solution.py:54
  187.5 0.4 convolution_bitcast_fusion.1
  188.2 0.9 copy.103
  189.1 3.5 %all-to-all-start.5 = ((bf16[16,8,8,128]{3,2,1,0:T(8,128)(2,1)}), bf16[16,8,8,128]{3,2,1,0:T(8,128)(2,1)S(1)}, u32[]{:S(2)}, u32[]{:S(2)}) async-start(bf16[16,8,8,128]{3,2,1,0:T(8,128)(2,1)} %copy.103), calls=%async_computation.5 | async-start | bytes 524288 | tf_op jit(solution)/shard_map/all_to_all | solution.py:48
  192.7 9.9 %all-to-all-done.5 = bf16[16,8,8,128]{3,2,1,0:T(8,128)(2,1)S(1)} async-done(((bf16[16,8,8,128]{3,2,1,0:T(8,128)(2,1)}), bf16[16,8,8,128]{3,2,1,0:T(8,128)(2,1)S(1)}, u32[]{:S(2)}, u32[]{:S(2)}) %all-to-all-start.5) | async-done | bytes 262176 | tf_op jit(solution)/shard_map/all_to_all | solution.py:48
  202.6 12.7 %all_to_all.107 = bf16[16,8,8,128]{3,1,2,0:T(8,128)(2,1)S(1)} all-to-all(bf16[16,8,8,128]{3,1,2,0:T(8,128)(2,1)S(1)} %copy.105), channel_id=1, replica_groups=mesh['grp'=2,'res'=16] {'res'}, dimensions={0} | all-to-all | bytes 524288 | tf_op jit(solution)/shard_map/all_to_all | solution.py:49
  215.6 0.8 copy.108
  216.4 3.5 %all-to-all-start.7 = ((bf16[1,8,16,8,128]{4,3,1,0,2:T(8,128)(2,1)}), bf16[1,8,16,8,128]{4,3,1,0,2:T(8,128)(2,1)S(1)}, u32[]{:S(2)}, u32[]{:S(2)}) async-start(bf16[1,8,16,8,128]{4,3,1,0,2:T(8,128)(2,1)} %copy.108), calls=%async_computation.7 | async-start | bytes 524288 | tf_op jit(solution)/shard_map/all_to_all | solution.py:54
  219.9 1.1 copy.112
  221.3 8.6 %all-to-all-done.7 = bf16[1,8,16,8,128]{4,3,1,0,2:T(8,128)(2,1)S(1)} async-done(((bf16[1,8,16,8,128]{4,3,1,0,2:T(8,128)(2,1)}), bf16[1,8,16,8,128]{4,3,1,0,2:T(8,128)(2,1)S(1)}, u32[]{:S(2)}, u32[]{:S(2)}) %all-to-all-start.7) | async-done | bytes 262176 | tf_op jit(solution)/shard_map/all_to_all | solution.py:54
  230.6 0.9 copy.113
  (97 shorter events, 11.2 us)
Async XLA Ops:
  7.2 79.8 %copy-start = (bf16[256,256]{1,0:T(8,128)(2,1)S(1)}, bf16[256,256]{1,0:T(8,128)(2,1)}, u32[]{:S(2)}) copy-start(bf16[256,256]{1,0:T(8,128)(2,1)} %param.17) | copy-start | bytes 393220
  7.2 12.9 %copy-start.7 = (bf16[8,128,128]{2,1,0:T(8,128)(2,1)S(1)}, bf16[8,128,128]{2,1,0:T(8,128)(2,1)}, u32[]{:S(2)}) copy-start(bf16[8,128,128]{2,1,0:T(8,128)(2,1)} %param.14) | copy-start | bytes 786436
  9.9 10.5 %copy-start.10 = (bf16[128,8]{0,1:T(8,128)(2,1)S(1)}, bf16[128,8]{0,1:T(8,128)(2,1)}, u32[]{:S(2)}) copy-start(bf16[128,8]{0,1:T(8,128)(2,1)} %param.16) | copy-start | bytes 6148
  12.4 34.7 %copy-start.5 = (bf16[256,1024]{1,0:T(8,128)(2,1)S(1)}, bf16[256,1024]{1,0:T(8,128)(2,1)}, u32[]{:S(2)}) copy-start(bf16[256,1024]{1,0:T(8,128)(2,1)} %param.15) | copy-start | bytes 1572868
  12.4 34.9 %all-to-all-start = ((bf16[128,8,256]{2,1,0:T(8,128)(2,1)}), bf16[128,8,256]{2,1,0:T(8,128)(2,1)S(1)}, u32[]{:S(2)}, u32[]{:S(2)}) async-start(bf16[128,8,256]{2,1,0:T(8,128)(2,1)} %copy.75), calls=%async_computation | async-start | bytes 1048576 | tf_op jit(solution)/shard_map/all_to_all | solution.py:85
  20.0 108.5 %all-gather.2.cloned.1.call-start = ((), (), s32[]{:S(2)}) async-start(), calls=%async_computation.8 | async-start | bytes 1114112 | tf_op jit(solution)/shard_map/all_gather | solution.py:144
  47.3 0.9 copy-start.3
  83.2 3.8 %copy-start.2 = (bf16[128,8,256]{2,1,0:T(8,128)(2,1)S(1)}, bf16[128,8,256]{2,1,0:T(8,128)(2,1)}, u32[]{:S(2)}) copy-start(bf16[128,8,256]{2,1,0:T(8,128)(2,1)} %param.13) | copy-start | bytes 1572868
  87.0 2.3 copy-start.9
  88.9 2.0 copy-start.6
  91.8 39.3 %copy-start.1 = (bf16[1024,128]{1,0:T(8,128)(2,1)S(1)}, bf16[1024,128]{1,0:T(8,128)(2,1)}, u32[]{:S(2)}) copy-start(bf16[1024,128]{1,0:T(8,128)(2,1)} %param.19) | copy-start | bytes 786436
  131.1 13.2 %copy-start.4 = (bf16[1,128,640]{1,2,0:T(8,128)(2,1)S(1)}, bf16[1,128,640]{1,2,0:T(8,128)(2,1)}, u32[]{:S(2)}) copy-start(bf16[1,128,640]{1,2,0:T(8,128)(2,1)} %copy.88) | copy-start | bytes 491524
  145.8 13.7 %all-to-all-start.2 = ((bf16[16,8,8,128]{3,1,2,0:T(8,128)(2,1)}), bf16[16,8,8,128]{3,1,2,0:T(8,128)(2,1)S(1)}, u32[]{:S(2)}, u32[]{:S(2)}) async-start(bf16[16,8,8,128]{3,1,2,0:T(8,128)(2,1)} %copy.91), calls=%async_computation.2 | async-start | bytes 524288 | tf_op jit(solution)/shard_map/all_to_all | solution.py:48
  173.2 13.5 %all-to-all-start.4 = ((bf16[1,8,16,8,128]{4,3,1,0,2:T(8,128)(2,1)}), bf16[1,8,16,8,128]{4,3,1,0,2:T(8,128)(2,1)S(1)}, u32[]{:S(2)}, u32[]{:S(2)}) async-start(bf16[1,8,16,8,128]{4,3,1,0,2:T(8,128)(2,1)} %copy.95), calls=%async_computation.4 | async-start | bytes 524288 | tf_op jit(solution)/shard_map/all_to_all | solution.py:54
  176.8 10.4 %copy-start.8 = (bf16[2,128,128]{2,1,0:T(8,128)(2,1)S(1)}, bf16[2,128,128]{2,1,0:T(8,128)(2,1)}, u32[]{:S(2)}) copy-start(bf16[2,128,128]{2,1,0:T(8,128)(2,1)} %param.21) | copy-start | bytes 196612
  189.1 13.5 %all-to-all-start.5 = ((bf16[16,8,8,128]{3,2,1,0:T(8,128)(2,1)}), bf16[16,8,8,128]{3,2,1,0:T(8,128)(2,1)S(1)}, u32[]{:S(2)}, u32[]{:S(2)}) async-start(bf16[16,8,8,128]{3,2,1,0:T(8,128)(2,1)} %copy.103), calls=%async_computation.5 | async-start | bytes 524288 | tf_op jit(solution)/shard_map/all_to_all | solution.py:48
  216.4 13.5 %all-to-all-start.7 = ((bf16[1,8,16,8,128]{4,3,1,0,2:T(8,128)(2,1)}), bf16[1,8,16,8,128]{4,3,1,0,2:T(8,128)(2,1)S(1)}, u32[]{:S(2)}, u32[]{:S(2)}) async-start(bf16[1,8,16,8,128]{4,3,1,0,2:T(8,128)(2,1)} %copy.108), calls=%async_computation.7 | async-start | bytes 524288 | tf_op jit(solution)/shard_map/all_to_all | solution.py:54
Sparse Core Ops, SparseCore 0:
  91.1 37.3 all-gather.1
where the time goes:
time: 239 us; the launch traced here: 238 us
  waiting for transfers between devices  74.6 us (31%)
  blocking collectives  68.8 us (29%)
  local copies, waits for them, and re-layouts  24.4 us (10%)
  matrix products  24 us (10%)
  starting transfers between devices  21.9 us (9%)
  between operations  14.6 us (6%)
  other arithmetic  9.61 us (4%)
    all_gather x1, waiting for transfers between devices, body(): piece = lax.all_gather(right_flat, 'res', axis=0, tiled=True)  36.6 us
    all_gather x1, blocking collectives, body(): full_bias = lax.all_gather(bias_rows, 'res', axis=1, tiled=True)  26.3 us
    all_to_all x2, blocking collectives, triangle(): lax.all_to_all(sending[1], 'res', split_axis=0, concat_axis=2, tiled=True)  25.4 us
    all_to_all x2, waiting for transfers between devices, triangle(): lax.all_to_all(sending[0], 'res', split_axis=0, concat_axis=2, tiled=True)  19.9 us
    all_to_all x2, waiting for transfers between devices, triangle(): lax.all_to_all(split_rows, 'res', split_axis=2, concat_axis=0, tiled=True)  18.1 us
    all_to_all x1, blocking collectives, body(): lax.all_to_all(mixed_signals.reshape(per_device, focus_group_tally, res_c...  17.2 us
    unnamed x30, local copies, waits for them, and re-layouts  9.33 us
    all_to_all x1, starting transfers between devices, body(): lax.all_to_all(alignment_standardised, 'res', split_axis=0, concat_axis=1...  7.55 us
  transfers between devices with their start and end apart: 6, of which 5 were waited for; matrix products, arithmetic and copies ran while one was open for 2% of the time, Pallas kernels for 0%

commit v1 on v0

v1 whole, which is shorter than its diff:
```python
import jax
import jax.numpy as jnp
from jax import lax
from jax.sharding import PartitionSpec as P


def standardise_entries(values_in, axis_num):
    values_in = values_in.astype(jnp.float32)
    centred = values_in - jnp.mean(values_in, axis=axis_num, keepdims=True)
    spread = jnp.mean(centred * centred, axis=axis_num, keepdims=True)
    return centred * lax.rsqrt(spread + 1e-05)


def exchange(blocks):
    return lax.all_to_all(blocks, "res", split_axis=0, concat_axis=0, tiled=True)


def with_partner(values):
    count = lax.axis_size("res")
    return lax.ppermute(values, "res", [(k, k ^ 1) for k in range(count)])


def triangle(pair_prev, weight_in, weight_out, contraction):
    local_strands, total_res, pair_width = pair_prev.shape
    count = lax.axis_size("res")
    share = pair_width // count
    normed = standardise_entries(pair_prev, -1).astype(jnp.bfloat16)
    five = weight_in.reshape(pair_width, 5, pair_width)
    paired = five[:, :4].reshape(pair_width, 2, 2, count, share).transpose(0, 2, 3, 1, 4)
    mapped = jnp.einsum(
        "rnc,ctwsk->twskrn", normed, paired, preferred_element_type=jnp.float32
    )
    edges = (jax.nn.sigmoid(mapped[0]) * mapped[1]).astype(jnp.bfloat16)
    arrived = exchange(edges)
    gate_pair = jax.nn.sigmoid(
        jnp.einsum("rnc,cf->rnf", normed, five[:, 4], preferred_element_type=jnp.float32)
    )
    product = jnp.einsum(
        contraction, arrived[:, 0], arrived[:, 1], preferred_element_type=jnp.float32
    ).astype(jnp.bfloat16)
    product = product.reshape(share, count, local_strands, total_res).transpose(1, 0, 2, 3)
    gathered = exchange(product).reshape(pair_width, local_strands, total_res)
    edge_norm = standardise_entries(gathered, 0).astype(jnp.bfloat16)
    update = jnp.einsum("crn,cf->rnf", edge_norm, weight_out, preferred_element_type=jnp.float32)
    return (pair_prev.astype(jnp.float32) + gate_pair * update).astype(jnp.bfloat16)


def body(
    alignment_embedding,
    coupling_embedding,
    query_key_matrix,
    coupling_logit_matrix,
    focus_final_matrix,
    tensor_average_matrix,
    tensor_average_final,
    trilateral_entry_matrix,
    trilateral_exit_matrix,
):
    chain_tally, local_strands, depth = alignment_embedding.shape
    total_res, pair_width = coupling_embedding.shape[1:]
    count = lax.axis_size("res")
    core = lax.axis_index("res") % 2
    heads = coupling_logit_matrix.shape[1]
    width = query_key_matrix.shape[1] // (4 * heads)
    per_device = chain_tally // count
    tensor_depth = tensor_average_matrix.shape[1] // 2
    half = total_res // 2

    rows = exchange(alignment_embedding).reshape(count, per_device, local_strands, depth)
    rows = rows.transpose(1, 0, 2, 3).reshape(per_device, total_res, depth)

    pair_norm = standardise_entries(coupling_embedding, -1).astype(jnp.bfloat16)
    bias_rows = jnp.einsum(
        "rnc,ch->hrn", pair_norm, coupling_logit_matrix, preferred_element_type=jnp.float32
    )
    upper = lax.reduce_precision(bias_rows, 8, 7)
    terms = jnp.stack([upper, bias_rows - upper]).astype(jnp.bfloat16)
    term = exchange(jnp.tile(terms, (count // 2, 1, 1, 1)))
    bias = term.astype(jnp.float32) + with_partner(term).astype(jnp.float32)
    bias = bias.transpose(1, 0, 2, 3).reshape(heads, total_res, total_res)

    standard = standardise_entries(rows, -1).astype(jnp.bfloat16)
    projection = query_key_matrix.reshape(depth, 4, heads, width)
    mapped = jnp.einsum(
        "snc,cthd->tshnd", standard, projection[:, :3], preferred_element_type=jnp.float32
    ).astype(jnp.bfloat16)
    gate = jax.nn.sigmoid(
        jnp.einsum("snc,chd->shnd", standard, projection[:, 3], preferred_element_type=jnp.float32)
    )
    scores = (
        jnp.einsum("shid,shjd->shij", mapped[0], mapped[1], preferred_element_type=jnp.float32)
        * width ** (-0.5)
        + bias
    )
    weights = jnp.exp(scores - jnp.max(scores, axis=-1, keepdims=True))
    weights = (weights / jnp.sum(weights, axis=-1, keepdims=True)).astype(jnp.bfloat16)
    attended = jnp.einsum(
        "shij,shjd->shid", weights, mapped[2], preferred_element_type=jnp.float32
    ).astype(jnp.bfloat16)
    gated = (attended.astype(jnp.float32) * gate).astype(jnp.bfloat16)
    increment = jnp.einsum(
        "shnd,hdc->snc",
        gated,
        focus_final_matrix.reshape(heads, width, depth),
        preferred_element_type=jnp.float32,
    )
    mixed = (rows.astype(jnp.float32) + increment).astype(jnp.bfloat16)

    tensor_scaled = standardise_entries(mixed, -1).astype(jnp.bfloat16)
    flank = jnp.einsum(
        "snc,ctk->tsnk",
        tensor_scaled,
        tensor_average_matrix.reshape(depth, 2, tensor_depth),
        preferred_element_type=jnp.float32,
    ).astype(jnp.bfloat16)
    left = flank[0].reshape(per_device, count // 2, 2, local_strands * tensor_depth)
    left = left.transpose(1, 2, 0, 3)
    right = flank[1].reshape(per_device, 2, half, tensor_depth).transpose(1, 0, 3, 2)
    right = right.reshape(2, per_device, tensor_depth * half)
    right = jnp.broadcast_to(right, (count // 2,) + right.shape)
    flanks = jnp.concatenate([left, right], axis=-1).reshape(count, per_device, -1)
    flanks = exchange(flanks)
    mixed_out = exchange(
        mixed.reshape(per_device, count, local_strands, depth).transpose(1, 0, 2, 3)
    ).reshape(chain_tally, local_strands, depth)

    flanks = flanks.reshape(chain_tally, -1)
    left_all = flanks[:, : local_strands * tensor_depth]
    mine = flanks[:, local_strands * tensor_depth :]
    other = with_partner(mine)
    both = jnp.stack([mine, other])
    both = jnp.where(core == 0, both, both[::-1]).reshape(2, chain_tally, tensor_depth, half)
    group = 4 if local_strands % 4 == 0 else 1
    final = tensor_average_final.reshape(tensor_depth, tensor_depth, pair_width)
    final = jnp.einsum(
        "ab,cef->eacbf", jnp.eye(group, dtype=final.dtype), final
    ).reshape(tensor_depth, group * tensor_depth, group * pair_width)
    outer = jnp.einsum(
        "xsej,sgm->exjgm",
        both,
        left_all.reshape(chain_tally, local_strands // group, group * tensor_depth),
        preferred_element_type=jnp.float32,
    ) * (1.0 / chain_tally)
    opm = jnp.einsum(
        "exjgm,emn->gxjn", outer.astype(jnp.bfloat16), final, preferred_element_type=jnp.float32
    )
    opm = opm.reshape(local_strands // group, total_res, group, pair_width)
    opm = opm.transpose(0, 2, 1, 3).reshape(local_strands, total_res, pair_width)
    pair_mid = (coupling_embedding.astype(jnp.float32) + opm).astype(jnp.bfloat16)

    pair_tri = triangle(
        pair_mid, trilateral_entry_matrix[0], trilateral_exit_matrix[0], "xcik,ycjk->cxiyj"
    )
    coupling_refreshed = triangle(
        pair_tri, trilateral_entry_matrix[1], trilateral_exit_matrix[1], "xcki,xckj->cij"
    )
    return (mixed_out, coupling_refreshed)


def solution(mesh):
    return jax.shard_map(
        body,
        mesh=mesh,
        in_specs=(P("grp", "res", None), P("res", "grp", None), P(), P(), P(), P(), P(), P(), P()),
        out_specs=(P("grp", "res", None), P("res", "grp", None)),
        check_vma=False,
    )
```

time: 239 us -> 184 us (0.77)
  blocking collectives: 68.8 us -> 35.9 us
  between operations: 14.6 us -> 1.26 us
  matrix products: 24 us -> 13.2 us
  starting transfers between devices: 21.9 us -> 24.3 us
    all_gather x1 -> x0, waiting for transfers between devices: 36.6 us -> none  [body(): piece = lax.all_gather(right_flat, 'res', axis=0, tiled=True)]
    all_to_all x5 -> x6, waiting for transfers between devices: 37.9 us -> 72.3 us  [exchange(): lax.all_to_all(blocks, 'res', split_axis=0, concat_axis=0, tiled=True)]
    all_gather x1 -> x0, blocking collectives: 26.3 us -> none  [body(): full_bias = lax.all_gather(bias_rows, 'res', axis=1, tiled=True)]
    dot_general x41 -> x12, matrix products: 20.3 us -> 11.9 us  [the longest x1 4.74 us: body(): jnp.einsum('exjgm,emn->gxjn', outer.astype(jnp.bfloat16), final, preferre...]
    reshape x2 -> x5, local copies, waits for them, and re-layouts: 1.55 us -> 8.49 us  [the longest x1 7.26 us: body(): final = jnp.einsum('ab,cef->eacbf', jnp.eye(group, dtype=final.dtype), fi...]
    all_to_all x3 -> x2, blocking collectives: 42.5 us -> 35.9 us  [exchange(): lax.all_to_all(blocks, 'res', split_axis=0, concat_axis=0, tiled=True)]
    unnamed x30 -> x21, local copies, waits for them, and re-layouts: 9.33 us -> 3.73 us
    transpose x0 -> x5, local copies, waits for them, and re-layouts: none -> 3.8 us  [the longest x1 2.69 us: triangle(): product.reshape(share, count, local_strands, total_res)]
  transfers between devices with their start and end apart: 6 -> 8, of which waited for: 5 -> 7; matrix products, arithmetic and copies ran while one was open for 2% -> 9% of each run, Pallas kernels for 0% -> 0%
where the time goes in v1:
time: 184 us; the launch traced here: 182 us
  waiting for transfers between devices  73.3 us (40%)
  blocking collectives  35.9 us (20%)
  local copies, waits for them, and re-layouts  24.4 us (13%)
  starting transfers between devices  24.3 us (13%)
  matrix products  13.2 us (7%)
  other arithmetic  10 us (5%)
    all_to_all x6, waiting for transfers between devices, exchange(): lax.all_to_all(blocks, 'res', split_axis=0, concat_axis=0, tiled=True)  72.3 us
    all_to_all x2, blocking collectives, exchange(): lax.all_to_all(blocks, 'res', split_axis=0, concat_axis=0, tiled=True)  35.9 us
    all_to_all x6, starting transfers between devices, exchange(): lax.all_to_all(blocks, 'res', split_axis=0, concat_axis=0, tiled=True)  23.7 us
    reshape x1, local copies, waits for them, and re-layouts, body(): final = jnp.einsum('ab,cef->eacbf', jnp.eye(group, dtype=final.dtype), fi...  7.26 us
    dot_general x1, matrix products, body(): jnp.einsum('exjgm,emn->gxjn', outer.astype(jnp.bfloat16), final, preferre...  4.74 us
    convert_element_type x1, local copies, waits for them, and re-layouts, triangle(): product = jnp.einsum(contraction, arrived[:, 0], arrived[:, 1], preferred...  4.24 us
    unnamed x21, local copies, waits for them, and re-layouts  3.73 us
  transfers between devices with their start and end apart: 8, of which 7 were waited for; matrix products, arithmetic and copies ran while one was open for 9% of the time, Pallas kernels for 0%

profile of v1, /device:TPU:0, one launch (start us, length us, event | category | flops | bytes accessed | tf_op | source)
XLA Modules:
  0.0 182.5 jit_solution(15703020352280968856)
XLA Ops:
  0.7 1.2 copy.143
  2.0 0.9 fusion.107
  2.9 17.2 %all_to_all.40 = bf16[16,8,8,128]{3,2,1,0:T(8,128)(2,1)S(1)} all-to-all(bf16[16,8,8,128]{3,2,1,0:T(8,128)(2,1)S(1)} %bitcast.273), channel_id=1, replica_groups=mesh['grp'=2,'res'=16] {'res'}, dimensions={0} | all-to-all | bytes 524288 | tf_op jit(solution)/shard_map/all_to_all | solution.py:15
  20.2 3.6 %all-to-all-start = ((bf16[128,8,256]{2,1,0:T(8,128)(2,1)}), bf16[128,8,256]{2,1,0:T(8,128)(2,1)S(1)}, u32[]{:S(2)}, u32[]{:S(2)}) async-start(bf16[128,8,256]{2,1,0:T(8,128)(2,1)} %param.9), calls=%async_computation | async-start | bytes 1048576 | tf_op jit(solution)/shard_map/all_to_all | solution.py:15
  23.8 0.4 collective-permute-start
  24.2 0.2 copy.142
  24.4 1.0 collective-permute-done
  25.5 0.2 copy.148
  25.7 12.3 %all-to-all-done = bf16[128,8,256]{2,1,0:T(8,128)(2,1)S(1)} async-done(((bf16[128,8,256]{2,1,0:T(8,128)(2,1)}), bf16[128,8,256]{2,1,0:T(8,128)(2,1)S(1)}, u32[]{:S(2)}, u32[]{:S(2)}) %all-to-all-start) | async-done | bytes 524320 | tf_op jit(solution)/shard_map/all_to_all | solution.py:15
  38.1 0.2 bitcast_reduce_fusion
  38.3 0.4 multiply_reduce_fusion
  38.9 0.8 fusion.8
  39.7 0.8 fusion.76
  40.5 1.3 fusion.118
  41.8 0.7 fusion.18
  42.5 1.0 convert_reduce_fusion
  43.5 0.4 fusion.40
  43.9 0.5 fusion.39
  44.5 0.2 reshape.220
  44.7 0.2 copy.152
  44.9 0.2 reshape_squeeze.12
  45.1 0.8 pad_maximum_fusion.1
  46.0 4.1 %all-to-all-start.3 = ((bf16[16,8,2304]{2,1,0:T(8,128)(2,1)}), bf16[16,8,2304]{2,1,0:T(8,128)(2,1)S(1)}, u32[]{:S(2)}, u32[]{:S(2)}) async-start(bf16[16,8,2304]{2,1,0:T(8,128)(2,1)} %bitcast.42), calls=%async_computation.3 | async-start | bytes 1179648 | tf_op jit(solution)/shard_map/all_to_all | solution.py:15
  50.2 15.2 %all-to-all-done.3 = bf16[16,8,2304]{2,1,0:T(8,128)(2,1)S(1)} async-done(((bf16[16,8,2304]{2,1,0:T(8,128)(2,1)}), bf16[16,8,2304]{2,1,0:T(8,128)(2,1)S(1)}, u32[]{:S(2)}, u32[]{:S(2)}) %all-to-all-start.3) | async-done | bytes 589856 | tf_op jit(solution)/shard_map/all_to_all | solution.py:15
  65.6 0.3 collective-permute-start.1
  65.9 3.6 %multiply_bitcast_fusion = bf16[32,4,32,4,128]{4,3,2,1,0:T(4,128)(2,1)} fusion(bf16[32,32,128]{2,0,1:T(8,128)(2,1)S(1)} %copy.151, bf16[4,4]{1,0:T(4,128)(2,1)S(1)} %fusion.109), kind=kLoop, calls=%fused_computation.4 | loop fusion | flops 2097152 | bytes 4456480 | tf_op jit(solution)/shard_map/ab,cef->eacbf/transpose | solution.py:135
  69.5 7.3 %reshape.249 = bf16[32,128,512,1,1]{2,1,0,3,4:T(8,128)(2,1)} reshape(bf16[32,4,32,4,128]{4,3,2,1,0:T(4,128)(2,1)} %multiply_bitcast_fusion) | data formatting | bytes 8388608 | tf_op jit(solution)/shard_map/reshape | solution.py:137
  76.8 0.7 fusion.116
  77.5 0.2 copy.160
  77.8 0.5 copy-done.2
  78.3 1.1 pad_maximum_fusion
  79.4 0.2 reverse_select_fusion
  79.7 0.7 copy.156
  80.3 4.7 %fusion.29 = f32[2,2,64,512]{3,2,0,1:T(8,128)S(1)} fusion(bf16[128,2,128,1,1]{0,2,4,1,3:T(8,128)(2,1)S(1)} %bitcast.285, bf16[2,128,32,64,1]{1,3,2,4,0:T(8,128)(2,1)S(1)} %bitcast.272, bf16[32,128,512,1,1]{2,1,0,3,4:T(8,128)(2,1)} %reshape.249), kind=kOutput, calls=%fused_computation.48 | convolution fusion | flops 1344274432 | bytes 5832704 | tf_op jit(solution)/shard_map/exjgm,emn->gxjn/dot_general | solution.py:144
  85.1 0.2 reshape.225
  85.3 0.2 copy.159
  85.7 0.4 convolution_bitcast_fusion.1
  86.2 0.3 fusion.86
  86.6 18.7 %all_to_all.41 = bf16[16,2,8,8,128]{4,2,1,3,0:T(8,128)(2,1)S(1)} all-to-all(bf16[16,2,8,8,128]{4,2,1,3,0:T(8,128)(2,1)S(1)} %copy.164), channel_id=1, replica_groups=mesh['grp'=2,'res'=16] {'res'}, dimensions={0} | all-to-all | bytes 1048576 | tf_op jit(solution)/shard_map/all_to_all | solution.py:15
  105.4 0.8 convolution_convert_fusion
  106.3 4.2 %copy.167 = bf16[8,16,8,16,8]{1,4,3,2,0:T(8,128)(2,1)} copy(bf16[8,16,8,16,8]{3,2,4,1,0:T(8,128)(2,1)S(1)} %convolution_convert_fusion) | data formatting | bytes 524288 | tf_op jit(solution)/shard_map/convert_element_type | solution.py:40
  110.5 2.7 %copy.168 = bf16[16,8,8,128]{3,2,1,0:T(8,128)(2,1)} copy(bf16[16,8,8,128]{0,3,2,1:T(8,128)(2,1)} %bitcast.265) | data formatting | bytes 524288 | tf_op jit(solution)/shard_map/transpose | solution.py:41
  113.2 4.2 %all-to-all-start.5 = ((bf16[16,8,8,128]{3,2,1,0:T(8,128)(2,1)}), bf16[16,8,8,128]{3,2,1,0:T(8,128)(2,1)S(1)}, u32[]{:S(2)}, u32[]{:S(2)}) async-start(bf16[16,8,8,128]{3,2,1,0:T(8,128)(2,1)} %copy.168), calls=%async_computation.5 | async-start | bytes 524288 | tf_op jit(solution)/shard_map/all_to_all | solution.py:15
  117.4 0.2 copy.211
  117.6 1.1 fusion.26
  118.6 8.7 %all-to-all-done.5 = bf16[16,8,8,128]{3,2,1,0:T(8,128)(2,1)S(1)} async-done(((bf16[16,8,8,128]{3,2,1,0:T(8,128)(2,1)}), bf16[16,8,8,128]{3,2,1,0:T(8,128)(2,1)S(1)}, u32[]{:S(2)}, u32[]{:S(2)}) %all-to-all-start.5) | async-done | bytes 262176 | tf_op jit(solution)/shard_map/all_to_all | solution.py:15
  127.5 0.1 fusion.66
  127.8 0.3 fusion.121
  128.1 0.4 convolution_bitcast_fusion
  128.6 0.3 fusion.87
  128.9 0.9 copy.177
  129.8 3.6 %all-to-all-start.6 = ((bf16[16,2,8,8,128]{4,2,1,3,0:T(8,128)(2,1)}), bf16[16,2,8,8,128]{4,2,1,3,0:T(8,128)(2,1)S(1)}, u32[]{:S(2)}, u32[]{:S(2)}) async-start(bf16[16,2,8,8,128]{4,2,1,3,0:T(8,128)(2,1)} %copy.177), calls=%async_computation.6 | async-start | bytes 1048576 | tf_op jit(solution)/shard_map/all_to_all | solution.py:15
  133.4 0.8 copy_bitcast_fusion
  134.2 13.4 %all-to-all-done.6 = bf16[16,2,8,8,128]{4,2,1,3,0:T(8,128)(2,1)S(1)} async-done(((bf16[16,2,8,8,128]{4,2,1,3,0:T(8,128)(2,1)}), bf16[16,2,8,8,128]{4,2,1,3,0:T(8,128)(2,1)S(1)}, u32[]{:S(2)}, u32[]{:S(2)}) %all-to-all-start.6) | async-done | bytes 524320 | tf_op jit(solution)/shard_map/all_to_all | solution.py:15
  147.6 4.1 %all-to-all-start.2 = ((bf16[16,8,8,256]{3,2,1,0:T(8,128)(2,1)}), bf16[16,8,8,256]{3,2,1,0:T(8,128)(2,1)S(1)}, u32[]{:S(2)}, u32[]{:S(2)}) async-start(bf16[16,8,8,256]{3,2,1,0:T(8,128)(2,1)} %copy_bitcast_fusion), calls=%async_computation.2 | async-start | bytes 1048576 | tf_op jit(solution)/shard_map/all_to_all | solution.py:15
  151.8 0.4 fusion.38
  152.3 0.8 copy.255
  153.1 12.9 %all-to-all-done.2 = bf16[16,8,8,256]{3,2,1,0:T(8,128)(2,1)S(1)} async-done(((bf16[16,8,8,256]{3,2,1,0:T(8,128)(2,1)}), bf16[16,8,8,256]{3,2,1,0:T(8,128)(2,1)S(1)}, u32[]{:S(2)}, u32[]{:S(2)}) %all-to-all-start.2) | async-done | bytes 524320 | tf_op jit(solution)/shard_map/all_to_all | solution.py:15
  166.0 4.2 %all-to-all-start.7 = ((bf16[16,8,8,128]{3,2,1,0:T(8,128)(2,1)}), bf16[16,8,8,128]{3,2,1,0:T(8,128)(2,1)S(1)}, u32[]{:S(2)}, u32[]{:S(2)}) async-start(bf16[16,8,8,128]{3,2,1,0:T(8,128)(2,1)} %bitcast.262), calls=%async_computation.7 | async-start | bytes 524288 | tf_op jit(solution)/shard_map/all_to_all | solution.py:15
  170.1 0.3 fusion.23
  170.5 9.7 %all-to-all-done.7 = bf16[16,8,8,128]{3,2,1,0:T(8,128)(2,1)S(1)} async-done(((bf16[16,8,8,128]{3,2,1,0:T(8,128)(2,1)}), bf16[16,8,8,128]{3,2,1,0:T(8,128)(2,1)S(1)}, u32[]{:S(2)}, u32[]{:S(2)}) %all-to-all-start.7) | async-done | bytes 262176 | tf_op jit(solution)/shard_map/all_to_all | solution.py:15
  180.5 0.3 fusion.37
  180.8 0.9 copy.183
  181.7 0.8 copy.258
  (64 shorter events, 2.5 us)
Async XLA Ops:
  0.6 41.8 %copy-start = (bf16[256,256]{1,0:T(8,128)(2,1)S(1)}, bf16[256,256]{1,0:T(8,128)(2,1)}, u32[]{:S(2)}) copy-start(bf16[256,256]{1,0:T(8,128)(2,1)} %param.13) | copy-start | bytes 393220
  0.6 23.5 %copy-start.3 = (bf16[256,1024]{1,0:T(8,128)(2,1)S(1)}, bf16[256,1024]{1,0:T(8,128)(2,1)}, u32[]{:S(2)}) copy-start(bf16[256,1024]{1,0:T(8,128)(2,1)} %param.11) | copy-start | bytes 1572868
  20.2 17.8 %all-to-all-start = ((bf16[128,8,256]{2,1,0:T(8,128)(2,1)}), bf16[128,8,256]{2,1,0:T(8,128)(2,1)S(1)}, u32[]{:S(2)}, u32[]{:S(2)}) async-start(bf16[128,8,256]{2,1,0:T(8,128)(2,1)} %param.9), calls=%async_computation | async-start | bytes 1048576 | tf_op jit(solution)/shard_map/all_to_all | solution.py:15
  23.8 1.6 collective-permute-start
  42.5 1.4 copy-start.7
  43.5 6.6 %copy-start.5 = (bf16[1024,128]{1,0:T(8,128)(2,1)S(1)}, bf16[1024,128]{1,0:T(8,128)(2,1)}, u32[]{:S(2)}) copy-start(bf16[1024,128]{1,0:T(8,128)(2,1)} %param.15) | copy-start | bytes 786436
  46.0 19.5 %all-to-all-start.3 = ((bf16[16,8,2304]{2,1,0:T(8,128)(2,1)}), bf16[16,8,2304]{2,1,0:T(8,128)(2,1)S(1)}, u32[]{:S(2)}, u32[]{:S(2)}) async-start(bf16[16,8,2304]{2,1,0:T(8,128)(2,1)} %bitcast.42), calls=%async_computation.3 | async-start | bytes 1179648 | tf_op jit(solution)/shard_map/all_to_all | solution.py:15
  65.6 12.2 %collective-permute-start.1 = (bf16[128,2048]{1,0:T(8,128)(2,1)S(1)}, bf16[128,2048]{1,0:T(8,128)(2,1)}, u32[]{:S(2)}, u32[]{:S(2)}) collective-permute-start(bf16[128,2048]{1,0:T(8,128)(2,1)S(1)} %get-tuple-element.15), channel_id=1, source_target_pairs={{0,1},{1,0},{2,3},{3,2},{4,5},{5,4},{6,7},{7,6},{8,9},{9,8},{10,11... | collective-permute-start | bytes 1572872 | tf_op jit(solution)/shard_map/ppermute | solution.py:20
  69.5 7.3 %copy-start.4 = (bf16[2,128,640]{2,1,0:T(8,128)(2,1)S(1)}, bf16[2,128,640]{2,1,0:T(8,128)(2,1)}, u32[]{:S(2)}) copy-start(bf16[2,128,640]{2,1,0:T(8,128)(2,1)} %param.16) | copy-start | bytes 983044
  77.6 0.7 copy-start.2
  106.2 11.1 %copy-start.1 = (bf16[1,128,640]{2,1,0:T(8,128)(2,1)S(1)}, bf16[1,128,640]{2,1,0:T(8,128)(2,1)}, u32[]{:S(2)}) copy-start(bf16[1,128,640]{2,1,0:T(8,128)(2,1)} %get-tuple-element.20) | copy-start | bytes 491524
  110.5 17.3 %copy-start.6 = (bf16[2,128,128]{2,1,0:T(8,128)(2,1)S(1)}, bf16[2,128,128]{2,1,0:T(8,128)(2,1)}, u32[]{:S(2)}) copy-start(bf16[2,128,128]{2,1,0:T(8,128)(2,1)} %param.17) | copy-start | bytes 196612
  113.2 14.2 %all-to-all-start.5 = ((bf16[16,8,8,128]{3,2,1,0:T(8,128)(2,1)}), bf16[16,8,8,128]{3,2,1,0:T(8,128)(2,1)S(1)}, u32[]{:S(2)}, u32[]{:S(2)}) async-start(bf16[16,8,8,128]{3,2,1,0:T(8,128)(2,1)} %copy.168), calls=%async_computation.5 | async-start | bytes 524288 | tf_op jit(solution)/shard_map/all_to_all | solution.py:15
  129.8 17.8 %all-to-all-start.6 = ((bf16[16,2,8,8,128]{4,2,1,3,0:T(8,128)(2,1)}), bf16[16,2,8,8,128]{4,2,1,3,0:T(8,128)(2,1)S(1)}, u32[]{:S(2)}, u32[]{:S(2)}) async-start(bf16[16,2,8,8,128]{4,2,1,3,0:T(8,128)(2,1)} %copy.177), calls=%async_computation.6 | async-start | bytes 1048576 | tf_op jit(solution)/shard_map/all_to_all | solution.py:15
  147.6 18.4 %all-to-all-start.2 = ((bf16[16,8,8,256]{3,2,1,0:T(8,128)(2,1)}), bf16[16,8,8,256]{3,2,1,0:T(8,128)(2,1)S(1)}, u32[]{:S(2)}, u32[]{:S(2)}) async-start(bf16[16,8,8,256]{3,2,1,0:T(8,128)(2,1)} %copy_bitcast_fusion), calls=%async_computation.2 | async-start | bytes 1048576 | tf_op jit(solution)/shard_map/all_to_all | solution.py:15
  166.0 14.2 %all-to-all-start.7 = ((bf16[16,8,8,128]{3,2,1,0:T(8,128)(2,1)}), bf16[16,8,8,128]{3,2,1,0:T(8,128)(2,1)S(1)}, u32[]{:S(2)}, u32[]{:S(2)}) async-start(bf16[16,8,8,128]{3,2,1,0:T(8,128)(2,1)} %bitcast.262), calls=%async_computation.7 | async-start | bytes 524288 | tf_op jit(solution)/shard_map/all_to_all | solution.py:15

commit v2 on v1

--- a/solution.py
+++ b/solution.py
@@ -1,6 +1,10 @@
+import math
+
 import jax
 import jax.numpy as jnp
 from jax import lax
+from jax.experimental import pallas as pl
+from jax.experimental.pallas import tpu as pltpu
 from jax.sharding import PartitionSpec as P
 
 
@@ -15,9 +19,457 @@
     return lax.all_to_all(blocks, "res", split_axis=0, concat_axis=0, tiled=True)
 
 
-def with_partner(values):
+def across(values, bit):
     count = lax.axis_size("res")
-    return lax.ppermute(values, "res", [(k, k ^ 1) for k in range(count)])
+    return lax.ppermute(values, "res", [(k, k ^ bit) for k in range(count)])
+
+
+def params(megabytes=16):
+    return pltpu.CompilerParams(vmem_limit_bytes=megabytes << 20)
+
+
+def whole(count):
+    return [pl.BlockSpec(memory_space=pltpu.VMEM)] * count
+
+
+def lanes_norm(values):
+    centred = values - jnp.mean(values, axis=-1, keepdims=True)
+    spread = jnp.mean(centred * centred, axis=-1, keepdims=True)
+    return centred * lax.rsqrt(spread + 1e-05)
+
+
+def row_edges(pair_row, entry, edges_ref, r):
+    count, _, _, share, lanes = edges_ref.shape
+    width = count * share
+    normed = lanes_norm(pair_row).astype(jnp.bfloat16)
+    mapped = lax.dot_general(
+        entry, normed, (((1,), (1,)), ((), ())), preferred_element_type=jnp.float32
+    )
+    for side in range(2):
+        base = 2 * side * width
+        edge = jax.nn.sigmoid(mapped[base : base + width]) * mapped[base + width : base + 2 * width]
+        edges_ref[:, side, r] = edge.reshape(count, share, lanes).astype(jnp.bfloat16)
+
+
+def product_kernel(incoming, arrived_ref, product_ref, left_ref, right_ref):
+    count, _, strands, share, lanes = arrived_ref.shape
+    rows = count * strands
+    for side, ref in enumerate((left_ref, right_ref)):
+        ref[...] = arrived_ref[:, side].astype(jnp.float32).reshape(rows * share, lanes)
+    dims = (((0,), (0,)), ((), ())) if incoming else (((1,), (1,)), ((), ()))
+    for ch in range(share):
+        left = left_ref[pl.ds(ch, rows, stride=share), :].astype(jnp.bfloat16)
+        right = right_ref[pl.ds(ch, rows, stride=share), :].astype(jnp.bfloat16)
+        out = lax.dot_general(left, right, dims, preferred_element_type=jnp.float32)
+        product_ref[:, ch] = out.reshape(count, strands, lanes).astype(jnp.bfloat16)
+
+
+def product_call(arrived, incoming):
+    count, _, strands, share, lanes = arrived.shape
+    scratch = pltpu.VMEM((count * strands * share, lanes), jnp.float32)
+    return pl.pallas_call(
+        lambda *refs: product_kernel(incoming, *refs),
+        out_shape=jax.ShapeDtypeStruct((count, share, strands, lanes), jnp.bfloat16),
+        in_specs=whole(1),
+        out_specs=pl.BlockSpec(memory_space=pltpu.VMEM),
+        scratch_shapes=[scratch, scratch],
+        compiler_params=params(),
+        name="edge_product",
+    )(arrived)
+
+
+def exit_rows(gathered_ref, exit_ref, pair_ref, gate_ref, out_ref, spread_ref, each):
+    count, share, strands, lanes = gathered_ref.shape
+    width = count * share
+    spread_ref[...] = gathered_ref[...].astype(jnp.float32).reshape(width * strands, lanes)
+    for r in range(strands):
+        edges = spread_ref[pl.ds(r, width, stride=strands), :]
+        centred = edges - jnp.mean(edges, axis=0, keepdims=True)
+        spread = jnp.mean(centred * centred, axis=0, keepdims=True)
+        normed = (centred * lax.rsqrt(spread + 1e-05)).astype(jnp.bfloat16)
+        update = lax.dot_general(
+            normed, exit_ref[...], (((0,), (0,)), ((), ())), preferred_element_type=jnp.float32
+        )
+        new = (pair_ref[r].astype(jnp.float32) + gate_ref[r] * update).astype(jnp.bfloat16)
+        out_ref[r] = new
+        each(r, new)
+
+
+def exit_entry_kernel(gathered_ref, exit_ref, pair_ref, gate_ref, entry_ref, out_ref, edges_ref, spread_ref):
+    entry = entry_ref[...]
+
+    def each(r, new):
+        row_edges(new.astype(jnp.float32), entry, edges_ref, r)
+
+    exit_rows(gathered_ref, exit_ref, pair_ref, gate_ref, out_ref, spread_ref, each)
+
+
+def exit_kernel(gathered_ref, exit_ref, pair_ref, gate_ref, out_ref, spread_ref):
+    exit_rows(gathered_ref, exit_ref, pair_ref, gate_ref, out_ref, spread_ref, lambda r, new: None)
+
+
+def exit_call(gathered, weight, pair_prev, gate, entry=None):
+    count, share, strands, lanes = gathered.shape
+    pair = jax.ShapeDtypeStruct(pair_prev.shape, jnp.bfloat16)
+    scratch = [pltpu.VMEM((count * share * strands, lanes), jnp.float32)]
+    if entry is None:
+        return pl.pallas_call(
+            exit_kernel,
+            out_shape=pair,
+            in_specs=whole(4),
+            out_specs=pl.BlockSpec(memory_space=pltpu.VMEM),
+            scratch_shapes=scratch,
+            compiler_params=params(),
+            name="triangle_exit",
+        )(gathered, weight, pair_prev, gate)
+    edges = jax.ShapeDtypeStruct((count, 2, strands, share, lanes), jnp.bfloat16)
+    return pl.pallas_call(
+        exit_entry_kernel,
+        out_shape=(pair, edges),
+        in_specs=whole(5),
+        out_specs=tuple(whole(2)),
+        scratch_shapes=scratch,
+        compiler_params=params(),
+        name="triangle_exit_entry",
+    )(gathered, weight, pair_prev, gate, entry)
+
+
+def opm_kernel(
+    core_ref, flanks_ref, other_ref, coupling_ref, final_ref, entry_ref, pair_ref, edges_ref, outer_ref
+):
+    chains = flanks_ref.shape[0]
+    strands, total_res, width = coupling_ref.shape
+    depth = final_ref.shape[0] // 128
+    groups = final_ref.shape[1] // width
+    half = total_res // 2
+    flat = strands * depth
+    span = 8 * depth
+    blocks = flat // 128
+    left = flanks_ref[:, :flat]
+    for which in range(2):
+        for pair in range(half // 16):
+            parts = []
+            for jg in (2 * pair, 2 * pair + 1):
+                source = other_ref if which else flanks_ref
+                right = source[:, flat + jg * span : flat + (jg + 1) * span]
+                part = lax.dot_general(
+                    right, left, (((0,), (0,)), ((), ())), preferred_element_type=jnp.float32
+                ) * (1.0 / chains)
+                parts.append(part.reshape(depth, 8, flat))
+            both = jnp.concatenate(parts, axis=1).astype(jnp.bfloat16)
+            for ig in range(blocks):
+                at = ig * total_res + which * half + pair * 16
+                for e in range(depth):
+                    outer_ref[at : at + 16, e * 128 : (e + 1) * 128] = both[e, :, ig * 128 : (ig + 1) * 128]
+    core = core_ref[0]
+    for ig in range(blocks):
+        update = jnp.dot(
+            outer_ref[ig * total_res : (ig + 1) * total_res, :],
+            final_ref[...],
+            preferred_element_type=jnp.float32,
+        )
+        for which in range(2):
+            at = pl.multiple_of(half * (core if which == 0 else 1 - core), half)
+            for i4 in range(groups):
+                i = ig * groups + i4
+                piece = update[which * half : (which + 1) * half, i4 * width : (i4 + 1) * width]
+                prev = coupling_ref[i, pl.ds(at, half), :].astype(jnp.float32)
+                pair_ref[i, pl.ds(at, half), :] = (prev + piece).astype(jnp.bfloat16)
+    entry = entry_ref[...]
+    for r in range(strands):
+        row_edges(pair_ref[r].astype(jnp.float32), entry, edges_ref, r)
+
+
+def opm_call(core, flanks, other, coupling, final, entry, count):
+    strands, total_res, width = coupling.shape
+    share = width // count
+    rows = strands * 128 // (128 * final.shape[1] // width) * total_res
+    return pl.pallas_call(
+        opm_kernel,
+        out_shape=(
+            jax.ShapeDtypeStruct(coupling.shape, jnp.bfloat16),
+            jax.ShapeDtypeStruct((count, 2, strands, share, total_res), jnp.bfloat16),
+        ),
+        in_specs=[pl.BlockSpec(memory_space=pltpu.SMEM)] + whole(5),
+        out_specs=tuple(whole(2)),
+        scratch_shapes=[pltpu.VMEM((rows, final.shape[0]), jnp.bfloat16)],
+        compiler_params=params(24),
+        name="outer_product_entry",
+    )(core, flanks, other, coupling, final, entry)
+
+
+def gate_kernel(pair_ref, weight_ref, gate_ref):
+    for r in range(pair_ref.shape[0]):
+        normed = lanes_norm(pair_ref[r].astype(jnp.float32)).astype(jnp.bfloat16)
+        gate_ref[r] = jax.nn.sigmoid(
+            jnp.dot(normed, weight_ref[...], preferred_element_type=jnp.float32)
+        )
+
+
+def gate_call(pair, weight):
+    return pl.pallas_call(
+        gate_kernel,
+        out_shape=jax.ShapeDtypeStruct(pair.shape, jnp.float32),
+        in_specs=whole(2),
+        out_specs=pl.BlockSpec(memory_space=pltpu.VMEM),
+        compiler_params=params(),
+        name="pair_gate",
+    )(pair, weight)
+
+
+def prepare_kernel(
+    final_ref,
+    entry_ref,
+    average_ref,
+    project_ref,
+    block_ref,
+    sides_ref,
+    gates_ref,
+    left_ref,
+    right_ref,
+    turned_ref,
+    wide_ref,
+):
+    turned_ref[...] = project_ref[...].astype(jnp.float32).T.astype(jnp.bfloat16)
+    channels = average_ref.shape[1] // 2
+    for ref, first, lane_of in (
+        (left_ref, 0, lambda ch, g, size: g * channels + ch),
+        (right_ref, channels, lambda ch, g, size: ch * size + g),
+    ):
+        size, _, lanes = ref.shape
+        for g in range(size):
+            ch = lax.broadcasted_iota(jnp.int32, (2 * channels, lanes), 0) - first
+            lane = lax.broadcasted_iota(jnp.int32, (2 * channels, lanes), 1)
+            chosen = (lane_of(ch, g, size) == lane) & (ch >= 0) & (ch < channels)
+            placed = jnp.dot(
+                average_ref[...],
+                jnp.where(chosen, 1.0, 0.0).astype(jnp.bfloat16),
+                preferred_element_type=jnp.float32,
+            )
+            ref[g] = placed.astype(jnp.bfloat16)
+    width = final_ref.shape[1]
+    depth = block_ref.shape[0] // 128
+    groups = 128 // depth
+    wide_ref[...] = final_ref[...].astype(jnp.float32)
+    block_ref[...] = jnp.zeros(block_ref.shape, block_ref.dtype)
+    for e in range(depth):
+        piece = wide_ref[pl.ds(e, depth, stride=depth), :].astype(jnp.bfloat16)
+        for g in range(groups):
+            at = e * 128 + g * depth
+            block_ref[at : at + depth, g * width : (g + 1) * width] = piece
+    for d in range(2):
+        sides = entry_ref[d, :, : 4 * width].astype(jnp.float32)
+        sides_ref[d] = sides.T.astype(jnp.bfloat16)
+        gates_ref[d] = entry_ref[d, :, 4 * width :]
+
+
+def prepare_call(final, entries, average, project):
+    depth = math.isqrt(final.shape[0])
+    width = final.shape[1]
+    groups = 128 // depth
+    return pl.pallas_call(
+        prepare_kernel,
+        out_shape=(
+            jax.ShapeDtypeStruct((depth * 128, groups * width), jnp.bfloat16),
+            jax.ShapeDtypeStruct((2, 4 * width, width), jnp.bfloat16),
+            jax.ShapeDtypeStruct((2, width, width), jnp.bfloat16),
+            jax.ShapeDtypeStruct((groups, average.shape[0], 128), jnp.bfloat16),
+            jax.ShapeDtypeStruct((8, average.shape[0], 8 * depth), jnp.bfloat16),
+            jax.ShapeDtypeStruct(project.shape[::-1], jnp.bfloat16),
+        ),
+        in_specs=whole(4),
+        out_specs=tuple(whole(6)),
+        scratch_shapes=[pltpu.VMEM(final.shape, jnp.float32)],
+        compiler_params=params(24),
+        name="prepare_weights",
+    )(final, entries, average, project)
+
+
+def pack_kernel(msa_ref, pair_ref, weight_ref, out_ref):
+    count, chains, parts = out_ref.shape[:3]
+    for d in range(count):
+        for k in range(parts - 1):
+            out_ref[d, :, k] = msa_ref[d * chains : (d + 1) * chains, :, k * 128 : (k + 1) * 128]
+    for r in range(pair_ref.shape[0]):
+        normed = lanes_norm(pair_ref[r].astype(jnp.float32)).astype(jnp.bfloat16)
+        bias = lax.dot_general(
+            weight_ref[...], normed, (((1,), (1,)), ((), ())), preferred_element_type=jnp.float32
+        )
+        upper = bias.astype(jnp.bfloat16)
+        lower = (bias - upper.astype(jnp.float32)).astype(jnp.bfloat16)
+        for d in range(count):
+            out_ref[d, r, parts - 1] = lower if d % 2 else upper
+
+
+def pack_call(msa, pair, weight, count):
+    chains, strands, depth = msa.shape
+    return pl.pallas_call(
+        pack_kernel,
+        out_shape=jax.ShapeDtypeStruct(
+            (count, chains // count, depth // 128 + 1, strands, 128), jnp.bfloat16
+        ),
+        in_specs=whole(3),
+        out_specs=pl.BlockSpec(memory_space=pltpu.VMEM),
+        compiler_params=params(),
+        name="pack_rows",
+    )(msa, pair, weight.T)
+
+
+def arrived_rows(arrived_ref, s):
+    count, _, parts, strands, lanes = arrived_ref.shape
+    pieces = [
+        arrived_ref[:, s, k].astype(jnp.float32).reshape(count * strands, lanes)
+        for k in range(parts - 1)
+    ]
+    return jnp.concatenate(pieces, axis=-1)
+
+
+def project_kernel(arrived_ref, weight_ref, query_ref, key_ref, value_ref, gate_ref):
+    inner = query_ref.shape[1]
+    for s in range(query_ref.shape[0]):
+        normed = lanes_norm(arrived_rows(arrived_ref, s)).astype(jnp.bfloat16)
+        mapped = lax.dot_general(
+            weight_ref[...], normed, (((1,), (1,)), ((), ())), preferred_element_type=jnp.float32
+        )
+        for k, ref in enumerate((query_ref, key_ref, value_ref)):
+            ref[s] = mapped[k * inner : (k + 1) * inner].astype(jnp.bfloat16)
+        gate_ref[s] = jax.nn.sigmoid(mapped[3 * inner :])
+
+
+def project_call(arrived, weight):
+    count, chains, _, strands, _ = arrived.shape
+    turned = (chains, weight.shape[0] // 4, count * strands)
+    half = jax.ShapeDtypeStruct(turned, jnp.bfloat16)
+    return pl.pallas_call(
+        project_kernel,
+        out_shape=(half, half, half, jax.ShapeDtypeStruct(turned, jnp.float32)),
+        in_specs=whole(2),
+        out_specs=tuple(whole(4)),
+        compiler_params=params(),
+        name="project_rows",
+    )(arrived, weight)
+
+
+def attend_kernel(
+    width,
+    arrived_ref,
+    other_ref,
+    query_ref,
+    key_ref,
+    value_ref,
+    gate_ref,
+    final_ref,
+    left_ref,
+    right_ref,
+    mixed_ref,
+    flanks_ref,
+    bias_ref,
+    turned_ref,
+    scaled_ref,
+):
+    count, chains, strands, depth = mixed_ref.shape
+    inner, total_res = query_ref.shape[1:]
+    heads = inner // width
+    mine = arrived_ref[:, :, arrived_ref.shape[2] - 1].astype(jnp.float32)
+    bias = mine + other_ref[...].astype(jnp.float32)
+    bias_ref[...] = bias.reshape(total_res * heads, total_res)
+    for h in range(heads):
+        turned_ref[h] = bias_ref[pl.ds(h, total_res, stride=heads), :].T
+    scale = width ** (-0.5)
+    for s in range(chains):
+        attended = []
+        for h in range(heads):
+            at = slice(h * width, (h + 1) * width)
+            scores = lax.dot_general(
+                key_ref[s, at],
+                query_ref[s, at],
+                (((0,), (0,)), ((), ())),
+                preferred_element_type=jnp.float32,
+            )
+            scores = scores * scale + turned_ref[h]
+            weights = jnp.exp(scores - jnp.max(scores, axis=0, keepdims=True))
+            weights = weights * (1.0 / jnp.sum(weights, axis=0, keepdims=True))
+            attended.append(
+                jnp.dot(
+                    value_ref[s, at],
+                    weights.astype(jnp.bfloat16),
+                    preferred_element_type=jnp.float32,
+                )
+            )
+        attended = jnp.concatenate(attended).astype(jnp.bfloat16).astype(jnp.float32)
+        gated = (attended * gate_ref[s]).astype(jnp.bfloat16)
+        increment = lax.dot_general(
+            gated, final_ref[...], (((0,), (0,)), ((), ())), preferred_element_type=jnp.float32
+        )
+        mixed = (arrived_rows(arrived_ref, s) + increment).astype(jnp.bfloat16)
+        mixed = mixed.astype(jnp.float32)
+        normed = lanes_norm(mixed)
+        for k in range(depth // 128):
+            scaled_ref[k, pl.ds(s, total_res, stride=chains), :] = normed[:, k * 128 : (k + 1) * 128]
+        mixed_ref[:, s] = mixed.reshape(count, strands, depth).astype(jnp.bfloat16)
+
+    scaled = jnp.concatenate([scaled_ref[k] for k in range(depth // 128)], axis=-1)
+    scaled = scaled.reshape(total_res, chains, depth)
+
+    def side(weights_ref):
+        group, _, lanes = weights_ref.shape
+        total = None
+        grouped = scaled.reshape(total_res // group, group, chains, depth)
+        for g in range(group):
+            part = grouped[:, g].reshape(total_res // group * chains, depth).astype(jnp.bfloat16)
+            out = jnp.dot(part, weights_ref[g], preferred_element_type=jnp.float32)
+            total = out if total is None else total + out
+        return total.reshape(total_res // group, chains, lanes).astype(jnp.bfloat16)
+
+    left, right = side(left_ref), side(right_ref)
+    lefts, rights = left.shape[0] // count, right.shape[0] // 2
+    for d in range(count):
+        at = 0
+        for k in range(lefts):
+            flanks_ref[d, :, at : at + left.shape[2]] = left[d * lefts + k]
+            at += left.shape[2]
+        for k in range(rights):
+            flanks_ref[d, :, at : at + right.shape[2]] = right[(d % 2) * rights + k]
+            at += right.shape[2]
+
+
+def attend_call(arrived, other, projected, width, final, left, right):
+    count, chains, parts, strands, _ = arrived.shape
+    inner, total_res = projected[0].shape[1:]
+    depth, heads = (parts - 1) * 128, inner // width
+    lanes = strands // left.shape[0] * left.shape[2] + total_res // 2 // right.shape[0] * right.shape[2]
+    return pl.pallas_call(
+        lambda *refs: attend_kernel(width, *refs),
+        out_shape=(
+            jax.ShapeDtypeStruct((count, chains, strands, depth), jnp.bfloat16),
+            jax.ShapeDtypeStruct((count, chains, lanes), jnp.bfloat16),
+        ),
+        in_specs=whole(9),
+        out_specs=tuple(whole(2)),
+        scratch_shapes=[
+            pltpu.VMEM((total_res * heads, total_res), jnp.float32),
+            pltpu.VMEM((heads, total_res, total_res), jnp.float32),
+            pltpu.VMEM((depth // 128, total_res * chains, 128), jnp.float32),
+        ],
+        compiler_params=params(),
+        name="attend_rows",
+    )(arrived, other, *projected, final, left, right)
+
+
+def pair_track(core, flanks, other, coupling, prepared, exits):
+    final, sides, gates = prepared[:3]
+    count = lax.axis_size("res")
+    pair, edges = opm_call(core, flanks, other, coupling, final, sides[0], count)
+    for d in range(2):
+        arrived = exchange(edges)
+        gate = gate_call(pair, gates[d])
+        product = product_call(arrived, d == 1)
+        gathered = exchange(product)
+        if d == 0:
+            pair, edges = exit_call(gathered, exits[0], pair, gate, sides[1])
+        else:
+            pair = exit_call(gathered, exits[1], pair, gate)
+    return pair
 
 
 def triangle(pair_prev, weight_in, weight_out, contraction):
@@ -66,18 +518,48 @@
     tensor_depth = tensor_average_matrix.shape[1] // 2
     half = total_res // 2
 
+    fits = (
+        pair_width == 128
+        and pair_width % (8 * count) == 0
+        and count & (count - 1) == 0
+        and total_res == 128
+        and local_strands == 8
+        and per_device == 8
+        and heads == 8
+        and heads * width == depth
+        and depth % 128 == 0
+        and tensor_depth == 32
+    )
+    if fits:
+        prepared = prepare_call(
+            tensor_average_final,
+            trilateral_entry_matrix,
+            tensor_average_matrix,
+            query_key_matrix,
+        )
+        packed = pack_call(alignment_embedding, coupling_embedding, coupling_logit_matrix, count)
+        arrived = exchange(packed)
+        other = across(arrived[:, :, -1], 1)
+        projected = project_call(arrived, prepared[5])
+        mixed, flanks = attend_call(
+            arrived, other, projected, width, focus_final_matrix, *prepared[3:5]
+        )
+        flanks = exchange(flanks)
+        flanks = flanks.reshape(chain_tally, -1)
+        other = across(flanks, 1)
+        mixed_out = exchange(mixed).reshape(chain_tally, local_strands, depth)
+        refreshed = pair_track(
+            core.reshape(1), flanks, other, coupling_embedding, prepared, trilateral_exit_matrix
+        )
+        return (mixed_out, refreshed)
+
     rows = exchange(alignment_embedding).reshape(count, per_device, local_strands, depth)
     rows = rows.transpose(1, 0, 2, 3).reshape(per_device, total_res, depth)
-
     pair_norm = standardise_entries(coupling_embedding, -1).astype(jnp.bfloat16)
     bias_rows = jnp.einsum(
         "rnc,ch->hrn", pair_norm, coupling_logit_matrix, preferred_element_type=jnp.float32
     )
-    upper = lax.reduce_precision(bias_rows, 8, 7)
-    terms = jnp.stack([upper, bias_rows - upper]).astype(jnp.bfloat16)
-    term = exchange(jnp.tile(terms, (count // 2, 1, 1, 1)))
-    bias = term.astype(jnp.float32) + with_partner(term).astype(jnp.float32)
-    bias = bias.transpose(1, 0, 2, 3).reshape(heads, total_res, total_res)
+    bias = lax.all_gather(bias_rows, "res", axis=1, tiled=True)
 
     standard = standardise_entries(rows, -1).astype(jnp.bfloat16)
     projection = query_key_matrix.reshape(depth, 4, heads, width)
@@ -115,7 +597,7 @@
     ).astype(jnp.bfloat16)
     left = flank[0].reshape(per_device, count // 2, 2, local_strands * tensor_depth)
     left = left.transpose(1, 2, 0, 3)
-    right = flank[1].reshape(per_device, 2, half, tensor_depth).transpose(1, 0, 3, 2)
+    right = flank[1].reshape(per_device, 2, half // 8, 8, tensor_depth).transpose(1, 0, 2, 4, 3)
     right = right.reshape(2, per_device, tensor_depth * half)
     right = jnp.broadcast_to(right, (count // 2,) + right.shape)
     flanks = jnp.concatenate([left, right], axis=-1).reshape(count, per_device, -1)
@@ -125,25 +607,24 @@
     ).reshape(chain_tally, local_strands, depth)
 
     flanks = flanks.reshape(chain_tally, -1)
+    mine = flanks[:, local_strands * tensor_depth :]
+    other = across(mine, 1)
+    group = max(1, 128 // tensor_depth)
+    final = tensor_average_final.reshape(tensor_depth, tensor_depth, pair_width)
+    final = jnp.einsum("ab,cef->eacbf", jnp.eye(group, dtype=final.dtype), final)
+    final = final.reshape(tensor_depth * group * tensor_depth, group * pair_width)
     left_all = flanks[:, : local_strands * tensor_depth]
-    mine = flanks[:, local_strands * tensor_depth :]
-    other = with_partner(mine)
     both = jnp.stack([mine, other])
-    both = jnp.where(core == 0, both, both[::-1]).reshape(2, chain_tally, tensor_depth, half)
-    group = 4 if local_strands % 4 == 0 else 1
-    final = tensor_average_final.reshape(tensor_depth, tensor_depth, pair_width)
-    final = jnp.einsum(
-        "ab,cef->eacbf", jnp.eye(group, dtype=final.dtype), final
-    ).reshape(tensor_depth, group * tensor_depth, group * pair_width)
+    both = jnp.where(core == 0, both, both[::-1])
+    both = both.reshape(2, chain_tally, half // 8, tensor_depth, 8)
     outer = jnp.einsum(
-        "xsej,sgm->exjgm",
+        "xsaej,sgm->gxajem",
         both,
         left_all.reshape(chain_tally, local_strands // group, group * tensor_depth),
         preferred_element_type=jnp.float32,
     ) * (1.0 / chain_tally)
-    opm = jnp.einsum(
-        "exjgm,emn->gxjn", outer.astype(jnp.bfloat16), final, preferred_element_type=jnp.float32
-    )
+    outer = outer.astype(jnp.bfloat16).reshape(local_strands // group, total_res, -1)
+    opm = jnp.einsum("gjk,kn->gjn", outer, final, preferred_element_type=jnp.float32)
     opm = opm.reshape(local_strands // group, total_res, group, pair_width)
     opm = opm.transpose(0, 2, 1, 3).reshape(local_strands, total_res, pair_width)
     pair_mid = (coupling_embedding.astype(jnp.float32) + opm).astype(jnp.bfloat16)

time: 184 us -> 160 us (0.87)
  blocking collectives: 35.9 us -> 81.8 us
  waiting for transfers between devices: 73.3 us -> 34.1 us
  Pallas kernels: 0 us -> 22.4 us
  local copies, waits for them, and re-layouts: 24.4 us -> 6.17 us
  matrix products: 13.2 us -> 0 us
  starting transfers between devices: 24.3 us -> 13.6 us
  other arithmetic: 10 us -> 0 us
    all_to_all x2 -> x4, blocking collectives: 35.9 us -> 81.8 us  [exchange(): lax.all_to_all(blocks, 'res', split_axis=0, concat_axis=0, tiled=True)]
    all_to_all x6 -> x3, waiting for transfers between devices: 72.3 us -> 32.2 us  [exchange(): lax.all_to_all(blocks, 'res', split_axis=0, concat_axis=0, tiled=True)]
    pallas_call x0 -> x11, Pallas kernels: none -> 22.4 us  [the longest x1 10.6 us: attend_call(): pl.pallas_call(lambda *refs: attend_kernel(width, *refs), out_shape=(jax....]
    dot_general x15 -> x0, matrix products: 13.2 us -> none  [the longest x1 4.74 us: body(): jnp.einsum('exjgm,emn->gxjn', outer.astype(jnp.bfloat16), final, preferre...]
    all_to_all x6 -> x3, starting transfers between devices: 23.7 us -> 12.5 us  [exchange(): lax.all_to_all(blocks, 'res', split_axis=0, concat_axis=0, tiled=True)]
    reshape x5 -> x0, local copies, waits for them, and re-layouts: 8.49 us -> none  [the longest x1 7.26 us: body(): final = jnp.einsum('ab,cef->eacbf', jnp.eye(group, dtype=final.dtype), fi...]
    convert_element_type x3 -> x0, local copies, waits for them, and re-layouts: 5.3 us -> none  [the longest x1 4.24 us: triangle(): product = jnp.einsum(contraction, arrived[:, 0], arrived[:, 1], preferred...]
    transpose x5 -> x0, local copies, waits for them, and re-layouts: 3.8 us -> none  [the longest x1 2.69 us: triangle(): product.reshape(share, count, local_strands, total_res)]
  transfers between devices with their start and end apart: 8 -> 5, of which waited for: 7 -> 4; matrix products, arithmetic and copies ran while one was open for 9% -> 0% of each run, Pallas kernels for 0% -> 3%
where the time goes in v2:
time: 160 us; the launch traced here: 159 us
  blocking collectives  81.8 us (51%)
  waiting for transfers between devices  34.1 us (21%)
  Pallas kernels  22.4 us (14%)
  starting transfers between devices  13.6 us (8%)
  local copies, waits for them, and re-layouts  6.17 us (4%)
    all_to_all x4, blocking collectives, exchange(): lax.all_to_all(blocks, 'res', split_axis=0, concat_axis=0, tiled=True)  81.8 us
    all_to_all x3, waiting for transfers between devices, exchange(): lax.all_to_all(blocks, 'res', split_axis=0, concat_axis=0, tiled=True)  32.2 us
    all_to_all x3, starting transfers between devices, exchange(): lax.all_to_all(blocks, 'res', split_axis=0, concat_axis=0, tiled=True)  12.5 us
    pallas_call x1, Pallas kernels, attend_call(): pl.pallas_call(lambda *refs: attend_kernel(width, *refs), out_shape=(jax....  10.6 us
    unnamed x26, local copies, waits for them, and re-layouts  5.8 us
  transfers between devices with their start and end apart: 5, of which 4 were waited for; matrix products, arithmetic and copies ran while one was open for 0% of the time, Pallas kernels for 3%

profile of v2, /device:TPU:0, one launch (start us, length us, event | category | flops | bytes accessed | tf_op | source)
XLA Modules:
  0.0 158.9 jit_solution(7511992057342961635)
XLA Ops:
  0.6 0.0 copy-start.2
  0.6 0.9 copy-done.2
  1.6 0.0 copy-start.4
  1.6 1.0 copy-done.4
  2.6 0.0 copy-start.9
  2.6 0.7 copy-done.9
  3.3 0.0 copy-start.11
  3.3 0.0 copy-start.5
  3.3 0.0 copy-start.6
  3.3 0.0 copy-start.7
  3.3 0.5 pack_rows.1
  3.9 0.0 copy-start.8
  3.9 0.2 copy.15
  4.1 27.3 %all_to_all.35 = bf16[16,8,3,8,128]{4,3,1,2,0:T(8,128)(2,1)S(1)} all-to-all(bf16[16,8,3,8,128]{4,3,1,2,0:T(8,128)(2,1)S(1)} %copy.15), channel_id=1, replica_groups=mesh['grp'=2,'res'=16] {'res'}, dimensions={0} | all-to-all | bytes 1572864 | tf_op jit(solution)/shard_map/all_to_all | solution.py:19
  31.4 1.0 collective-permute-start
  32.4 0.0 copy-done.11
  32.4 0.1 copy.17.average_ref
  32.5 0.0 copy-done.5
  32.5 0.0 copy-done.6
  32.6 0.0 copy-done.7
  32.6 1.1 prepare_weights.1
  33.7 0.0 copy-start
  33.7 0.1 copy.19.arrived_ref.refs_0_
  33.8 0.0 copy-start.3
  33.9 1.4 project_rows.1
  35.3 0.0 collective-permute-done.refs_1_
  35.3 0.0 copy-done.8
  35.3 10.6 %attend_rows.1 = (bf16[16,8,8,256]{3,2,1,0:T(8,128)(2,1)}, bf16[16,8,2304]{2,1,0:T(8,128)(2,1)S(1)}) custom-call(bf16[16,8,3,8,128]{4,3,2,1,0:T(8,128)(2,1)S(1)} %copy.19.arrived_ref.refs_0_, bf16[16,8,8,128]{3,2,1,0:T(8,128)(2,1)S(1)} %collective-permute-done.refs_1_, bf16[8,256,128]{2,1,0:T(8,128)(2,1)S(1)} %get-tuple-element.19.refs_2_, ...), custom_call_target="tpu_custom_call" | custom-call | tf_op jit(solution)/shard_map/attend_rows/pallas_call | solution.py:441
  45.9 20.4 %all_to_all.36 = bf16[16,8,2304]{2,1,0:T(8,128)(2,1)S(1)} all-to-all(bf16[16,8,2304]{2,1,0:T(8,128)(2,1)S(1)} %get-tuple-element.26), channel_id=1, replica_groups=mesh['grp'=2,'res'=16] {'res'}, dimensions={0} | all-to-all | bytes 1179648 | tf_op jit(solution)/shard_map/all_to_all | solution.py:19
  66.3 0.0 copy-done
  66.3 0.1 collective-permute-start.1
  66.4 0.0 copy-start.10
  66.4 1.9 %collective-permute-done.1.other_ref = bf16[128,2304]{1,0:T(8,128)(2,1)S(1)} collective-permute-done((bf16[128,2304]{1,0:T(8,128)(2,1)S(1)}, bf16[128,2304]{1,0:T(8,128)(2,1)S(1)}, u32[]{:S(2)}, u32[]{:S(2)}) %collective-permute-start.1) | collective-permute-done | bytes 589856 | tf_op jit(solution)/shard_map/ppermute | solution.py:24
  68.3 0.0 copy-done.3
  68.3 0.0 copy-start.1
  68.3 2.2 %copy-done.1 = bf16[4096,512]{1,0:T(8,128)(2,1)S(1)} copy-done((bf16[4096,512]{1,0:T(8,128)(2,1)S(1)}, bf16[4096,512]{1,0:T(8,128)(2,1)}, u32[]{:S(2)}) %copy-start.1) | copy-done | bytes 4194328
  70.5 2.7 %outer_product_entry.1 = (bf16[8,128,128]{2,1,0:T(8,128)(2,1)S(1)}, bf16[16,2,8,8,128]{4,3,2,1,0:T(8,128)(2,1)S(1)}) custom-call(s32[1]{0:T(128)} %bitcast.3.core_ref, bf16[128,2304]{1,0:T(8,128)(2,1)S(1)} %bitcast.21, bf16[128,2304]{1,0:T(8,128)(2,1)S(1)} %collective-permute-done.1.other_ref, bf16[8,128,128]{2,1,0:T(8,128)(2,1)S(1)} %copy-done.3, ...), custom_call_target="tpu_custom_call" | custom-call | tf_op jit(solution)/shard_map/outer_product_entry/pallas_call | solution.py:187
  73.2 17.1 %all_to_all.37.refs_0_ = bf16[16,2,8,8,128]{4,3,2,1,0:T(8,128)(2,1)S(1)} all-to-all(bf16[16,2,8,8,128]{4,3,2,1,0:T(8,128)(2,1)S(1)} %get-tuple-element.29), channel_id=1, replica_groups=mesh['grp'=2,'res'=16] {'res'}, dimensions={0} | all-to-all | bytes 1048576 | tf_op jit(solution)/shard_map/all_to_all | solution.py:19
  90.3 1.0 edge_product.2
  91.3 4.2 %all-to-all-start.4 = ((bf16[16,8,8,128]{3,2,1,0:T(8,128)(2,1)}), bf16[16,8,8,128]{3,2,1,0:T(8,128)(2,1)S(1)}, u32[]{:S(2)}, u32[]{:S(2)}) async-start(bf16[16,8,8,128]{3,2,1,0:T(8,128)(2,1)} %edge_product.2), calls=%async_computation.4 | async-start | bytes 524288 | tf_op jit(solution)/shard_map/all_to_all | solution.py:19
  95.5 0.0 copy-done.10
  95.5 0.5 pair_gate.2.gate_ref
  96.0 9.5 %all-to-all-done.4.gathered_ref = bf16[16,8,8,128]{3,2,1,0:T(8,128)(2,1)S(1)} async-done(((bf16[16,8,8,128]{3,2,1,0:T(8,128)(2,1)}), bf16[16,8,8,128]{3,2,1,0:T(8,128)(2,1)S(1)}, u32[]{:S(2)}, u32[]{:S(2)}) %all-to-all-start.4) | async-done | bytes 262176 | tf_op jit(solution)/shard_map/all_to_all | solution.py:19
  105.5 1.9 %triangle_exit_entry.1 = (bf16[8,128,128]{2,1,0:T(8,128)(2,1)S(1)}, bf16[16,2,8,8,128]{4,3,2,1,0:T(8,128)(2,1)S(1)}) custom-call(bf16[16,8,8,128]{3,2,1,0:T(8,128)(2,1)S(1)} %all-to-all-done.4.gathered_ref, bf16[128,128]{1,0:T(8,128)(2,1)S(1)} %get-tuple-element.39.exit_ref, bf16[8,128,128]{2,1,0:T(8,128)(2,1)S(1)} %get-tuple-element.30.pair_ref, ...), custom_call_target="tpu_custom_call" | custom-call | tf_op jit(solution)/shard_map/triangle_exit_entry/pallas_call | solution.py:126
  107.4 16.9 %all_to_all.38.refs_0_ = bf16[16,2,8,8,128]{4,3,2,1,0:T(8,128)(2,1)S(1)} all-to-all(bf16[16,2,8,8,128]{4,3,2,1,0:T(8,128)(2,1)S(1)} %get-tuple-element.32), channel_id=1, replica_groups=mesh['grp'=2,'res'=16] {'res'}, dimensions={0} | all-to-all | bytes 1048576 | tf_op jit(solution)/shard_map/all_to_all | solution.py:19
  124.3 4.2 %all-to-all-start.1 = ((bf16[16,8,8,256]{3,2,1,0:T(8,128)(2,1)}), bf16[16,8,8,256]{3,2,1,0:T(8,128)(2,1)S(1)}, u32[]{:S(2)}, u32[]{:S(2)}) async-start(bf16[16,8,8,256]{3,2,1,0:T(8,128)(2,1)} %get-tuple-element.25), calls=%async_computation.1 | async-start | bytes 1048576 | tf_op jit(solution)/shard_map/all_to_all | solution.py:19
  128.5 1.1 edge_product.3
  129.6 13.2 %all-to-all-done.1 = bf16[16,8,8,256]{3,2,1,0:T(8,128)(2,1)S(1)} async-done(((bf16[16,8,8,256]{3,2,1,0:T(8,128)(2,1)}), bf16[16,8,8,256]{3,2,1,0:T(8,128)(2,1)S(1)}, u32[]{:S(2)}, u32[]{:S(2)}) %all-to-all-start.1) | async-done | bytes 524320 | tf_op jit(solution)/shard_map/all_to_all | solution.py:19
  142.8 4.2 %all-to-all-start.6 = ((bf16[16,8,8,128]{3,2,1,0:T(8,128)(2,1)}), bf16[16,8,8,128]{3,2,1,0:T(8,128)(2,1)S(1)}, u32[]{:S(2)}, u32[]{:S(2)}) async-start(bf16[16,8,8,128]{3,2,1,0:T(8,128)(2,1)} %edge_product.3), calls=%async_computation.6 | async-start | bytes 524288 | tf_op jit(solution)/shard_map/all_to_all | solution.py:19
  147.0 0.5 pair_gate.3.gate_ref
  147.4 9.5 %all-to-all-done.6.gathered_ref = bf16[16,8,8,128]{3,2,1,0:T(8,128)(2,1)S(1)} async-done(((bf16[16,8,8,128]{3,2,1,0:T(8,128)(2,1)}), bf16[16,8,8,128]{3,2,1,0:T(8,128)(2,1)S(1)}, u32[]{:S(2)}, u32[]{:S(2)}) %all-to-all-start.6) | async-done | bytes 262176 | tf_op jit(solution)/shard_map/all_to_all | solution.py:19
  157.0 1.1 triangle_exit.1
  158.1 0.8 copy.22
  (4 shorter events, 0.0 us)
Async XLA Ops:
  0.6 1.0 copy-start.2
  1.6 1.0 copy-start.4
  2.6 0.7 copy-start.9
  3.3 29.1 %copy-start.11 = (bf16[256,64]{0,1:T(8,128)(2,1)S(1)}, bf16[256,64]{0,1:T(8,128)(2,1)}, u32[]{:S(2)}) copy-start(bf16[256,64]{0,1:T(8,128)(2,1)} %param.14) | copy-start | bytes 98308
  3.3 29.2 %copy-start.5 = (bf16[256,1024]{1,0:T(8,128)(2,1)S(1)}, bf16[256,1024]{1,0:T(8,128)(2,1)}, u32[]{:S(2)}) copy-start(bf16[256,1024]{1,0:T(8,128)(2,1)} %project_ref.1) | copy-start | bytes 1572868
  3.3 29.2 %copy-start.6 = (bf16[2,128,640]{2,1,0:T(8,128)(2,1)S(1)}, bf16[2,128,640]{2,1,0:T(8,128)(2,1)}, u32[]{:S(2)}) copy-start(bf16[2,128,640]{2,1,0:T(8,128)(2,1)} %entry_ref.1) | copy-start | bytes 983044
  3.3 29.2 %copy-start.7 = (bf16[1024,128]{1,0:T(8,128)(2,1)S(1)}, bf16[1024,128]{1,0:T(8,128)(2,1)}, u32[]{:S(2)}) copy-start(bf16[1024,128]{1,0:T(8,128)(2,1)} %final_ref.1) | copy-start | bytes 786436
  3.9 31.4 %copy-start.8 = (bf16[256,256]{1,0:T(8,128)(2,1)S(1)}, bf16[256,256]{1,0:T(8,128)(2,1)}, u32[]{:S(2)}) copy-start(bf16[256,256]{1,0:T(8,128)(2,1)} %refs_6_.1) | copy-start | bytes 393220
  31.4 3.9 %collective-permute-start = (bf16[16,8,8,128]{3,2,1,0:T(8,128)(2,1)S(1)}, bf16[16,8,8,128]{3,2,1,0:T(8,128)(2,1)S(1)}, u32[]{:S(2)}, u32[]{:S(2)}) collective-permute-start(bf16[16,8,8,128]{3,2,1,0:T(8,128)(2,1)S(1)} %slice_bitcast_fusion), channel_id=1, source_target_pairs={{0,1},{1,0},{2,3},{3,2},{4,5},{5,4},{6,7},{7,6},{8,9},{9,8},{10,11... | collective-permute-start | bytes 786440 | tf_op jit(solution)/shard_map/ppermute | solution.py:24
  33.7 32.6 %copy-start = (bf16[4096,512]{1,0:T(8,128)(2,1)}, bf16[4096,512]{1,0:T(8,128)(2,1)S(1)}, u32[]{:S(2)}) copy-start(bf16[4096,512]{1,0:T(8,128)(2,1)S(1)} %get-tuple-element.27.final_ref) | copy-start | bytes 12582916
  33.8 34.5 %copy-start.3 = (bf16[8,128,128]{2,1,0:T(8,128)(2,1)S(1)}, bf16[8,128,128]{2,1,0:T(8,128)(2,1)}, u32[]{:S(2)}) copy-start(bf16[8,128,128]{2,1,0:T(8,128)(2,1)} %coupling_ref.1) | copy-start | bytes 786436
  66.3 2.0 %collective-permute-start.1 = (bf16[128,2304]{1,0:T(8,128)(2,1)S(1)}, bf16[128,2304]{1,0:T(8,128)(2,1)S(1)}, u32[]{:S(2)}, u32[]{:S(2)}) collective-permute-start(bf16[128,2304]{1,0:T(8,128)(2,1)S(1)} %bitcast.20), channel_id=1, source_target_pairs={{0,1},{1,0},{2,3},{3,2},{4,5},{5,4},{6,7},{7,6},{8,9},{9,8},{10,11... | collective-permute-start | bytes 1769480 | tf_op jit(solution)/shard_map/ppermute | solution.py:24
  66.4 29.1 %copy-start.10 = (bf16[2,128,128]{2,1,0:T(8,128)(2,1)S(1)}, bf16[2,128,128]{2,1,0:T(8,128)(2,1)}, u32[]{:S(2)}) copy-start(bf16[2,128,128]{2,1,0:T(8,128)(2,1)} %param.17) | copy-start | bytes 196612
  68.3 2.2 %copy-start.1 = (bf16[4096,512]{1,0:T(8,128)(2,1)S(1)}, bf16[4096,512]{1,0:T(8,128)(2,1)}, u32[]{:S(2)}) copy-start(bf16[4096,512]{1,0:T(8,128)(2,1)} %copy-done) | copy-start | bytes 12582916
  91.3 14.2 %all-to-all-start.4 = ((bf16[16,8,8,128]{3,2,1,0:T(8,128)(2,1)}), bf16[16,8,8,128]{3,2,1,0:T(8,128)(2,1)S(1)}, u32[]{:S(2)}, u32[]{:S(2)}) async-start(bf16[16,8,8,128]{3,2,1,0:T(8,128)(2,1)} %edge_product.2), calls=%async_computation.4 | async-start | bytes 524288 | tf_op jit(solution)/shard_map/all_to_all | solution.py:19
  124.3 18.4 %all-to-all-start.1 = ((bf16[16,8,8,256]{3,2,1,0:T(8,128)(2,1)}), bf16[16,8,8,256]{3,2,1,0:T(8,128)(2,1)S(1)}, u32[]{:S(2)}, u32[]{:S(2)}) async-start(bf16[16,8,8,256]{3,2,1,0:T(8,128)(2,1)} %get-tuple-element.25), calls=%async_computation.1 | async-start | bytes 1048576 | tf_op jit(solution)/shard_map/all_to_all | solution.py:19
  142.8 14.2 %all-to-all-start.6 = ((bf16[16,8,8,128]{3,2,1,0:T(8,128)(2,1)}), bf16[16,8,8,128]{3,2,1,0:T(8,128)(2,1)S(1)}, u32[]{:S(2)}, u32[]{:S(2)}) async-start(bf16[16,8,8,128]{3,2,1,0:T(8,128)(2,1)} %edge_product.3), calls=%async_computation.6 | async-start | bytes 524288 | tf_op jit(solution)/shard_map/all_to_all | solution.py:19

commit v3 on v2

--- a/solution.py
+++ b/solution.py
@@ -8,6 +8,9 @@
 from jax.sharding import PartitionSpec as P
 
 
+LOG2E = math.log2(math.e)
+
+
 def standardise_entries(values_in, axis_num):
     values_in = values_in.astype(jnp.float32)
     centred = values_in - jnp.mean(values_in, axis=axis_num, keepdims=True)
@@ -38,17 +41,38 @@
     return centred * lax.rsqrt(spread + 1e-05)
 
 
-def row_edges(pair_row, entry, edges_ref, r):
-    count, _, _, share, lanes = edges_ref.shape
+def edges_in_turn(new_row, entry_ref, edges_ref, gate_ref):
+    count, _, strands, share, lanes = edges_ref.shape
     width = count * share
-    normed = lanes_norm(pair_row).astype(jnp.bfloat16)
-    mapped = lax.dot_general(
-        entry, normed, (((1,), (1,)), ((), ())), preferred_element_type=jnp.float32
-    )
-    for side in range(2):
-        base = 2 * side * width
-        edge = jax.nn.sigmoid(mapped[base : base + width]) * mapped[base + width : base + 2 * width]
-        edges_ref[:, side, r] = edge.reshape(count, share, lanes).astype(jnp.bfloat16)
+    mapped, gates = {}, {}
+    for n in range(strands // 2 + 1):
+        if n < strands // 2:
+            normed = [lanes_norm(new_row(2 * n + k)).astype(jnp.bfloat16) for k in range(2)]
+            normed = jnp.concatenate(normed)
+            mapped[n] = [
+                lax.dot_general(
+                    entry_ref[2 * side * width : 2 * (side + 1) * width],
+                    normed,
+                    (((1,), (1,)), ((), ())),
+                    preferred_element_type=jnp.float32,
+                )
+                for side in range(2)
+            ]
+            gates[n] = lax.dot_general(
+                normed,
+                entry_ref[4 * width :],
+                (((1,), (1,)), ((), ())),
+                preferred_element_type=jnp.float32,
+            )
+        if n:
+            gate = jax.nn.sigmoid(gates.pop(n - 1))
+            for k in range(2):
+                gate_ref[2 * n - 2 + k] = gate[k * lanes : (k + 1) * lanes]
+            for side, both in enumerate(mapped.pop(n - 1)):
+                edge = jax.nn.sigmoid(both[:width]) * both[width:]
+                for k in range(2):
+                    part = edge[:, k * lanes : (k + 1) * lanes].reshape(count, share, lanes)
+                    edges_ref[:, side, 2 * n - 2 + k] = part.astype(jnp.bfloat16)
 
 
 def product_kernel(incoming, arrived_ref, product_ref, left_ref, right_ref):
@@ -78,64 +102,105 @@
     )(arrived)
 
 
-def exit_rows(gathered_ref, exit_ref, pair_ref, gate_ref, out_ref, spread_ref, each):
+def exit_rows(which, gathered_ref, exit_ref, pair_ref, gate_ref, out_ref, spread_ref):
     count, share, strands, lanes = gathered_ref.shape
     width = count * share
     spread_ref[...] = gathered_ref[...].astype(jnp.float32).reshape(width * strands, lanes)
-    for r in range(strands):
+
+    def update(r):
         edges = spread_ref[pl.ds(r, width, stride=strands), :]
         centred = edges - jnp.mean(edges, axis=0, keepdims=True)
         spread = jnp.mean(centred * centred, axis=0, keepdims=True)
         normed = (centred * lax.rsqrt(spread + 1e-05)).astype(jnp.bfloat16)
-        update = lax.dot_general(
-            normed, exit_ref[...], (((0,), (0,)), ((), ())), preferred_element_type=jnp.float32
-        )
-        new = (pair_ref[r].astype(jnp.float32) + gate_ref[r] * update).astype(jnp.bfloat16)
+        return lax.dot_general(
+            normed, exit_ref[which], (((0,), (0,)), ((), ())), preferred_element_type=jnp.float32
+        )
+
+    updates = {0: update(0)}
+
+    def new_row(r):
+        if r + 1 < strands:
+            updates[r + 1] = update(r + 1)
+        new = pair_ref[r].astype(jnp.float32) + gate_ref[r] * updates.pop(r)
+        new = new.astype(jnp.bfloat16)
         out_ref[r] = new
-        each(r, new)
-
-
-def exit_entry_kernel(gathered_ref, exit_ref, pair_ref, gate_ref, entry_ref, out_ref, edges_ref, spread_ref):
-    entry = entry_ref[...]
-
-    def each(r, new):
-        row_edges(new.astype(jnp.float32), entry, edges_ref, r)
-
-    exit_rows(gathered_ref, exit_ref, pair_ref, gate_ref, out_ref, spread_ref, each)
-
-
-def exit_kernel(gathered_ref, exit_ref, pair_ref, gate_ref, out_ref, spread_ref):
-    exit_rows(gathered_ref, exit_ref, pair_ref, gate_ref, out_ref, spread_ref, lambda r, new: None)
-
-
-def exit_call(gathered, weight, pair_prev, gate, entry=None):
+        return new.astype(jnp.float32)
+
+    return new_row
+
+
+def exit_entry_kernel(
+    gathered_ref,
+    exit_ref,
+    pair_ref,
+    gate_ref,
+    entry_ref,
+    arrived_ref,
+    out_ref,
+    edges_ref,
+    next_gate_ref,
+    mixed_ref,
+    spread_ref,
+    sems,
+):
+    copies = [
+        pltpu.make_async_copy(
+            arrived_ref.at[:, 2 + k], mixed_ref.at[:, :, :, pl.ds(k * 128, 128)], sems.at[k]
+        )
+        for k in range(arrived_ref.shape[1] - 2)
+    ]
+    for copy in copies:
+        copy.start()
+    new_row = exit_rows(0, gathered_ref, exit_ref, pair_ref, gate_ref, out_ref, spread_ref)
+    edges_in_turn(new_row, entry_ref.at[1], edges_ref, next_gate_ref)
+    for copy in copies:
+        copy.wait()
+
+
+def exit_entry_call(gathered, weight, pair_prev, gate, entry, arrived):
     count, share, strands, lanes = gathered.shape
-    pair = jax.ShapeDtypeStruct(pair_prev.shape, jnp.bfloat16)
-    scratch = [pltpu.VMEM((count * share * strands, lanes), jnp.float32)]
-    if entry is None:
-        return pl.pallas_call(
-            exit_kernel,
-            out_shape=pair,
-            in_specs=whole(4),
-            out_specs=pl.BlockSpec(memory_space=pltpu.VMEM),
-            scratch_shapes=scratch,
-            compiler_params=params(),
-            name="triangle_exit",
-        )(gathered, weight, pair_prev, gate)
-    edges = jax.ShapeDtypeStruct((count, 2, strands, share, lanes), jnp.bfloat16)
+    parts = arrived.shape[1] - 2
+    anywhere = pl.BlockSpec(memory_space=pl.ANY)
     return pl.pallas_call(
         exit_entry_kernel,
-        out_shape=(pair, edges),
-        in_specs=whole(5),
-        out_specs=tuple(whole(2)),
-        scratch_shapes=scratch,
+        out_shape=(
+            jax.ShapeDtypeStruct(pair_prev.shape, jnp.bfloat16),
+            jax.ShapeDtypeStruct((count, 2, strands, share, lanes), jnp.bfloat16),
+            jax.ShapeDtypeStruct(pair_prev.shape, jnp.float32),
+            jax.ShapeDtypeStruct((count, strands, share, parts * 128), jnp.bfloat16),
+        ),
+        in_specs=whole(5) + [anywhere],
+        out_specs=tuple(whole(3)) + (pl.BlockSpec(memory_space=pltpu.HBM),),
+        scratch_shapes=[
+            pltpu.VMEM((count * share * strands, lanes), jnp.float32),
+            pltpu.SemaphoreType.DMA((parts,)),
+        ],
         compiler_params=params(),
         name="triangle_exit_entry",
-    )(gathered, weight, pair_prev, gate, entry)
+    )(gathered, weight, pair_prev, gate, entry, arrived)
+
+
+def exit_kernel(gathered_ref, exit_ref, pair_ref, gate_ref, out_ref, spread_ref):
+    new_row = exit_rows(1, gathered_ref, exit_ref, pair_ref, gate_ref, out_ref, spread_ref)
+    for r in range(pair_ref.shape[0]):
+        new_row(r)
+
+
+def exit_call(gathered, weight, pair_prev, gate):
+    count, share, strands, lanes = gathered.shape
+    return pl.pallas_call(
+        exit_kernel,
+        out_shape=jax.ShapeDtypeStruct(pair_prev.shape, jnp.bfloat16),
+        in_specs=whole(4),
+        out_specs=pl.BlockSpec(memory_space=pltpu.VMEM),
+        scratch_shapes=[pltpu.VMEM((count * share * strands, lanes), jnp.float32)],
+        compiler_params=params(),
+        name="triangle_exit",
+    )(gathered, weight, pair_prev, gate)
 
 
 def opm_kernel(
-    core_ref, flanks_ref, other_ref, coupling_ref, final_ref, entry_ref, pair_ref, edges_ref, outer_ref
+    core_ref, flanks_ref, other_ref, mixed_ref, coupling_ref, final_ref, entry_ref, pair_ref, edges_ref, gate_ref, outer_ref
 ):
     chains = flanks_ref.shape[0]
     strands, total_res, width = coupling_ref.shape
@@ -146,6 +211,8 @@
     span = 8 * depth
     blocks = flat // 128
     left = flanks_ref[:, :flat]
+    for k in range(edges_ref.shape[1] - 2):
+        edges_ref[:, 2 + k] = mixed_ref[:, :, :, k * 128 : (k + 1) * 128]
     for which in range(2):
         for pair in range(half // 16):
             parts = []
@@ -161,26 +228,29 @@
                 at = ig * total_res + which * half + pair * 16
                 for e in range(depth):
                     outer_ref[at : at + 16, e * 128 : (e + 1) * 128] = both[e, :, ig * 128 : (ig + 1) * 128]
-    core = core_ref[0]
-    for ig in range(blocks):
-        update = jnp.dot(
-            outer_ref[ig * total_res : (ig + 1) * total_res, :],
-            final_ref[...],
-            preferred_element_type=jnp.float32,
-        )
-        for which in range(2):
-            at = pl.multiple_of(half * (core if which == 0 else 1 - core), half)
-            for i4 in range(groups):
-                i = ig * groups + i4
-                piece = update[which * half : (which + 1) * half, i4 * width : (i4 + 1) * width]
-                prev = coupling_ref[i, pl.ds(at, half), :].astype(jnp.float32)
-                pair_ref[i, pl.ds(at, half), :] = (prev + piece).astype(jnp.bfloat16)
-    entry = entry_ref[...]
-    for r in range(strands):
-        row_edges(pair_ref[r].astype(jnp.float32), entry, edges_ref, r)
-
-
-def opm_call(core, flanks, other, coupling, final, entry, count):
+    first = core_ref[0] == 0
+
+    product = jnp.dot(outer_ref[...], final_ref[...], preferred_element_type=jnp.float32)
+
+    def new_row(r):
+        ig, i4 = divmod(r, groups)
+        mine, theirs = (
+            product[
+                ig * total_res + which * half : ig * total_res + (which + 1) * half,
+                i4 * width : (i4 + 1) * width,
+            ]
+            for which in range(2)
+        )
+        piece = jnp.concatenate([jnp.where(first, mine, theirs), jnp.where(first, theirs, mine)])
+        new = (coupling_ref[r].astype(jnp.float32) + piece).astype(jnp.bfloat16)
+        pair_ref[r] = new
+        return new.astype(jnp.float32)
+
+    edges_in_turn(new_row, entry_ref.at[0], edges_ref, gate_ref)
+
+
+def opm_call(core, flanks, other, mixed, coupling, final, entry):
+    count, _, _, depth = mixed.shape
     strands, total_res, width = coupling.shape
     share = width // count
     rows = strands * 128 // (128 * final.shape[1] // width) * total_res
@@ -188,47 +258,54 @@
         opm_kernel,
         out_shape=(
             jax.ShapeDtypeStruct(coupling.shape, jnp.bfloat16),
-            jax.ShapeDtypeStruct((count, 2, strands, share, total_res), jnp.bfloat16),
+            jax.ShapeDtypeStruct(
+                (count, 2 + depth // 128, strands, share, total_res), jnp.bfloat16
+            ),
+            jax.ShapeDtypeStruct(coupling.shape, jnp.float32),
         ),
-        in_specs=[pl.BlockSpec(memory_space=pltpu.SMEM)] + whole(5),
-        out_specs=tuple(whole(2)),
+        in_specs=[pl.BlockSpec(memory_space=pltpu.SMEM)] + whole(6),
+        out_specs=tuple(whole(3)),
         scratch_shapes=[pltpu.VMEM((rows, final.shape[0]), jnp.bfloat16)],
         compiler_params=params(24),
         name="outer_product_entry",
-    )(core, flanks, other, coupling, final, entry)
-
-
-def gate_kernel(pair_ref, weight_ref, gate_ref):
-    for r in range(pair_ref.shape[0]):
-        normed = lanes_norm(pair_ref[r].astype(jnp.float32)).astype(jnp.bfloat16)
-        gate_ref[r] = jax.nn.sigmoid(
-            jnp.dot(normed, weight_ref[...], preferred_element_type=jnp.float32)
-        )
-
-
-def gate_call(pair, weight):
-    return pl.pallas_call(
-        gate_kernel,
-        out_shape=jax.ShapeDtypeStruct(pair.shape, jnp.float32),
-        in_specs=whole(2),
+    )(core, flanks, other, mixed, coupling, final, entry)
+
+
+def spread_kernel(final_ref, block_ref, wide_ref):
+    width = final_ref.shape[1]
+    depth = block_ref.shape[0] // 128
+    groups = 128 // depth
+    wide_ref[...] = final_ref[...].astype(jnp.float32)
+    block_ref[...] = jnp.zeros(block_ref.shape, block_ref.dtype)
+    for e in range(depth):
+        piece = wide_ref[pl.ds(e, depth, stride=depth), :].astype(jnp.bfloat16)
+        for g in range(groups):
+            at = e * 128 + g * depth
+            block_ref[at : at + depth, g * width : (g + 1) * width] = piece
+
+
+def spread_call(final):
+    depth = math.isqrt(final.shape[0])
+    width = final.shape[1]
+    return pl.pallas_call(
+        spread_kernel,
+        out_shape=jax.ShapeDtypeStruct((depth * 128, 128 // depth * width), jnp.bfloat16),
+        in_specs=whole(1),
         out_specs=pl.BlockSpec(memory_space=pltpu.VMEM),
+        scratch_shapes=[pltpu.VMEM(final.shape, jnp.float32)],
         compiler_params=params(),
-        name="pair_gate",
-    )(pair, weight)
+        name="spread_weight",
+    )(final)
 
 
 def prepare_kernel(
-    final_ref,
     entry_ref,
     average_ref,
     project_ref,
-    block_ref,
     sides_ref,
-    gates_ref,
     left_ref,
     right_ref,
     turned_ref,
-    wide_ref,
 ):
     turned_ref[...] = project_ref[...].astype(jnp.float32).T.astype(jnp.bfloat16)
     channels = average_ref.shape[1] // 2
@@ -247,78 +324,102 @@
                 preferred_element_type=jnp.float32,
             )
             ref[g] = placed.astype(jnp.bfloat16)
-    width = final_ref.shape[1]
-    depth = block_ref.shape[0] // 128
-    groups = 128 // depth
-    wide_ref[...] = final_ref[...].astype(jnp.float32)
-    block_ref[...] = jnp.zeros(block_ref.shape, block_ref.dtype)
-    for e in range(depth):
-        piece = wide_ref[pl.ds(e, depth, stride=depth), :].astype(jnp.bfloat16)
-        for g in range(groups):
-            at = e * 128 + g * depth
-            block_ref[at : at + depth, g * width : (g + 1) * width] = piece
     for d in range(2):
-        sides = entry_ref[d, :, : 4 * width].astype(jnp.float32)
-        sides_ref[d] = sides.T.astype(jnp.bfloat16)
-        gates_ref[d] = entry_ref[d, :, 4 * width :]
-
-
-def prepare_call(final, entries, average, project):
-    depth = math.isqrt(final.shape[0])
-    width = final.shape[1]
-    groups = 128 // depth
+        sides_ref[d] = entry_ref[d].astype(jnp.float32).T.astype(jnp.bfloat16)
+
+
+def prepare_call(entries, average, project):
+    depth = average.shape[1] // 2
+    width = entries.shape[1]
     return pl.pallas_call(
         prepare_kernel,
         out_shape=(
-            jax.ShapeDtypeStruct((depth * 128, groups * width), jnp.bfloat16),
-            jax.ShapeDtypeStruct((2, 4 * width, width), jnp.bfloat16),
-            jax.ShapeDtypeStruct((2, width, width), jnp.bfloat16),
-            jax.ShapeDtypeStruct((groups, average.shape[0], 128), jnp.bfloat16),
+            jax.ShapeDtypeStruct((2, 5 * width, width), jnp.bfloat16),
+            jax.ShapeDtypeStruct((128 // depth, average.shape[0], 128), jnp.bfloat16),
             jax.ShapeDtypeStruct((8, average.shape[0], 8 * depth), jnp.bfloat16),
             jax.ShapeDtypeStruct(project.shape[::-1], jnp.bfloat16),
         ),
-        in_specs=whole(4),
-        out_specs=tuple(whole(6)),
-        scratch_shapes=[pltpu.VMEM(final.shape, jnp.float32)],
-        compiler_params=params(24),
+        in_specs=whole(3),
+        out_specs=tuple(whole(4)),
+        compiler_params=params(),
         name="prepare_weights",
-    )(final, entries, average, project)
-
-
-def pack_kernel(msa_ref, pair_ref, weight_ref, out_ref):
-    count, chains, parts = out_ref.shape[:3]
-    for d in range(count):
-        for k in range(parts - 1):
-            out_ref[d, :, k] = msa_ref[d * chains : (d + 1) * chains, :, k * 128 : (k + 1) * 128]
-    for r in range(pair_ref.shape[0]):
-        normed = lanes_norm(pair_ref[r].astype(jnp.float32)).astype(jnp.bfloat16)
+    )(entries, average, project)
+
+
+def pack_kernel(
+    msa_ref, pair_ref, weight_ref, out_ref, own_ref, rows_ref, logit_ref, term_ref, in_sems, out_sems
+):
+    count, parts = out_ref.shape[:2]
+    loads = [
+        pltpu.make_async_copy(pair_ref, rows_ref, in_sems.at[0]),
+        pltpu.make_async_copy(weight_ref, logit_ref, in_sems.at[1]),
+    ]
+    own = pltpu.make_async_copy(msa_ref, own_ref, in_sems.at[2])
+    stores = [
+        pltpu.make_async_copy(
+            own_ref.at[:, :, :, pl.ds(k * 128, 128)], out_ref.at[:, k], out_sems.at[count + k]
+        )
+        for k in range(parts - 1)
+    ]
+    for copy in loads + [own]:
+        copy.start()
+    for copy in loads:
+        copy.wait()
+    for r in range(rows_ref.shape[0]):
+        if r == 1:
+            own.wait()
+            for copy in stores:
+                copy.start()
+        normed = lanes_norm(rows_ref[r].astype(jnp.float32)).astype(jnp.bfloat16)
         bias = lax.dot_general(
-            weight_ref[...], normed, (((1,), (1,)), ((), ())), preferred_element_type=jnp.float32
+            logit_ref[...], normed, (((1,), (1,)), ((), ())), preferred_element_type=jnp.float32
         )
         upper = bias.astype(jnp.bfloat16)
-        lower = (bias - upper.astype(jnp.float32)).astype(jnp.bfloat16)
-        for d in range(count):
-            out_ref[d, r, parts - 1] = lower if d % 2 else upper
+        term_ref[0, r] = upper
+        term_ref[1, r] = (bias - upper.astype(jnp.float32)).astype(jnp.bfloat16)
+    terms = [
+        pltpu.make_async_copy(term_ref.at[d % 2], out_ref.at[d, parts - 1], out_sems.at[d])
+        for d in range(count)
+    ]
+    for copy in terms:
+        copy.start()
+    for copy in stores + terms:
+        copy.wait()
 
 
 def pack_call(msa, pair, weight, count):
     chains, strands, depth = msa.shape
+    parts, heads = depth // 128, weight.shape[1]
+    anywhere = pl.BlockSpec(memory_space=pltpu.HBM)
     return pl.pallas_call(
         pack_kernel,
         out_shape=jax.ShapeDtypeStruct(
-            (count, chains // count, depth // 128 + 1, strands, 128), jnp.bfloat16
+            (count, parts + 1, chains // count, strands, 128), jnp.bfloat16
         ),
-        in_specs=whole(3),
-        out_specs=pl.BlockSpec(memory_space=pltpu.VMEM),
+        in_specs=[anywhere] * 3,
+        out_specs=anywhere,
+        scratch_shapes=[
+            pltpu.VMEM((count, chains // count, strands, depth), jnp.bfloat16),
+            pltpu.VMEM(pair.shape, jnp.bfloat16),
+            pltpu.VMEM((heads, pair.shape[2]), jnp.bfloat16),
+            pltpu.VMEM((2, strands, heads, pair.shape[1]), jnp.bfloat16),
+            pltpu.SemaphoreType.DMA((3,)),
+            pltpu.SemaphoreType.DMA((count + parts,)),
+        ],
         compiler_params=params(),
         name="pack_rows",
-    )(msa, pair, weight.T)
+    )(
+        *(
+            pltpu.with_memory_space_constraint(operand, pltpu.HBM)
+            for operand in (msa.reshape(count, chains // count, strands, depth), pair, weight.T)
+        )
+    )
 
 
 def arrived_rows(arrived_ref, s):
-    count, _, parts, strands, lanes = arrived_ref.shape
+    count, parts, _, strands, lanes = arrived_ref.shape
     pieces = [
-        arrived_ref[:, s, k].astype(jnp.float32).reshape(count * strands, lanes)
+        arrived_ref[:, k, s].astype(jnp.float32).reshape(count * strands, lanes)
         for k in range(parts - 1)
     ]
     return jnp.concatenate(pieces, axis=-1)
@@ -326,18 +427,24 @@
 
 def project_kernel(arrived_ref, weight_ref, query_ref, key_ref, value_ref, gate_ref):
     inner = query_ref.shape[1]
-    for s in range(query_ref.shape[0]):
-        normed = lanes_norm(arrived_rows(arrived_ref, s)).astype(jnp.bfloat16)
+    total_res = query_ref.shape[2]
+    for s in range(0, query_ref.shape[0], 2):
+        rows = jnp.concatenate([arrived_rows(arrived_ref, s + k) for k in range(2)])
         mapped = lax.dot_general(
-            weight_ref[...], normed, (((1,), (1,)), ((), ())), preferred_element_type=jnp.float32
-        )
-        for k, ref in enumerate((query_ref, key_ref, value_ref)):
-            ref[s] = mapped[k * inner : (k + 1) * inner].astype(jnp.bfloat16)
-        gate_ref[s] = jax.nn.sigmoid(mapped[3 * inner :])
+            weight_ref[...],
+            lanes_norm(rows).astype(jnp.bfloat16),
+            (((1,), (1,)), ((), ())),
+            preferred_element_type=jnp.float32,
+        )
+        for k in range(2):
+            part = mapped[:, k * total_res : (k + 1) * total_res]
+            for block, ref in enumerate((query_ref, key_ref, value_ref)):
+                ref[s + k] = part[block * inner : (block + 1) * inner].astype(jnp.bfloat16)
+            gate_ref[s + k] = jax.nn.sigmoid(part[3 * inner :])
 
 
 def project_call(arrived, weight):
-    count, chains, _, strands, _ = arrived.shape
+    count, _, chains, strands, _ = arrived.shape
     turned = (chains, weight.shape[0] // 4, count * strands)
     half = jax.ShapeDtypeStruct(turned, jnp.bfloat16)
     return pl.pallas_call(
@@ -370,32 +477,29 @@
     count, chains, strands, depth = mixed_ref.shape
     inner, total_res = query_ref.shape[1:]
     heads = inner // width
-    mine = arrived_ref[:, :, arrived_ref.shape[2] - 1].astype(jnp.float32)
+    mine = arrived_ref[:, arrived_ref.shape[1] - 1].astype(jnp.float32)
     bias = mine + other_ref[...].astype(jnp.float32)
     bias_ref[...] = bias.reshape(total_res * heads, total_res)
     for h in range(heads):
-        turned_ref[h] = bias_ref[pl.ds(h, total_res, stride=heads), :].T
-    scale = width ** (-0.5)
-    for s in range(chains):
-        attended = []
-        for h in range(heads):
-            at = slice(h * width, (h + 1) * width)
-            scores = lax.dot_general(
-                key_ref[s, at],
-                query_ref[s, at],
-                (((0,), (0,)), ((), ())),
-                preferred_element_type=jnp.float32,
-            )
-            scores = scores * scale + turned_ref[h]
-            weights = jnp.exp(scores - jnp.max(scores, axis=0, keepdims=True))
-            weights = weights * (1.0 / jnp.sum(weights, axis=0, keepdims=True))
-            attended.append(
-                jnp.dot(
-                    value_ref[s, at],
-                    weights.astype(jnp.bfloat16),
-                    preferred_element_type=jnp.float32,
-                )
-            )
+        turned_ref[h] = bias_ref[pl.ds(h, total_res, stride=heads), :].T * LOG2E
+    scale = width ** (-0.5) * LOG2E
+
+    def score(s, h):
+        at = slice(h * width, (h + 1) * width)
+        return lax.dot_general(
+            key_ref[s, at],
+            query_ref[s, at],
+            (((0,), (0,)), ((), ())),
+            preferred_element_type=jnp.float32,
+        )
+
+    def weigh(scores, h):
+        scores = scores * scale + turned_ref[h]
+        weights = jnp.exp2(scores - jnp.max(scores, axis=0, keepdims=True))
+        total = jnp.sum(weights, axis=0, keepdims=True)
+        return (weights * (1.0 / total)).astype(jnp.bfloat16)
+
+    def finish(s, attended):
         attended = jnp.concatenate(attended).astype(jnp.bfloat16).astype(jnp.float32)
         gated = (attended * gate_ref[s]).astype(jnp.bfloat16)
         increment = lax.dot_general(
@@ -407,6 +511,28 @@
         for k in range(depth // 128):
             scaled_ref[k, pl.ds(s, total_res, stride=chains), :] = normed[:, k * 128 : (k + 1) * 128]
         mixed_ref[:, s] = mixed.reshape(count, strands, depth).astype(jnp.bfloat16)
+
+    steps = [(s, h) for s in range(chains) for h in range(heads)]
+    ahead = 2
+    scores = {n: score(*steps[n]) for n in range(ahead)}
+    weighed, attended = {}, []
+    for n in range(len(steps) + 1):
+        if n + ahead < len(steps):
+            scores[n + ahead] = score(*steps[n + ahead])
+        if n < len(steps):
+            weighed[n] = weigh(scores.pop(n), steps[n][1])
+        if n:
+            s, h = steps[n - 1]
+            attended.append(
+                jnp.dot(
+                    value_ref[s, h * width : (h + 1) * width],
+                    weighed.pop(n - 1),
+                    preferred_element_type=jnp.float32,
+                )
+            )
+            if h + 1 == heads:
+                finish(s, attended)
+                attended = []
 
     scaled = jnp.concatenate([scaled_ref[k] for k in range(depth // 128)], axis=-1)
     scaled = scaled.reshape(total_res, chains, depth)
@@ -434,7 +560,7 @@
 
 
 def attend_call(arrived, other, projected, width, final, left, right):
-    count, chains, parts, strands, _ = arrived.shape
+    count, parts, chains, strands, _ = arrived.shape
     inner, total_res = projected[0].shape[1:]
     depth, heads = (parts - 1) * 128, inner // width
     lanes = strands // left.shape[0] * left.shape[2] + total_res // 2 // right.shape[0] * right.shape[2]
@@ -456,20 +582,20 @@
     )(arrived, other, *projected, final, left, right)
 
 
-def pair_track(core, flanks, other, coupling, prepared, exits):
-    final, sides, gates = prepared[:3]
-    count = lax.axis_size("res")
-    pair, edges = opm_call(core, flanks, other, coupling, final, sides[0], count)
+def pair_track(core, flanks, other, mixed, coupling, final, prepared, exits):
+    sides = prepared[0]
+    pair, edges, gate = opm_call(core, flanks, other, mixed, coupling, final, sides)
     for d in range(2):
         arrived = exchange(edges)
-        gate = gate_call(pair, gates[d])
         product = product_call(arrived, d == 1)
         gathered = exchange(product)
         if d == 0:
-            pair, edges = exit_call(gathered, exits[0], pair, gate, sides[1])
+            pair, edges, gate, returned = exit_entry_call(
+                gathered, exits, pair, gate, sides, arrived
+            )
         else:
-            pair = exit_call(gathered, exits[1], pair, gate)
-    return pair
+            pair = exit_call(gathered, exits, pair, gate)
+    return returned.reshape((-1,) + mixed.shape[2:]), pair
 
 
 def triangle(pair_prev, weight_in, weight_out, contraction):
@@ -531,27 +657,28 @@
         and tensor_depth == 32
     )
     if fits:
-        prepared = prepare_call(
-            tensor_average_final,
-            trilateral_entry_matrix,
-            tensor_average_matrix,
-            query_key_matrix,
-        )
+        prepared = prepare_call(trilateral_entry_matrix, tensor_average_matrix, query_key_matrix)
         packed = pack_call(alignment_embedding, coupling_embedding, coupling_logit_matrix, count)
         arrived = exchange(packed)
-        other = across(arrived[:, :, -1], 1)
-        projected = project_call(arrived, prepared[5])
+        other = across(arrived[:, -1], 1)
+        projected = project_call(arrived, prepared[3])
         mixed, flanks = attend_call(
-            arrived, other, projected, width, focus_final_matrix, *prepared[3:5]
+            arrived, other, projected, width, focus_final_matrix, *prepared[1:3]
         )
         flanks = exchange(flanks)
         flanks = flanks.reshape(chain_tally, -1)
         other = across(flanks, 1)
-        mixed_out = exchange(mixed).reshape(chain_tally, local_strands, depth)
-        refreshed = pair_track(
-            core.reshape(1), flanks, other, coupling_embedding, prepared, trilateral_exit_matrix
-        )
-        return (mixed_out, refreshed)
+        final = spread_call(tensor_average_final)
+        return pair_track(
+            core.reshape(1),
+            flanks,
+            other,
+            mixed,
+            coupling_embedding,
+            final,
+            prepared,
+            trilateral_exit_matrix,
+        )
 
     rows = exchange(alignment_embedding).reshape(count, per_device, local_strands, depth)
     rows = rows.transpose(1, 0, 2, 3).reshape(per_device, total_res, depth)

time: 160 us -> 146 us (0.912)
  blocking collectives: 81.8 us -> 121 us
  waiting for transfers between devices: 34.1 us -> 0.01 us
  starting transfers between devices: 13.6 us -> 1.1 us
  Pallas kernels: 22.4 us -> 15.3 us
    all_to_all x4 -> x6, blocking collectives: 81.8 us -> 121 us  [exchange(): lax.all_to_all(blocks, 'res', split_axis=0, concat_axis=0, tiled=True)]
    all_to_all x3 -> x0, waiting for transfers between devices: 32.2 us -> none  [exchange(): lax.all_to_all(blocks, 'res', split_axis=0, concat_axis=0, tiled=True)]
    all_to_all x3 -> x0, starting transfers between devices: 12.5 us -> none  [exchange(): lax.all_to_all(blocks, 'res', split_axis=0, concat_axis=0, tiled=True)]
    pallas_call x1, Pallas kernels: 10.6 us -> 4.17 us  [attend_call(): pl.pallas_call(lambda *refs: attend_kernel(width, *refs), out_shape=(jax....]
    ppermute x2, waiting for transfers between devices: 1.87 us -> 0.01 us  [across(): return lax.ppermute(values, 'res', [(k, k ^ bit) for k in range(count)])]
    unnamed x26 -> x17, local copies, waits for them, and re-layouts: 5.8 us -> 7.03 us
    pallas_call x6 -> x5, Pallas kernels: 5.6 us -> 6.71 us  [the longest x1 2.43 us: pack_call(): pl.pallas_call(pack_kernel, out_shape=jax.ShapeDtypeStruct((count, parts...]
  transfers between devices with their start and end apart: 5 -> 2, of which waited for: 4 -> 0; matrix products, arithmetic and copies ran while one was open for 0% -> 1% of each run, Pallas kernels for 3% -> 1%
where the time goes in v3:
time: 146 us; the launch traced here: 145 us
  blocking collectives  121 us (83%)
  Pallas kernels  15.3 us (10%)
  local copies, waits for them, and re-layouts  7.05 us (5%)
    all_to_all x6, blocking collectives, exchange(): lax.all_to_all(blocks, 'res', split_axis=0, concat_axis=0, tiled=True)  121 us
    unnamed x17, local copies, waits for them, and re-layouts  7.03 us
    pallas_call x1, Pallas kernels, attend_call(): pl.pallas_call(lambda *refs: attend_kernel(width, *refs), out_shape=(jax....  4.17 us
  transfers between devices with their start and end apart: 2, of which 0 were waited for; matrix products, arithmetic and copies ran while one was open for 1% of the time, Pallas kernels for 1%

profile of v3, /device:TPU:0, one launch (start us, length us, event | category | flops | bytes accessed | tf_op | source)
XLA Modules:
  0.0 145.3 jit_solution(12371369656911495624)
XLA Ops:
  0.6 0.0 copy-start.7
  0.6 2.4 %pack_rows.1 = bf16[16,3,8,8,128]{4,3,2,1,0:T(8,128)(2,1)S(1)} custom-call(bf16[16,8,8,256]{3,2,1,0:T(8,128)(2,1)} %bitcast.11, bf16[8,128,128]{2,1,0:T(8,128)(2,1)} %coupling_ref.1, bf16[8,128]{1,0:T(8,128)(2,1)} %bitcast.12), custom_call_target="tpu_custom_call" | custom-call | tf_op jit(solution)/shard_map/pack_rows/pallas_call | solution.py:394
  3.1 27.3 %all_to_all.30.arrived_ref.refs_0_ = bf16[16,3,8,8,128]{4,3,2,1,0:T(8,128)(2,1)S(1)} all-to-all(bf16[16,3,8,8,128]{4,3,2,1,0:T(8,128)(2,1)S(1)} %pack_rows.1), channel_id=1, replica_groups=mesh['grp'=2,'res'=16] {'res'}, dimensions={0} | all-to-all | bytes 1572864 | tf_op jit(solution)/shard_map/all_to_all | solution.py:22
  30.4 1.0 collective-permute-start
  31.4 0.9 copy.16.average_ref
  32.3 0.0 copy-start.3
  32.3 1.0 copy-done.3
  33.3 0.0 copy-start.4
  33.4 1.0 copy-done.4
  34.3 0.0 copy-start.5
  34.3 0.5 prepare_weights.1
  34.8 1.0 project_rows.1
  35.8 0.0 collective-permute-done.refs_1_
  35.8 0.0 copy-done.7
  35.8 0.0 copy-start.2
  35.8 4.2 %attend_rows.1 = (bf16[16,8,8,256]{3,2,1,0:T(8,128)(2,1)S(1)}, bf16[16,8,2304]{2,1,0:T(8,128)(2,1)S(1)}) custom-call(bf16[16,3,8,8,128]{4,3,2,1,0:T(8,128)(2,1)S(1)} %all_to_all.30.arrived_ref.refs_0_, bf16[16,8,8,128]{3,2,1,0:T(8,128)(2,1)S(1)} %collective-permute-done.refs_1_, bf16[8,256,128]{2,1,0:T(8,128)(2,1)S(1)} %get-tuple-element.20.refs_2_, ...), custom_call_target="tpu_custom_call" | custom-call | tf_op jit(solution)/shard_map/attend_rows/pallas_call | solution.py:567
  40.0 20.4 %all_to_all.31 = bf16[16,8,2304]{2,1,0:T(8,128)(2,1)S(1)} all-to-all(bf16[16,8,2304]{2,1,0:T(8,128)(2,1)S(1)} %get-tuple-element.26), channel_id=1, replica_groups=mesh['grp'=2,'res'=16] {'res'}, dimensions={0} | all-to-all | bytes 1179648 | tf_op jit(solution)/shard_map/all_to_all | solution.py:22
  60.4 0.1 collective-permute-start.1
  60.5 0.0 copy-done.5
  60.6 0.7 spread_weight.1.final_ref
  61.3 0.0 copy-start
  61.3 1.9 %copy-done = bf16[4096,512]{1,0:T(8,128)(2,1)} copy-done((bf16[4096,512]{1,0:T(8,128)(2,1)}, bf16[4096,512]{1,0:T(8,128)(2,1)S(1)}, u32[]{:S(2)}) %copy-start) | copy-done | bytes 4194328
  63.2 0.0 collective-permute-done.1.other_ref
  63.2 0.0 copy-done.2
  63.2 0.0 copy-start.1
  63.2 2.2 %copy-done.1 = bf16[4096,512]{1,0:T(8,128)(2,1)S(1)} copy-done((bf16[4096,512]{1,0:T(8,128)(2,1)S(1)}, bf16[4096,512]{1,0:T(8,128)(2,1)}, u32[]{:S(2)}) %copy-start.1) | copy-done | bytes 4194328
  65.4 0.0 copy-start.6
  65.4 2.8 %outer_product_entry.1 = (bf16[8,128,128]{2,1,0:T(8,128)(2,1)S(1)}, bf16[16,4,8,8,128]{4,3,2,1,0:T(8,128)(2,1)S(1)}, f32[8,128,128]{2,1,0:T(8,128)S(1)}) custom-call(s32[1]{0:T(128)} %bitcast.core_ref, bf16[128,2304]{1,0:T(8,128)(2,1)S(1)} %bitcast.10, bf16[128,2304]{1,0:T(8,128)(2,1)S(1)} %collective-permute-done.1.other_ref, ...), custom_call_target="tpu_custom_call" | custom-call | tf_op jit(solution)/shard_map/outer_product_entry/pallas_call | solution.py:257
  68.2 27.5 %all_to_all.32.refs_0_.arrived_ref = bf16[16,4,8,8,128]{4,3,2,1,0:T(8,128)(2,1)S(1)} all-to-all(bf16[16,4,8,8,128]{4,3,2,1,0:T(8,128)(2,1)S(1)} %get-tuple-element.29), channel_id=1, replica_groups=mesh['grp'=2,'res'=16] {'res'}, dimensions={0} | all-to-all | bytes 2097152 | tf_op jit(solution)/shard_map/all_to_all | solution.py:22
  95.7 0.3 edge_product.2
  96.0 14.8 %all_to_all.33.gathered_ref = bf16[16,8,8,128]{3,2,1,0:T(8,128)(2,1)S(1)} all-to-all(bf16[16,8,8,128]{3,2,1,0:T(8,128)(2,1)S(1)} %edge_product.2), channel_id=1, replica_groups=mesh['grp'=2,'res'=16] {'res'}, dimensions={0} | all-to-all | bytes 524288 | tf_op jit(solution)/shard_map/all_to_all | solution.py:22
  110.9 0.0 copy-done.6
  110.9 2.0 %triangle_exit_entry.1 = (bf16[8,128,128]{2,1,0:T(8,128)(2,1)S(1)}, bf16[16,2,8,8,128]{4,3,2,1,0:T(8,128)(2,1)S(1)}, f32[8,128,128]{2,1,0:T(8,128)S(1)}, bf16[16,8,8,256]{3,2,1,0:T(8,128)(2,1)}) custom-call(bf16[16,8,8,128]{3,2,1,0:T(8,128)(2,1)S(1)} %all_to_all.33.gathered_ref, bf16[2,128,128]{2,1,0:T(8,128)(2,1)S(1)} %copy-done.6, ...), custom_call_target="tpu_custom_call" | custom-call | tf_op jit(solution)/shard_map/triangle_exit_entry/pallas_call | solution.py:164
  112.8 17.0 %all_to_all.34.refs_0_ = bf16[16,2,8,8,128]{4,3,2,1,0:T(8,128)(2,1)S(1)} all-to-all(bf16[16,2,8,8,128]{4,3,2,1,0:T(8,128)(2,1)S(1)} %get-tuple-element.33), channel_id=1, replica_groups=mesh['grp'=2,'res'=16] {'res'}, dimensions={0} | all-to-all | bytes 1048576 | tf_op jit(solution)/shard_map/all_to_all | solution.py:22
  129.8 0.4 edge_product.3
  130.2 14.0 %all_to_all.35.gathered_ref = bf16[16,8,8,128]{3,2,1,0:T(8,128)(2,1)S(1)} all-to-all(bf16[16,8,8,128]{3,2,1,0:T(8,128)(2,1)S(1)} %edge_product.3), channel_id=1, replica_groups=mesh['grp'=2,'res'=16] {'res'}, dimensions={0} | all-to-all | bytes 524288 | tf_op jit(solution)/shard_map/all_to_all | solution.py:22
  144.1 1.1 triangle_exit.1
  (1 shorter events, 0.0 us)
Async XLA Ops:
  0.6 35.2 %copy-start.7 = (bf16[256,256]{1,0:T(8,128)(2,1)S(1)}, bf16[256,256]{1,0:T(8,128)(2,1)}, u32[]{:S(2)}) copy-start(bf16[256,256]{1,0:T(8,128)(2,1)} %refs_6_.1) | copy-start | bytes 393220
  30.4 5.4 %collective-permute-start = (bf16[16,8,8,128]{3,2,1,0:T(8,128)(2,1)S(1)}, bf16[16,8,8,128]{3,2,1,0:T(8,128)(2,1)S(1)}, u32[]{:S(2)}, u32[]{:S(2)}) collective-permute-start(bf16[16,8,8,128]{3,2,1,0:T(8,128)(2,1)S(1)} %slice_bitcast_fusion), channel_id=1, source_target_pairs={{0,1},{1,0},{2,3},{3,2},{4,5},{5,4},{6,7},{7,6},{8,9},{9,8},{10,11... | collective-permute-start | bytes 786440 | tf_op jit(solution)/shard_map/ppermute | solution.py:27
  32.3 1.0 copy-start.3
  33.3 1.0 copy-start.4
  34.3 26.2 %copy-start.5 = (bf16[1024,128]{1,0:T(8,128)(2,1)S(1)}, bf16[1024,128]{1,0:T(8,128)(2,1)}, u32[]{:S(2)}) copy-start(bf16[1024,128]{1,0:T(8,128)(2,1)} %final_ref.1) | copy-start | bytes 786436
  35.8 27.4 %copy-start.2 = (bf16[8,128,128]{2,1,0:T(8,128)(2,1)S(1)}, bf16[8,128,128]{2,1,0:T(8,128)(2,1)}, u32[]{:S(2)}) copy-start(bf16[8,128,128]{2,1,0:T(8,128)(2,1)} %coupling_ref.1) | copy-start | bytes 786436
  60.4 2.8 %collective-permute-start.1 = (bf16[128,2304]{1,0:T(8,128)(2,1)S(1)}, bf16[128,2304]{1,0:T(8,128)(2,1)S(1)}, u32[]{:S(2)}, u32[]{:S(2)}) collective-permute-start(bf16[128,2304]{1,0:T(8,128)(2,1)S(1)} %bitcast.9), channel_id=1, source_target_pairs={{0,1},{1,0},{2,3},{3,2},{4,5},{5,4},{6,7},{7,6},{8,9},{9,8},{10,11... | collective-permute-start | bytes 1769480 | tf_op jit(solution)/shard_map/ppermute | solution.py:27
  61.3 1.9 %copy-start = (bf16[4096,512]{1,0:T(8,128)(2,1)}, bf16[4096,512]{1,0:T(8,128)(2,1)S(1)}, u32[]{:S(2)}) copy-start(bf16[4096,512]{1,0:T(8,128)(2,1)S(1)} %spread_weight.1.final_ref) | copy-start | bytes 12582916
  63.2 2.2 %copy-start.1 = (bf16[4096,512]{1,0:T(8,128)(2,1)S(1)}, bf16[4096,512]{1,0:T(8,128)(2,1)}, u32[]{:S(2)}) copy-start(bf16[4096,512]{1,0:T(8,128)(2,1)} %copy-done) | copy-start | bytes 12582916
  65.4 45.4 %copy-start.6 = (bf16[2,128,128]{2,1,0:T(8,128)(2,1)S(1)}, bf16[2,128,128]{2,1,0:T(8,128)(2,1)}, u32[]{:S(2)}) copy-start(bf16[2,128,128]{2,1,0:T(8,128)(2,1)} %exit_ref.3) | copy-start | bytes 196612

commit v4 on v3

--- a/solution.py
+++ b/solution.py
@@ -44,35 +44,38 @@
 def edges_in_turn(new_row, entry_ref, edges_ref, gate_ref):
     count, _, strands, share, lanes = edges_ref.shape
     width = count * share
-    mapped, gates = {}, {}
-    for n in range(strands // 2 + 1):
-        if n < strands // 2:
-            normed = [lanes_norm(new_row(2 * n + k)).astype(jnp.bfloat16) for k in range(2)]
-            normed = jnp.concatenate(normed)
-            mapped[n] = [
+    normed, mapped, gates = {}, {}, {}
+    pairs = strands // 2
+    for n in range(pairs + 2):
+        if n < pairs:
+            rows = [lanes_norm(new_row(2 * n + k)).astype(jnp.bfloat16) for k in range(2)]
+            normed[n] = jnp.concatenate(rows)
+        if 0 < n <= pairs:
+            rows = normed.pop(n - 1)
+            mapped[n - 1] = [
                 lax.dot_general(
                     entry_ref[2 * side * width : 2 * (side + 1) * width],
-                    normed,
+                    rows,
                     (((1,), (1,)), ((), ())),
                     preferred_element_type=jnp.float32,
                 )
                 for side in range(2)
             ]
-            gates[n] = lax.dot_general(
-                normed,
+            gates[n - 1] = lax.dot_general(
+                rows,
                 entry_ref[4 * width :],
                 (((1,), (1,)), ((), ())),
                 preferred_element_type=jnp.float32,
             )
-        if n:
-            gate = jax.nn.sigmoid(gates.pop(n - 1))
+        if n > 1:
+            gate = jax.nn.sigmoid(gates.pop(n - 2))
             for k in range(2):
-                gate_ref[2 * n - 2 + k] = gate[k * lanes : (k + 1) * lanes]
-            for side, both in enumerate(mapped.pop(n - 1)):
+                gate_ref[2 * n - 4 + k] = gate[k * lanes : (k + 1) * lanes]
+            for side, both in enumerate(mapped.pop(n - 2)):
                 edge = jax.nn.sigmoid(both[:width]) * both[width:]
                 for k in range(2):
                     part = edge[:, k * lanes : (k + 1) * lanes].reshape(count, share, lanes)
-                    edges_ref[:, side, 2 * n - 2 + k] = part.astype(jnp.bfloat16)
+                    edges_ref[:, side, 2 * n - 4 + k] = part.astype(jnp.bfloat16)
 
 
 def product_kernel(incoming, arrived_ref, product_ref, left_ref, right_ref):
@@ -116,11 +119,12 @@
             normed, exit_ref[which], (((0,), (0,)), ((), ())), preferred_element_type=jnp.float32
         )
 
-    updates = {0: update(0)}
+    ahead = 2
+    updates = {r: update(r) for r in range(ahead)}
 
     def new_row(r):
-        if r + 1 < strands:
-            updates[r + 1] = update(r + 1)
+        if r + ahead < strands:
+            updates[r + ahead] = update(r + ahead)
         new = pair_ref[r].astype(jnp.float32) + gate_ref[r] * updates.pop(r)
         new = new.astype(jnp.bfloat16)
         out_ref[r] = new
@@ -199,48 +203,73 @@
     )(gathered, weight, pair_prev, gate)
 
 
+def half_product(flanks_ref, left, final_ref, outer_ref):
+    chains, flat = left.shape
+    depth = final_ref.shape[0] // 128
+    span, blocks = 8 * depth, flat // 128
+    half = (flanks_ref.shape[1] - flat) // depth
+    for pair in range(half // 16):
+        parts = []
+        for jg in (2 * pair, 2 * pair + 1):
+            part = lax.dot_general(
+                flanks_ref[:, flat + jg * span : flat + (jg + 1) * span],
+                left,
+                (((0,), (0,)), ((), ())),
+                preferred_element_type=jnp.float32,
+            ) * (1.0 / chains)
+            parts.append(part.reshape(depth, 8, flat))
+        both = jnp.concatenate(parts, axis=1).astype(jnp.bfloat16)
+        for ig in range(blocks):
+            at = ig * half + pair * 16
+            for e in range(depth):
+                outer_ref[at : at + 16, e * 128 : (e + 1) * 128] = both[e, :, ig * 128 : (ig + 1) * 128]
+    return jnp.dot(outer_ref[...], final_ref[...], preferred_element_type=jnp.float32)
+
+
+def own_kernel(flat, flanks_ref, final_ref, product_ref, outer_ref):
+    product_ref[...] = half_product(flanks_ref, flanks_ref[:, :flat], final_ref, outer_ref)
+
+
+def own_call(flanks, final, flat, half):
+    rows = flat // 128 * half
+    return pl.pallas_call(
+        lambda *refs: own_kernel(flat, *refs),
+        out_shape=jax.ShapeDtypeStruct((rows, final.shape[1]), jnp.float32),
+        in_specs=whole(2),
+        out_specs=pl.BlockSpec(memory_space=pltpu.VMEM),
+        scratch_shapes=[pltpu.VMEM((rows, final.shape[0]), jnp.bfloat16)],
+        compiler_params=params(24),
+        name="outer_product_own",
+    )(flanks, final)
+
+
 def opm_kernel(
-    core_ref, flanks_ref, other_ref, mixed_ref, coupling_ref, final_ref, entry_ref, pair_ref, edges_ref, gate_ref, outer_ref
+    flat,
+    core_ref,
+    flanks_ref,
+    other_ref,
+    own_ref,
+    mixed_ref,
+    coupling_ref,
+    final_ref,
+    entry_ref,
+    pair_ref,
+    edges_ref,
+    gate_ref,
+    outer_ref,
 ):
-    chains = flanks_ref.shape[0]
-    strands, total_res, width = coupling_ref.shape
-    depth = final_ref.shape[0] // 128
+    _, total_res, width = coupling_ref.shape
     groups = final_ref.shape[1] // width
     half = total_res // 2
-    flat = strands * depth
-    span = 8 * depth
-    blocks = flat // 128
-    left = flanks_ref[:, :flat]
     for k in range(edges_ref.shape[1] - 2):
         edges_ref[:, 2 + k] = mixed_ref[:, :, :, k * 128 : (k + 1) * 128]
-    for which in range(2):
-        for pair in range(half // 16):
-            parts = []
-            for jg in (2 * pair, 2 * pair + 1):
-                source = other_ref if which else flanks_ref
-                right = source[:, flat + jg * span : flat + (jg + 1) * span]
-                part = lax.dot_general(
-                    right, left, (((0,), (0,)), ((), ())), preferred_element_type=jnp.float32
-                ) * (1.0 / chains)
-                parts.append(part.reshape(depth, 8, flat))
-            both = jnp.concatenate(parts, axis=1).astype(jnp.bfloat16)
-            for ig in range(blocks):
-                at = ig * total_res + which * half + pair * 16
-                for e in range(depth):
-                    outer_ref[at : at + 16, e * 128 : (e + 1) * 128] = both[e, :, ig * 128 : (ig + 1) * 128]
     first = core_ref[0] == 0
-
-    product = jnp.dot(outer_ref[...], final_ref[...], preferred_element_type=jnp.float32)
+    product = half_product(other_ref, flanks_ref[:, :flat], final_ref, outer_ref)
 
     def new_row(r):
         ig, i4 = divmod(r, groups)
-        mine, theirs = (
-            product[
-                ig * total_res + which * half : ig * total_res + (which + 1) * half,
-                i4 * width : (i4 + 1) * width,
-            ]
-            for which in range(2)
-        )
+        rows, lanes = slice(ig * half, (ig + 1) * half), slice(i4 * width, (i4 + 1) * width)
+        mine, theirs = own_ref[rows, lanes], product[rows, lanes]
         piece = jnp.concatenate([jnp.where(first, mine, theirs), jnp.where(first, theirs, mine)])
         new = (coupling_ref[r].astype(jnp.float32) + piece).astype(jnp.bfloat16)
         pair_ref[r] = new
@@ -249,13 +278,12 @@
     edges_in_turn(new_row, entry_ref.at[0], edges_ref, gate_ref)
 
 
-def opm_call(core, flanks, other, mixed, coupling, final, entry):
+def opm_call(core, flanks, other, own, mixed, coupling, final, entry, flat):
     count, _, _, depth = mixed.shape
     strands, total_res, width = coupling.shape
     share = width // count
-    rows = strands * 128 // (128 * final.shape[1] // width) * total_res
-    return pl.pallas_call(
-        opm_kernel,
+    return pl.pallas_call(
+        lambda *refs: opm_kernel(flat, *refs),
         out_shape=(
             jax.ShapeDtypeStruct(coupling.shape, jnp.bfloat16),
             jax.ShapeDtypeStruct(
@@ -263,12 +291,12 @@
             ),
             jax.ShapeDtypeStruct(coupling.shape, jnp.float32),
         ),
-        in_specs=[pl.BlockSpec(memory_space=pltpu.SMEM)] + whole(6),
+        in_specs=[pl.BlockSpec(memory_space=pltpu.SMEM)] + whole(7),
         out_specs=tuple(whole(3)),
-        scratch_shapes=[pltpu.VMEM((rows, final.shape[0]), jnp.bfloat16)],
+        scratch_shapes=[pltpu.VMEM((own.shape[0], final.shape[0]), jnp.bfloat16)],
         compiler_params=params(24),
         name="outer_product_entry",
-    )(core, flanks, other, mixed, coupling, final, entry)
+    )(core, flanks, other, own, mixed, coupling, final, entry)
 
 
 def spread_kernel(final_ref, block_ref, wide_ref):
@@ -302,11 +330,14 @@
     entry_ref,
     average_ref,
     project_ref,
+    focus_ref,
     sides_ref,
     left_ref,
     right_ref,
     turned_ref,
+    near_focus_ref,
 ):
+    near_focus_ref[...] = focus_ref[...]
     turned_ref[...] = project_ref[...].astype(jnp.float32).T.astype(jnp.bfloat16)
     channels = average_ref.shape[1] // 2
     for ref, first, lane_of in (
@@ -328,7 +359,7 @@
         sides_ref[d] = entry_ref[d].astype(jnp.float32).T.astype(jnp.bfloat16)
 
 
-def prepare_call(entries, average, project):
+def prepare_call(entries, average, project, focus):
     depth = average.shape[1] // 2
     width = entries.shape[1]
     return pl.pallas_call(
@@ -338,12 +369,13 @@
             jax.ShapeDtypeStruct((128 // depth, average.shape[0], 128), jnp.bfloat16),
             jax.ShapeDtypeStruct((8, average.shape[0], 8 * depth), jnp.bfloat16),
             jax.ShapeDtypeStruct(project.shape[::-1], jnp.bfloat16),
+            jax.ShapeDtypeStruct(focus.shape, jnp.bfloat16),
         ),
-        in_specs=whole(3),
-        out_specs=tuple(whole(4)),
+        in_specs=whole(4),
+        out_specs=tuple(whole(5)),
         compiler_params=params(),
         name="prepare_weights",
-    )(entries, average, project)
+    )(entries, average, project, focus)
 
 
 def pack_kernel(
@@ -582,9 +614,10 @@
     )(arrived, other, *projected, final, left, right)
 
 
-def pair_track(core, flanks, other, mixed, coupling, final, prepared, exits):
+def pair_track(core, flanks, other, mixed, coupling, final, prepared, exits, flat):
     sides = prepared[0]
-    pair, edges, gate = opm_call(core, flanks, other, mixed, coupling, final, sides)
+    own = own_call(flanks, final, flat, coupling.shape[1] // 2)
+    pair, edges, gate = opm_call(core, flanks, other, own, mixed, coupling, final, sides, flat)
     for d in range(2):
         arrived = exchange(edges)
         product = product_call(arrived, d == 1)
@@ -657,14 +690,17 @@
         and tensor_depth == 32
     )
     if fits:
-        prepared = prepare_call(trilateral_entry_matrix, tensor_average_matrix, query_key_matrix)
+        prepared = prepare_call(
+            trilateral_entry_matrix,
+            tensor_average_matrix,
+            query_key_matrix,
+            focus_final_matrix,
+        )
         packed = pack_call(alignment_embedding, coupling_embedding, coupling_logit_matrix, count)
         arrived = exchange(packed)
         other = across(arrived[:, -1], 1)
         projected = project_call(arrived, prepared[3])
-        mixed, flanks = attend_call(
-            arrived, other, projected, width, focus_final_matrix, *prepared[1:3]
-        )
+        mixed, flanks = attend_call(arrived, other, projected, width, prepared[4], *prepared[1:3])
         flanks = exchange(flanks)
         flanks = flanks.reshape(chain_tally, -1)
         other = across(flanks, 1)
@@ -678,6 +714,7 @@
             final,
             prepared,
             trilateral_exit_matrix,
+            local_strands * tensor_depth,
         )
 
     rows = exchange(alignment_embedding).reshape(count, per_device, local_strands, depth)

time: 146 us -> 147 us (level)
  local copies, waits for them, and re-layouts: 7.05 us -> 9.05 us
    unnamed x17 -> x19, local copies, waits for them, and re-layouts: 7.03 us -> 9.03 us
    pallas_call x1 -> x2, Pallas kernels: 2.77 us -> 3.08 us  [the longest x1 2.02 us: opm_call(): pl.pallas_call(lambda *refs: opm_kernel(flat, *refs), out_shape=(jax.Shap...]
  transfers between devices with their start and end apart: 2 -> 2, of which waited for: 0 -> 0; matrix products, arithmetic and copies ran while one was open for 1% -> 1% of each run, Pallas kernels for 1% -> 2%
where the time goes in v4:
time: 147 us
  blocking collectives  121 us (82%)
  Pallas kernels  14.9 us (10%)
  local copies, waits for them, and re-layouts  9.05 us (6%)
    all_to_all x6, blocking collectives, exchange(): lax.all_to_all(blocks, 'res', split_axis=0, concat_axis=0, tiled=True)  121 us
    unnamed x19, local copies, waits for them, and re-layouts  9.03 us
    pallas_call x1, Pallas kernels, attend_call(): pl.pallas_call(lambda *refs: attend_kernel(width, *refs), out_shape=(jax....  4.18 us
  transfers between devices with their start and end apart: 2, of which 0 were waited for; matrix products, arithmetic and copies ran while one was open for 1% of the time, Pallas kernels for 2%

profile of v4, /device:TPU:0, one launch (start us, length us, event | category | flops | bytes accessed | tf_op | source)
XLA Modules:
  0.0 146.8 jit_solution(17704515809272188919)
XLA Ops:
  0.6 2.4 %pack_rows.1 = bf16[16,3,8,8,128]{4,3,2,1,0:T(8,128)(2,1)S(1)} custom-call(bf16[16,8,8,256]{3,2,1,0:T(8,128)(2,1)} %bitcast.12, bf16[8,128,128]{2,1,0:T(8,128)(2,1)} %refs_5_.1, bf16[8,128]{1,0:T(8,128)(2,1)} %bitcast.13), custom_call_target="tpu_custom_call" | custom-call | tf_op jit(solution)/shard_map/pack_rows/pallas_call | solution.py:426
  3.0 27.3 %all_to_all.30.arrived_ref.refs_0_ = bf16[16,3,8,8,128]{4,3,2,1,0:T(8,128)(2,1)S(1)} all-to-all(bf16[16,3,8,8,128]{4,3,2,1,0:T(8,128)(2,1)S(1)} %pack_rows.1), channel_id=1, replica_groups=mesh['grp'=2,'res'=16] {'res'}, dimensions={0} | all-to-all | bytes 1572864 | tf_op jit(solution)/shard_map/all_to_all | solution.py:22
  30.4 1.0 collective-permute-start
  31.4 0.9 copy.16.average_ref
  32.3 0.0 copy-start.4
  32.3 1.0 copy-done.4
  33.3 0.0 copy-start.5
  33.3 1.0 copy-done.5
  34.3 0.0 copy-start.8
  34.3 0.9 copy-done.8
  35.2 0.0 copy-start.6
  35.2 0.5 prepare_weights.1
  35.7 1.0 project_rows.1
  36.7 0.0 collective-permute-done.refs_1_
  36.7 4.2 %attend_rows.1 = (bf16[16,8,8,256]{3,2,1,0:T(8,128)(2,1)S(1)}, bf16[16,8,2304]{2,1,0:T(8,128)(2,1)S(1)}) custom-call(bf16[16,3,8,8,128]{4,3,2,1,0:T(8,128)(2,1)S(1)} %all_to_all.30.arrived_ref.refs_0_, bf16[16,8,8,128]{3,2,1,0:T(8,128)(2,1)S(1)} %collective-permute-done.refs_1_, bf16[8,256,128]{2,1,0:T(8,128)(2,1)S(1)} %get-tuple-element.21.refs_2_, ...), custom_call_target="tpu_custom_call" | custom-call | tf_op jit(solution)/shard_map/attend_rows/pallas_call | solution.py:599
  40.8 20.4 %all_to_all.31 = bf16[16,8,2304]{2,1,0:T(8,128)(2,1)S(1)} all-to-all(bf16[16,8,2304]{2,1,0:T(8,128)(2,1)S(1)} %get-tuple-element.28), channel_id=1, replica_groups=mesh['grp'=2,'res'=16] {'res'}, dimensions={0} | all-to-all | bytes 1179648 | tf_op jit(solution)/shard_map/all_to_all | solution.py:22
  61.3 0.1 collective-permute-start.1
  61.4 0.0 copy-done.6
  61.4 0.0 copy-start.3
  61.4 0.7 spread_weight.1.refs_1_.refs_6_
  62.1 0.0 copy-start
  62.1 1.9 %copy-done = bf16[4096,512]{1,0:T(8,128)(2,1)} copy-done((bf16[4096,512]{1,0:T(8,128)(2,1)}, bf16[4096,512]{1,0:T(8,128)(2,1)S(1)}, u32[]{:S(2)}) %copy-start) | copy-done | bytes 4194328
  64.1 0.0 copy-start.1
  64.1 2.2 %copy-done.1 = bf16[4096,512]{1,0:T(8,128)(2,1)S(1)} copy-done((bf16[4096,512]{1,0:T(8,128)(2,1)S(1)}, bf16[4096,512]{1,0:T(8,128)(2,1)}, u32[]{:S(2)}) %copy-start.1) | copy-done | bytes 4194328
  66.3 0.0 copy-start.2
  66.3 1.1 outer_product_own.1.refs_3_
  67.3 0.0 collective-permute-done.1.refs_2_
  67.3 0.0 copy-done.3
  67.3 1.1 copy-done.2
  68.4 0.0 copy-start.7
  68.5 2.0 %outer_product_entry.1 = (bf16[8,128,128]{2,1,0:T(8,128)(2,1)S(1)}, bf16[16,4,8,8,128]{4,3,2,1,0:T(8,128)(2,1)S(1)}, f32[8,128,128]{2,1,0:T(8,128)S(1)}) custom-call(s32[1]{0:T(128)} %bitcast.refs_0_, bf16[128,2304]{1,0:T(8,128)(2,1)S(1)} %bitcast.11, bf16[128,2304]{1,0:T(8,128)(2,1)S(1)} %collective-permute-done.1.refs_2_, ...), custom_call_target="tpu_custom_call" | custom-call | tf_op jit(solution)/shard_map/outer_product_entry/pallas_call | solution.py:285
  70.5 27.5 %all_to_all.32.refs_0_.arrived_ref = bf16[16,4,8,8,128]{4,3,2,1,0:T(8,128)(2,1)S(1)} all-to-all(bf16[16,4,8,8,128]{4,3,2,1,0:T(8,128)(2,1)S(1)} %get-tuple-element.31), channel_id=1, replica_groups=mesh['grp'=2,'res'=16] {'res'}, dimensions={0} | all-to-all | bytes 2097152 | tf_op jit(solution)/shard_map/all_to_all | solution.py:22
  98.0 0.3 edge_product.2
  98.3 14.8 %all_to_all.33.gathered_ref = bf16[16,8,8,128]{3,2,1,0:T(8,128)(2,1)S(1)} all-to-all(bf16[16,8,8,128]{3,2,1,0:T(8,128)(2,1)S(1)} %edge_product.2), channel_id=1, replica_groups=mesh['grp'=2,'res'=16] {'res'}, dimensions={0} | all-to-all | bytes 524288 | tf_op jit(solution)/shard_map/all_to_all | solution.py:22
  113.1 0.0 copy-done.7
  113.1 1.3 triangle_exit_entry.1
  114.4 16.9 %all_to_all.34.refs_0_ = bf16[16,2,8,8,128]{4,3,2,1,0:T(8,128)(2,1)S(1)} all-to-all(bf16[16,2,8,8,128]{4,3,2,1,0:T(8,128)(2,1)S(1)} %get-tuple-element.35), channel_id=1, replica_groups=mesh['grp'=2,'res'=16] {'res'}, dimensions={0} | all-to-all | bytes 1048576 | tf_op jit(solution)/shard_map/all_to_all | solution.py:22
  131.4 0.4 edge_product.3
  131.7 14.0 %all_to_all.35.gathered_ref = bf16[16,8,8,128]{3,2,1,0:T(8,128)(2,1)S(1)} all-to-all(bf16[16,8,8,128]{3,2,1,0:T(8,128)(2,1)S(1)} %edge_product.3), channel_id=1, replica_groups=mesh['grp'=2,'res'=16] {'res'}, dimensions={0} | all-to-all | bytes 524288 | tf_op jit(solution)/shard_map/all_to_all | solution.py:22
  145.7 1.1 triangle_exit.1
  (1 shorter events, 0.0 us)
Async XLA Ops:
  30.4 6.3 %collective-permute-start = (bf16[16,8,8,128]{3,2,1,0:T(8,128)(2,1)S(1)}, bf16[16,8,8,128]{3,2,1,0:T(8,128)(2,1)S(1)}, u32[]{:S(2)}, u32[]{:S(2)}) collective-permute-start(bf16[16,8,8,128]{3,2,1,0:T(8,128)(2,1)S(1)} %slice_bitcast_fusion), channel_id=1, source_target_pairs={{0,1},{1,0},{2,3},{3,2},{4,5},{5,4},{6,7},{7,6},{8,9},{9,8},{10,11... | collective-permute-start | bytes 786440 | tf_op jit(solution)/shard_map/ppermute | solution.py:27
  32.3 1.0 copy-start.4
  33.3 1.0 copy-start.5
  34.3 0.9 copy-start.8
  35.2 26.2 %copy-start.6 = (bf16[1024,128]{1,0:T(8,128)(2,1)S(1)}, bf16[1024,128]{1,0:T(8,128)(2,1)}, u32[]{:S(2)}) copy-start(bf16[1024,128]{1,0:T(8,128)(2,1)} %final_ref.1) | copy-start | bytes 786436
  61.3 6.1 %collective-permute-start.1 = (bf16[128,2304]{1,0:T(8,128)(2,1)S(1)}, bf16[128,2304]{1,0:T(8,128)(2,1)S(1)}, u32[]{:S(2)}, u32[]{:S(2)}) collective-permute-start(bf16[128,2304]{1,0:T(8,128)(2,1)S(1)} %bitcast.9), channel_id=1, source_target_pairs={{0,1},{1,0},{2,3},{3,2},{4,5},{5,4},{6,7},{7,6},{8,9},{9,8},{10,11... | collective-permute-start | bytes 1769480 | tf_op jit(solution)/shard_map/ppermute | solution.py:27
  61.4 5.9 %copy-start.3 = (bf16[8,128,128]{2,1,0:T(8,128)(2,1)S(1)}, bf16[8,128,128]{2,1,0:T(8,128)(2,1)}, u32[]{:S(2)}) copy-start(bf16[8,128,128]{2,1,0:T(8,128)(2,1)} %refs_5_.1) | copy-start | bytes 786436
  62.1 2.0 %copy-start = (bf16[4096,512]{1,0:T(8,128)(2,1)}, bf16[4096,512]{1,0:T(8,128)(2,1)S(1)}, u32[]{:S(2)}) copy-start(bf16[4096,512]{1,0:T(8,128)(2,1)S(1)} %spread_weight.1.refs_1_.refs_6_) | copy-start | bytes 12582916
  64.1 2.2 %copy-start.1 = (bf16[4096,512]{1,0:T(8,128)(2,1)S(1)}, bf16[4096,512]{1,0:T(8,128)(2,1)}, u32[]{:S(2)}) copy-start(bf16[4096,512]{1,0:T(8,128)(2,1)} %copy-done) | copy-start | bytes 12582916
  66.3 2.2 %copy-start.2 = (bf16[4096,512]{1,0:T(8,128)(2,1)S(1)}, bf16[4096,512]{1,0:T(8,128)(2,1)}, u32[]{:S(2)}) copy-start(bf16[4096,512]{1,0:T(8,128)(2,1)} %copy-done) | copy-start | bytes 12582916
  68.4 44.7 %copy-start.7 = (bf16[2,128,128]{2,1,0:T(8,128)(2,1)S(1)}, bf16[2,128,128]{2,1,0:T(8,128)(2,1)}, u32[]{:S(2)}) copy-start(bf16[2,128,128]{2,1,0:T(8,128)(2,1)} %exit_ref.3) | copy-start | bytes 196612

commit v5 on v4

--- a/solution.py
+++ b/solution.py
@@ -545,20 +545,20 @@
         mixed_ref[:, s] = mixed.reshape(count, strands, depth).astype(jnp.bfloat16)
 
     steps = [(s, h) for s in range(chains) for h in range(heads)]
-    ahead = 2
+    ahead, lag = 4, 3
     scores = {n: score(*steps[n]) for n in range(ahead)}
     weighed, attended = {}, []
-    for n in range(len(steps) + 1):
+    for n in range(len(steps) + lag):
         if n + ahead < len(steps):
             scores[n + ahead] = score(*steps[n + ahead])
         if n < len(steps):
             weighed[n] = weigh(scores.pop(n), steps[n][1])
-        if n:
-            s, h = steps[n - 1]
+        if n >= lag:
+            s, h = steps[n - lag]
             attended.append(
                 jnp.dot(
                     value_ref[s, h * width : (h + 1) * width],
-                    weighed.pop(n - 1),
+                    weighed.pop(n - lag),
                     preferred_element_type=jnp.float32,
                 )
             )

time: 147 us -> 147 us (level)
  no operation moved by 1% of the time
where the time goes in v5:
time: 147 us; the launch traced here: 146 us
  blocking collectives  121 us (82%)
  Pallas kernels  14.1 us (10%)
  local copies, waits for them, and re-layouts  9.05 us (6%)
    all_to_all x6, blocking collectives, exchange(): lax.all_to_all(blocks, 'res', split_axis=0, concat_axis=0, tiled=True)  121 us
    unnamed x19, local copies, waits for them, and re-layouts  9.03 us
    pallas_call x1, Pallas kernels, attend_call(): pl.pallas_call(lambda *refs: attend_kernel(width, *refs), out_shape=(jax....  3.43 us
  transfers between devices with their start and end apart: 2, of which 0 were waited for; matrix products, arithmetic and copies ran while one was open for 1% of the time, Pallas kernels for 2%

profile of v5, /device:TPU:0, one launch (start us, length us, event | category | flops | bytes accessed | tf_op | source)
XLA Modules:
  0.0 146.1 jit_solution(17689400066807225738)
XLA Ops:
  0.6 2.4 %pack_rows.1 = bf16[16,3,8,8,128]{4,3,2,1,0:T(8,128)(2,1)S(1)} custom-call(bf16[16,8,8,256]{3,2,1,0:T(8,128)(2,1)} %bitcast.12, bf16[8,128,128]{2,1,0:T(8,128)(2,1)} %refs_5_.1, bf16[8,128]{1,0:T(8,128)(2,1)} %bitcast.13), custom_call_target="tpu_custom_call" | custom-call | tf_op jit(solution)/shard_map/pack_rows/pallas_call | solution.py:426
  3.0 27.3 %all_to_all.30.arrived_ref.refs_0_ = bf16[16,3,8,8,128]{4,3,2,1,0:T(8,128)(2,1)S(1)} all-to-all(bf16[16,3,8,8,128]{4,3,2,1,0:T(8,128)(2,1)S(1)} %pack_rows.1), channel_id=1, replica_groups=mesh['grp'=2,'res'=16] {'res'}, dimensions={0} | all-to-all | bytes 1572864 | tf_op jit(solution)/shard_map/all_to_all | solution.py:22
  30.4 1.0 collective-permute-start
  31.4 0.9 copy.16.average_ref
  32.3 0.0 copy-start.4
  32.3 1.0 copy-done.4
  33.3 0.0 copy-start.5
  33.3 1.0 copy-done.5
  34.3 0.0 copy-start.8
  34.3 0.9 copy-done.8
  35.2 0.0 copy-start.6
  35.2 0.5 prepare_weights.1
  35.7 1.0 project_rows.1
  36.7 0.0 collective-permute-done.refs_1_
  36.7 3.4 %attend_rows.1 = (bf16[16,8,8,256]{3,2,1,0:T(8,128)(2,1)S(1)}, bf16[16,8,2304]{2,1,0:T(8,128)(2,1)S(1)}) custom-call(bf16[16,3,8,8,128]{4,3,2,1,0:T(8,128)(2,1)S(1)} %all_to_all.30.arrived_ref.refs_0_, bf16[16,8,8,128]{3,2,1,0:T(8,128)(2,1)S(1)} %collective-permute-done.refs_1_, bf16[8,256,128]{2,1,0:T(8,128)(2,1)S(1)} %get-tuple-element.21.refs_2_, ...), custom_call_target="tpu_custom_call" | custom-call | tf_op jit(solution)/shard_map/attend_rows/pallas_call | solution.py:599
  40.1 20.4 %all_to_all.31 = bf16[16,8,2304]{2,1,0:T(8,128)(2,1)S(1)} all-to-all(bf16[16,8,2304]{2,1,0:T(8,128)(2,1)S(1)} %get-tuple-element.28), channel_id=1, replica_groups=mesh['grp'=2,'res'=16] {'res'}, dimensions={0} | all-to-all | bytes 1179648 | tf_op jit(solution)/shard_map/all_to_all | solution.py:22
  60.5 0.1 collective-permute-start.1
  60.6 0.0 copy-done.6
  60.6 0.0 copy-start.3
  60.7 0.7 spread_weight.1.refs_1_.refs_6_
  61.4 0.0 copy-start
  61.4 1.9 %copy-done = bf16[4096,512]{1,0:T(8,128)(2,1)} copy-done((bf16[4096,512]{1,0:T(8,128)(2,1)}, bf16[4096,512]{1,0:T(8,128)(2,1)S(1)}, u32[]{:S(2)}) %copy-start) | copy-done | bytes 4194328
  63.3 0.0 copy-start.1
  63.3 2.2 %copy-done.1 = bf16[4096,512]{1,0:T(8,128)(2,1)S(1)} copy-done((bf16[4096,512]{1,0:T(8,128)(2,1)S(1)}, bf16[4096,512]{1,0:T(8,128)(2,1)}, u32[]{:S(2)}) %copy-start.1) | copy-done | bytes 4194328
  65.5 0.0 copy-start.2
  65.5 1.1 outer_product_own.1.refs_3_
  66.6 0.0 collective-permute-done.1.refs_2_
  66.6 0.0 copy-done.3
  66.6 1.1 copy-done.2
  67.7 0.0 copy-start.7
  67.7 2.0 %outer_product_entry.1 = (bf16[8,128,128]{2,1,0:T(8,128)(2,1)S(1)}, bf16[16,4,8,8,128]{4,3,2,1,0:T(8,128)(2,1)S(1)}, f32[8,128,128]{2,1,0:T(8,128)S(1)}) custom-call(s32[1]{0:T(128)} %bitcast.refs_0_, bf16[128,2304]{1,0:T(8,128)(2,1)S(1)} %bitcast.11, bf16[128,2304]{1,0:T(8,128)(2,1)S(1)} %collective-permute-done.1.refs_2_, ...), custom_call_target="tpu_custom_call" | custom-call | tf_op jit(solution)/shard_map/outer_product_entry/pallas_call | solution.py:285
  69.7 27.5 %all_to_all.32.refs_0_.arrived_ref = bf16[16,4,8,8,128]{4,3,2,1,0:T(8,128)(2,1)S(1)} all-to-all(bf16[16,4,8,8,128]{4,3,2,1,0:T(8,128)(2,1)S(1)} %get-tuple-element.31), channel_id=1, replica_groups=mesh['grp'=2,'res'=16] {'res'}, dimensions={0} | all-to-all | bytes 2097152 | tf_op jit(solution)/shard_map/all_to_all | solution.py:22
  97.2 0.3 edge_product.2
  97.6 14.8 %all_to_all.33.gathered_ref = bf16[16,8,8,128]{3,2,1,0:T(8,128)(2,1)S(1)} all-to-all(bf16[16,8,8,128]{3,2,1,0:T(8,128)(2,1)S(1)} %edge_product.2), channel_id=1, replica_groups=mesh['grp'=2,'res'=16] {'res'}, dimensions={0} | all-to-all | bytes 524288 | tf_op jit(solution)/shard_map/all_to_all | solution.py:22
  112.4 0.0 copy-done.7
  112.4 1.3 triangle_exit_entry.1
  113.7 16.9 %all_to_all.34.refs_0_ = bf16[16,2,8,8,128]{4,3,2,1,0:T(8,128)(2,1)S(1)} all-to-all(bf16[16,2,8,8,128]{4,3,2,1,0:T(8,128)(2,1)S(1)} %get-tuple-element.35), channel_id=1, replica_groups=mesh['grp'=2,'res'=16] {'res'}, dimensions={0} | all-to-all | bytes 1048576 | tf_op jit(solution)/shard_map/all_to_all | solution.py:22
  130.6 0.4 edge_product.3
  131.0 14.0 %all_to_all.35.gathered_ref = bf16[16,8,8,128]{3,2,1,0:T(8,128)(2,1)S(1)} all-to-all(bf16[16,8,8,128]{3,2,1,0:T(8,128)(2,1)S(1)} %edge_product.3), channel_id=1, replica_groups=mesh['grp'=2,'res'=16] {'res'}, dimensions={0} | all-to-all | bytes 524288 | tf_op jit(solution)/shard_map/all_to_all | solution.py:22
  145.0 1.1 triangle_exit.1
  (1 shorter events, 0.0 us)
Async XLA Ops:
  30.4 6.3 %collective-permute-start = (bf16[16,8,8,128]{3,2,1,0:T(8,128)(2,1)S(1)}, bf16[16,8,8,128]{3,2,1,0:T(8,128)(2,1)S(1)}, u32[]{:S(2)}, u32[]{:S(2)}) collective-permute-start(bf16[16,8,8,128]{3,2,1,0:T(8,128)(2,1)S(1)} %slice_bitcast_fusion), channel_id=1, source_target_pairs={{0,1},{1,0},{2,3},{3,2},{4,5},{5,4},{6,7},{7,6},{8,9},{9,8},{10,11... | collective-permute-start | bytes 786440 | tf_op jit(solution)/shard_map/ppermute | solution.py:27
  32.3 1.0 copy-start.4
  33.3 1.0 copy-start.5
  34.3 0.9 copy-start.8
  35.2 25.5 %copy-start.6 = (bf16[1024,128]{1,0:T(8,128)(2,1)S(1)}, bf16[1024,128]{1,0:T(8,128)(2,1)}, u32[]{:S(2)}) copy-start(bf16[1024,128]{1,0:T(8,128)(2,1)} %final_ref.1) | copy-start | bytes 786436
  60.5 6.1 %collective-permute-start.1 = (bf16[128,2304]{1,0:T(8,128)(2,1)S(1)}, bf16[128,2304]{1,0:T(8,128)(2,1)S(1)}, u32[]{:S(2)}, u32[]{:S(2)}) collective-permute-start(bf16[128,2304]{1,0:T(8,128)(2,1)S(1)} %bitcast.9), channel_id=1, source_target_pairs={{0,1},{1,0},{2,3},{3,2},{4,5},{5,4},{6,7},{7,6},{8,9},{9,8},{10,11... | collective-permute-start | bytes 1769480 | tf_op jit(solution)/shard_map/ppermute | solution.py:27
  60.6 5.9 %copy-start.3 = (bf16[8,128,128]{2,1,0:T(8,128)(2,1)S(1)}, bf16[8,128,128]{2,1,0:T(8,128)(2,1)}, u32[]{:S(2)}) copy-start(bf16[8,128,128]{2,1,0:T(8,128)(2,1)} %refs_5_.1) | copy-start | bytes 786436
  61.4 2.0 %copy-start = (bf16[4096,512]{1,0:T(8,128)(2,1)}, bf16[4096,512]{1,0:T(8,128)(2,1)S(1)}, u32[]{:S(2)}) copy-start(bf16[4096,512]{1,0:T(8,128)(2,1)S(1)} %spread_weight.1.refs_1_.refs_6_) | copy-start | bytes 12582916
  63.3 2.2 %copy-start.1 = (bf16[4096,512]{1,0:T(8,128)(2,1)S(1)}, bf16[4096,512]{1,0:T(8,128)(2,1)}, u32[]{:S(2)}) copy-start(bf16[4096,512]{1,0:T(8,128)(2,1)} %copy-done) | copy-start | bytes 12582916
  65.5 2.2 %copy-start.2 = (bf16[4096,512]{1,0:T(8,128)(2,1)S(1)}, bf16[4096,512]{1,0:T(8,128)(2,1)}, u32[]{:S(2)}) copy-start(bf16[4096,512]{1,0:T(8,128)(2,1)} %copy-done) | copy-start | bytes 12582916
  67.7 44.7 %copy-start.7 = (bf16[2,128,128]{2,1,0:T(8,128)(2,1)S(1)}, bf16[2,128,128]{2,1,0:T(8,128)(2,1)}, u32[]{:S(2)}) copy-start(bf16[2,128,128]{2,1,0:T(8,128)(2,1)} %exit_ref.3) | copy-start | bytes 196612

commit v6 on v5

--- a/solution.py
+++ b/solution.py
@@ -184,10 +184,17 @@
     )(gathered, weight, pair_prev, gate, entry, arrived)
 
 
-def exit_kernel(gathered_ref, exit_ref, pair_ref, gate_ref, out_ref, spread_ref):
-    new_row = exit_rows(1, gathered_ref, exit_ref, pair_ref, gate_ref, out_ref, spread_ref)
+def exit_kernel(gathered_ref, exit_ref, pair_ref, gate_ref, out_ref, near_ref, spread_ref, sems):
+    new_row = exit_rows(1, gathered_ref, exit_ref, pair_ref, gate_ref, near_ref, spread_ref)
+    copies = []
     for r in range(pair_ref.shape[0]):
         new_row(r)
+        if r % 2:
+            at = pl.ds(r - 1, 2)
+            copies.append(pltpu.make_async_copy(near_ref.at[at], out_ref.at[at], sems.at[r // 2]))
+            copies[-1].start()
+    for copy in copies:
+        copy.wait()
 
 
 def exit_call(gathered, weight, pair_prev, gate):
@@ -196,8 +203,12 @@
         exit_kernel,
         out_shape=jax.ShapeDtypeStruct(pair_prev.shape, jnp.bfloat16),
         in_specs=whole(4),
-        out_specs=pl.BlockSpec(memory_space=pltpu.VMEM),
-        scratch_shapes=[pltpu.VMEM((count * share * strands, lanes), jnp.float32)],
+        out_specs=pl.BlockSpec(memory_space=pltpu.HBM),
+        scratch_shapes=[
+            pltpu.VMEM(pair_prev.shape, jnp.bfloat16),
+            pltpu.VMEM((count * share * strands, lanes), jnp.float32),
+            pltpu.SemaphoreType.DMA((strands // 2,)),
+        ],
         compiler_params=params(),
         name="triangle_exit",
     )(gathered, weight, pair_prev, gate)
@@ -257,12 +268,19 @@
     edges_ref,
     gate_ref,
     outer_ref,
+    sems,
 ):
     _, total_res, width = coupling_ref.shape
     groups = final_ref.shape[1] // width
     half = total_res // 2
-    for k in range(edges_ref.shape[1] - 2):
-        edges_ref[:, 2 + k] = mixed_ref[:, :, :, k * 128 : (k + 1) * 128]
+    copies = [
+        pltpu.make_async_copy(
+            mixed_ref.at[:, :, :, pl.ds(k * 128, 128)], edges_ref.at[:, 2 + k], sems.at[k]
+        )
+        for k in range(edges_ref.shape[1] - 2)
+    ]
+    for copy in copies:
+        copy.start()
     first = core_ref[0] == 0
     product = half_product(other_ref, flanks_ref[:, :flat], final_ref, outer_ref)
 
@@ -276,6 +294,8 @@
         return new.astype(jnp.float32)
 
     edges_in_turn(new_row, entry_ref.at[0], edges_ref, gate_ref)
+    for copy in copies:
+        copy.wait()
 
 
 def opm_call(core, flanks, other, own, mixed, coupling, final, entry, flat):
@@ -293,7 +313,10 @@
         ),
         in_specs=[pl.BlockSpec(memory_space=pltpu.SMEM)] + whole(7),
         out_specs=tuple(whole(3)),
-        scratch_shapes=[pltpu.VMEM((own.shape[0], final.shape[0]), jnp.bfloat16)],
+        scratch_shapes=[
+            pltpu.VMEM((own.shape[0], final.shape[0]), jnp.bfloat16),
+            pltpu.SemaphoreType.DMA((depth // 128,)),
+        ],
         compiler_params=params(24),
         name="outer_product_entry",
     )(core, flanks, other, own, mixed, coupling, final, entry)
@@ -545,7 +568,7 @@
         mixed_ref[:, s] = mixed.reshape(count, strands, depth).astype(jnp.bfloat16)
 
     steps = [(s, h) for s in range(chains) for h in range(heads)]
-    ahead, lag = 4, 3
+    ahead, lag = 6, 4
     scores = {n: score(*steps[n]) for n in range(ahead)}
     weighed, attended = {}, []
     for n in range(len(steps) + lag):

time: 147 us -> 147 us (level)
  no operation moved by 1% of the time
where the time goes in v6:
time: 147 us; the launch traced here: 146 us
  blocking collectives  121 us (82%)
  Pallas kernels  14.1 us (10%)
  local copies, waits for them, and re-layouts  9.05 us (6%)
    all_to_all x6, blocking collectives, exchange(): lax.all_to_all(blocks, 'res', split_axis=0, concat_axis=0, tiled=True)  121 us
    unnamed x19, local copies, waits for them, and re-layouts  9.03 us
    pallas_call x1, Pallas kernels, attend_call(): pl.pallas_call(lambda *refs: attend_kernel(width, *refs), out_shape=(jax....  3.41 us
  transfers between devices with their start and end apart: 2, of which 0 were waited for; matrix products, arithmetic and copies ran while one was open for 1% of the time, Pallas kernels for 2%

profile of v6, /device:TPU:0, one launch (start us, length us, event | category | flops | bytes accessed | tf_op | source)
XLA Modules:
  0.0 146.1 jit_solution(13035977090646406056)
XLA Ops:
  0.6 2.4 %pack_rows.1 = bf16[16,3,8,8,128]{4,3,2,1,0:T(8,128)(2,1)S(1)} custom-call(bf16[16,8,8,256]{3,2,1,0:T(8,128)(2,1)} %bitcast.12, bf16[8,128,128]{2,1,0:T(8,128)(2,1)} %refs_5_.1, bf16[8,128]{1,0:T(8,128)(2,1)} %bitcast.13), custom_call_target="tpu_custom_call" | custom-call | tf_op jit(solution)/shard_map/pack_rows/pallas_call | solution.py:449
  3.0 27.3 %all_to_all.30.arrived_ref.refs_0_ = bf16[16,3,8,8,128]{4,3,2,1,0:T(8,128)(2,1)S(1)} all-to-all(bf16[16,3,8,8,128]{4,3,2,1,0:T(8,128)(2,1)S(1)} %pack_rows.1), channel_id=1, replica_groups=mesh['grp'=2,'res'=16] {'res'}, dimensions={0} | all-to-all | bytes 1572864 | tf_op jit(solution)/shard_map/all_to_all | solution.py:22
  30.4 1.0 collective-permute-start
  31.4 0.9 copy.16.average_ref
  32.3 0.0 copy-start.4
  32.3 1.0 copy-done.4
  33.3 0.0 copy-start.5
  33.3 1.0 copy-done.5
  34.3 0.0 copy-start.8
  34.3 0.9 copy-done.8
  35.2 0.0 copy-start.6
  35.2 0.5 prepare_weights.1
  35.7 1.0 project_rows.1
  36.7 0.0 collective-permute-done.refs_1_
  36.7 3.4 %attend_rows.1 = (bf16[16,8,8,256]{3,2,1,0:T(8,128)(2,1)S(1)}, bf16[16,8,2304]{2,1,0:T(8,128)(2,1)S(1)}) custom-call(bf16[16,3,8,8,128]{4,3,2,1,0:T(8,128)(2,1)S(1)} %all_to_all.30.arrived_ref.refs_0_, bf16[16,8,8,128]{3,2,1,0:T(8,128)(2,1)S(1)} %collective-permute-done.refs_1_, bf16[8,256,128]{2,1,0:T(8,128)(2,1)S(1)} %get-tuple-element.21.refs_2_, ...), custom_call_target="tpu_custom_call" | custom-call | tf_op jit(solution)/shard_map/attend_rows/pallas_call | solution.py:622
  40.1 20.4 %all_to_all.31 = bf16[16,8,2304]{2,1,0:T(8,128)(2,1)S(1)} all-to-all(bf16[16,8,2304]{2,1,0:T(8,128)(2,1)S(1)} %get-tuple-element.28), channel_id=1, replica_groups=mesh['grp'=2,'res'=16] {'res'}, dimensions={0} | all-to-all | bytes 1179648 | tf_op jit(solution)/shard_map/all_to_all | solution.py:22
  60.5 0.1 collective-permute-start.1
  60.6 0.0 copy-done.6
  60.6 0.0 copy-start.3
  60.6 0.7 spread_weight.1.refs_1_.refs_6_
  61.4 0.0 copy-start
  61.4 1.9 %copy-done = bf16[4096,512]{1,0:T(8,128)(2,1)} copy-done((bf16[4096,512]{1,0:T(8,128)(2,1)}, bf16[4096,512]{1,0:T(8,128)(2,1)S(1)}, u32[]{:S(2)}) %copy-start) | copy-done | bytes 4194328
  63.3 0.0 copy-start.1
  63.3 2.2 %copy-done.1 = bf16[4096,512]{1,0:T(8,128)(2,1)S(1)} copy-done((bf16[4096,512]{1,0:T(8,128)(2,1)S(1)}, bf16[4096,512]{1,0:T(8,128)(2,1)}, u32[]{:S(2)}) %copy-start.1) | copy-done | bytes 4194328
  65.5 0.0 copy-start.2
  65.5 1.1 outer_product_own.1.refs_3_
  66.6 0.0 collective-permute-done.1.refs_2_
  66.6 0.0 copy-done.3
  66.6 1.1 copy-done.2
  67.7 0.0 copy-start.7
  67.7 2.1 %outer_product_entry.1 = (bf16[8,128,128]{2,1,0:T(8,128)(2,1)S(1)}, bf16[16,4,8,8,128]{4,3,2,1,0:T(8,128)(2,1)S(1)}, f32[8,128,128]{2,1,0:T(8,128)S(1)}) custom-call(s32[1]{0:T(128)} %bitcast.refs_0_, bf16[128,2304]{1,0:T(8,128)(2,1)S(1)} %bitcast.11, bf16[128,2304]{1,0:T(8,128)(2,1)S(1)} %collective-permute-done.1.refs_2_, ...), custom_call_target="tpu_custom_call" | custom-call | tf_op jit(solution)/shard_map/outer_product_entry/pallas_call | solution.py:305
  69.8 27.5 %all_to_all.32.refs_0_.arrived_ref = bf16[16,4,8,8,128]{4,3,2,1,0:T(8,128)(2,1)S(1)} all-to-all(bf16[16,4,8,8,128]{4,3,2,1,0:T(8,128)(2,1)S(1)} %get-tuple-element.31), channel_id=1, replica_groups=mesh['grp'=2,'res'=16] {'res'}, dimensions={0} | all-to-all | bytes 2097152 | tf_op jit(solution)/shard_map/all_to_all | solution.py:22
  97.2 0.3 edge_product.2
  97.6 14.8 %all_to_all.33.gathered_ref = bf16[16,8,8,128]{3,2,1,0:T(8,128)(2,1)S(1)} all-to-all(bf16[16,8,8,128]{3,2,1,0:T(8,128)(2,1)S(1)} %edge_product.2), channel_id=1, replica_groups=mesh['grp'=2,'res'=16] {'res'}, dimensions={0} | all-to-all | bytes 524288 | tf_op jit(solution)/shard_map/all_to_all | solution.py:22
  112.4 0.0 copy-done.7
  112.4 1.3 triangle_exit_entry.1
  113.7 17.0 %all_to_all.34.refs_0_ = bf16[16,2,8,8,128]{4,3,2,1,0:T(8,128)(2,1)S(1)} all-to-all(bf16[16,2,8,8,128]{4,3,2,1,0:T(8,128)(2,1)S(1)} %get-tuple-element.35), channel_id=1, replica_groups=mesh['grp'=2,'res'=16] {'res'}, dimensions={0} | all-to-all | bytes 1048576 | tf_op jit(solution)/shard_map/all_to_all | solution.py:22
  130.6 0.4 edge_product.3
  131.0 14.0 %all_to_all.35.gathered_ref = bf16[16,8,8,128]{3,2,1,0:T(8,128)(2,1)S(1)} all-to-all(bf16[16,8,8,128]{3,2,1,0:T(8,128)(2,1)S(1)} %edge_product.3), channel_id=1, replica_groups=mesh['grp'=2,'res'=16] {'res'}, dimensions={0} | all-to-all | bytes 524288 | tf_op jit(solution)/shard_map/all_to_all | solution.py:22
  145.0 1.1 triangle_exit.1
  (1 shorter events, 0.0 us)
Async XLA Ops:
  30.4 6.3 %collective-permute-start = (bf16[16,8,8,128]{3,2,1,0:T(8,128)(2,1)S(1)}, bf16[16,8,8,128]{3,2,1,0:T(8,128)(2,1)S(1)}, u32[]{:S(2)}, u32[]{:S(2)}) collective-permute-start(bf16[16,8,8,128]{3,2,1,0:T(8,128)(2,1)S(1)} %slice_bitcast_fusion), channel_id=1, source_target_pairs={{0,1},{1,0},{2,3},{3,2},{4,5},{5,4},{6,7},{7,6},{8,9},{9,8},{10,11... | collective-permute-start | bytes 786440 | tf_op jit(solution)/shard_map/ppermute | solution.py:27
  32.3 1.0 copy-start.4
  33.3 1.0 copy-start.5
  34.3 0.9 copy-start.8
  35.2 25.5 %copy-start.6 = (bf16[1024,128]{1,0:T(8,128)(2,1)S(1)}, bf16[1024,128]{1,0:T(8,128)(2,1)}, u32[]{:S(2)}) copy-start(bf16[1024,128]{1,0:T(8,128)(2,1)} %final_ref.1) | copy-start | bytes 786436
  60.5 6.1 %collective-permute-start.1 = (bf16[128,2304]{1,0:T(8,128)(2,1)S(1)}, bf16[128,2304]{1,0:T(8,128)(2,1)S(1)}, u32[]{:S(2)}, u32[]{:S(2)}) collective-permute-start(bf16[128,2304]{1,0:T(8,128)(2,1)S(1)} %bitcast.9), channel_id=1, source_target_pairs={{0,1},{1,0},{2,3},{3,2},{4,5},{5,4},{6,7},{7,6},{8,9},{9,8},{10,11... | collective-permute-start | bytes 1769480 | tf_op jit(solution)/shard_map/ppermute | solution.py:27
  60.6 5.9 %copy-start.3 = (bf16[8,128,128]{2,1,0:T(8,128)(2,1)S(1)}, bf16[8,128,128]{2,1,0:T(8,128)(2,1)}, u32[]{:S(2)}) copy-start(bf16[8,128,128]{2,1,0:T(8,128)(2,1)} %refs_5_.1) | copy-start | bytes 786436
  61.4 2.0 %copy-start = (bf16[4096,512]{1,0:T(8,128)(2,1)}, bf16[4096,512]{1,0:T(8,128)(2,1)S(1)}, u32[]{:S(2)}) copy-start(bf16[4096,512]{1,0:T(8,128)(2,1)S(1)} %spread_weight.1.refs_1_.refs_6_) | copy-start | bytes 12582916
  63.3 2.2 %copy-start.1 = (bf16[4096,512]{1,0:T(8,128)(2,1)S(1)}, bf16[4096,512]{1,0:T(8,128)(2,1)}, u32[]{:S(2)}) copy-start(bf16[4096,512]{1,0:T(8,128)(2,1)} %copy-done) | copy-start | bytes 12582916
  65.5 2.2 %copy-start.2 = (bf16[4096,512]{1,0:T(8,128)(2,1)S(1)}, bf16[4096,512]{1,0:T(8,128)(2,1)}, u32[]{:S(2)}) copy-start(bf16[4096,512]{1,0:T(8,128)(2,1)} %copy-done) | copy-start | bytes 12582916
  67.7 44.7 %copy-start.7 = (bf16[2,128,128]{2,1,0:T(8,128)(2,1)S(1)}, bf16[2,128,128]{2,1,0:T(8,128)(2,1)}, u32[]{:S(2)}) copy-start(bf16[2,128,128]{2,1,0:T(8,128)(2,1)} %exit_ref.3) | copy-start | bytes 196612

commit v7 on v6

--- a/solution.py
+++ b/solution.py
@@ -594,13 +594,15 @@
 
     def side(weights_ref):
         group, _, lanes = weights_ref.shape
-        total = None
-        grouped = scaled.reshape(total_res // group, group, chains, depth)
-        for g in range(group):
-            part = grouped[:, g].reshape(total_res // group * chains, depth).astype(jnp.bfloat16)
-            out = jnp.dot(part, weights_ref[g], preferred_element_type=jnp.float32)
-            total = out if total is None else total + out
-        return total.reshape(total_res // group, chains, lanes).astype(jnp.bfloat16)
+        rows = total_res // group
+        grouped = scaled.reshape(rows, group, chains, depth)
+        parts = [grouped[:, g].reshape(rows * chains, depth) for g in range(group)]
+        total = jnp.dot(
+            jnp.concatenate(parts, axis=-1).astype(jnp.bfloat16),
+            weights_ref[...].reshape(group * depth, lanes),
+            preferred_element_type=jnp.float32,
+        )
+        return total.reshape(rows, chains, lanes).astype(jnp.bfloat16)
 
     left, right = side(left_ref), side(right_ref)
     lefts, rights = left.shape[0] // count, right.shape[0] // 2

time: 147 us -> 147 us (level)
  no operation moved by 1% of the time
where the time goes in v7:
time: 147 us; the launch traced here: 146 us
  blocking collectives  121 us (82%)
  Pallas kernels  14.1 us (10%)
  local copies, waits for them, and re-layouts  9.05 us (6%)
    all_to_all x6, blocking collectives, exchange(): lax.all_to_all(blocks, 'res', split_axis=0, concat_axis=0, tiled=True)  121 us
    unnamed x19, local copies, waits for them, and re-layouts  9.03 us
    pallas_call x1, Pallas kernels, attend_call(): pl.pallas_call(lambda *refs: attend_kernel(width, *refs), out_shape=(jax....  3.42 us
  transfers between devices with their start and end apart: 2, of which 0 were waited for; matrix products, arithmetic and copies ran while one was open for 1% of the time, Pallas kernels for 2%

profile of v7, /device:TPU:0, one launch (start us, length us, event | category | flops | bytes accessed | tf_op | source)
XLA Modules:
  0.0 146.1 jit_solution(13213616932293412186)
XLA Ops:
  0.6 2.4 %pack_rows.1 = bf16[16,3,8,8,128]{4,3,2,1,0:T(8,128)(2,1)S(1)} custom-call(bf16[16,8,8,256]{3,2,1,0:T(8,128)(2,1)} %bitcast.12, bf16[8,128,128]{2,1,0:T(8,128)(2,1)} %refs_5_.1, bf16[8,128]{1,0:T(8,128)(2,1)} %bitcast.13), custom_call_target="tpu_custom_call" | custom-call | tf_op jit(solution)/shard_map/pack_rows/pallas_call | solution.py:449
  3.0 27.3 %all_to_all.30.arrived_ref.refs_0_ = bf16[16,3,8,8,128]{4,3,2,1,0:T(8,128)(2,1)S(1)} all-to-all(bf16[16,3,8,8,128]{4,3,2,1,0:T(8,128)(2,1)S(1)} %pack_rows.1), channel_id=1, replica_groups=mesh['grp'=2,'res'=16] {'res'}, dimensions={0} | all-to-all | bytes 1572864 | tf_op jit(solution)/shard_map/all_to_all | solution.py:22
  30.4 1.0 collective-permute-start
  31.4 0.9 copy.16.average_ref
  32.3 0.0 copy-start.4
  32.3 1.0 copy-done.4
  33.3 0.0 copy-start.5
  33.3 1.0 copy-done.5
  34.3 0.0 copy-start.8
  34.3 0.9 copy-done.8
  35.2 0.0 copy-start.6
  35.2 0.5 prepare_weights.1
  35.7 1.0 project_rows.1
  36.7 0.0 collective-permute-done.refs_1_
  36.7 3.4 %attend_rows.1 = (bf16[16,8,8,256]{3,2,1,0:T(8,128)(2,1)S(1)}, bf16[16,8,2304]{2,1,0:T(8,128)(2,1)S(1)}) custom-call(bf16[16,3,8,8,128]{4,3,2,1,0:T(8,128)(2,1)S(1)} %all_to_all.30.arrived_ref.refs_0_, bf16[16,8,8,128]{3,2,1,0:T(8,128)(2,1)S(1)} %collective-permute-done.refs_1_, bf16[8,256,128]{2,1,0:T(8,128)(2,1)S(1)} %get-tuple-element.21.refs_2_, ...), custom_call_target="tpu_custom_call" | custom-call | tf_op jit(solution)/shard_map/attend_rows/pallas_call | solution.py:624
  40.1 20.4 %all_to_all.31 = bf16[16,8,2304]{2,1,0:T(8,128)(2,1)S(1)} all-to-all(bf16[16,8,2304]{2,1,0:T(8,128)(2,1)S(1)} %get-tuple-element.28), channel_id=1, replica_groups=mesh['grp'=2,'res'=16] {'res'}, dimensions={0} | all-to-all | bytes 1179648 | tf_op jit(solution)/shard_map/all_to_all | solution.py:22
  60.5 0.1 collective-permute-start.1
  60.6 0.0 copy-done.6
  60.6 0.0 copy-start.3
  60.6 0.7 spread_weight.1.refs_1_.refs_6_
  61.4 0.0 copy-start
  61.4 1.9 %copy-done = bf16[4096,512]{1,0:T(8,128)(2,1)} copy-done((bf16[4096,512]{1,0:T(8,128)(2,1)}, bf16[4096,512]{1,0:T(8,128)(2,1)S(1)}, u32[]{:S(2)}) %copy-start) | copy-done | bytes 4194328
  63.3 0.0 copy-start.1
  63.3 2.2 %copy-done.1 = bf16[4096,512]{1,0:T(8,128)(2,1)S(1)} copy-done((bf16[4096,512]{1,0:T(8,128)(2,1)S(1)}, bf16[4096,512]{1,0:T(8,128)(2,1)}, u32[]{:S(2)}) %copy-start.1) | copy-done | bytes 4194328
  65.5 0.0 copy-start.2
  65.5 1.1 outer_product_own.1.refs_3_
  66.6 0.0 collective-permute-done.1.refs_2_
  66.6 0.0 copy-done.3
  66.6 1.1 copy-done.2
  67.7 0.0 copy-start.7
  67.7 2.1 %outer_product_entry.1 = (bf16[8,128,128]{2,1,0:T(8,128)(2,1)S(1)}, bf16[16,4,8,8,128]{4,3,2,1,0:T(8,128)(2,1)S(1)}, f32[8,128,128]{2,1,0:T(8,128)S(1)}) custom-call(s32[1]{0:T(128)} %bitcast.refs_0_, bf16[128,2304]{1,0:T(8,128)(2,1)S(1)} %bitcast.11, bf16[128,2304]{1,0:T(8,128)(2,1)S(1)} %collective-permute-done.1.refs_2_, ...), custom_call_target="tpu_custom_call" | custom-call | tf_op jit(solution)/shard_map/outer_product_entry/pallas_call | solution.py:305
  69.8 27.5 %all_to_all.32.refs_0_.arrived_ref = bf16[16,4,8,8,128]{4,3,2,1,0:T(8,128)(2,1)S(1)} all-to-all(bf16[16,4,8,8,128]{4,3,2,1,0:T(8,128)(2,1)S(1)} %get-tuple-element.31), channel_id=1, replica_groups=mesh['grp'=2,'res'=16] {'res'}, dimensions={0} | all-to-all | bytes 2097152 | tf_op jit(solution)/shard_map/all_to_all | solution.py:22
  97.2 0.3 edge_product.2
  97.6 14.8 %all_to_all.33.gathered_ref = bf16[16,8,8,128]{3,2,1,0:T(8,128)(2,1)S(1)} all-to-all(bf16[16,8,8,128]{3,2,1,0:T(8,128)(2,1)S(1)} %edge_product.2), channel_id=1, replica_groups=mesh['grp'=2,'res'=16] {'res'}, dimensions={0} | all-to-all | bytes 524288 | tf_op jit(solution)/shard_map/all_to_all | solution.py:22
  112.4 0.0 copy-done.7
  112.4 1.3 triangle_exit_entry.1
  113.7 16.9 %all_to_all.34.refs_0_ = bf16[16,2,8,8,128]{4,3,2,1,0:T(8,128)(2,1)S(1)} all-to-all(bf16[16,2,8,8,128]{4,3,2,1,0:T(8,128)(2,1)S(1)} %get-tuple-element.35), channel_id=1, replica_groups=mesh['grp'=2,'res'=16] {'res'}, dimensions={0} | all-to-all | bytes 1048576 | tf_op jit(solution)/shard_map/all_to_all | solution.py:22
  130.6 0.4 edge_product.3
  131.0 14.0 %all_to_all.35.gathered_ref = bf16[16,8,8,128]{3,2,1,0:T(8,128)(2,1)S(1)} all-to-all(bf16[16,8,8,128]{3,2,1,0:T(8,128)(2,1)S(1)} %edge_product.3), channel_id=1, replica_groups=mesh['grp'=2,'res'=16] {'res'}, dimensions={0} | all-to-all | bytes 524288 | tf_op jit(solution)/shard_map/all_to_all | solution.py:22
  145.0 1.1 triangle_exit.1
  (1 shorter events, 0.0 us)
Async XLA Ops:
  30.4 6.3 %collective-permute-start = (bf16[16,8,8,128]{3,2,1,0:T(8,128)(2,1)S(1)}, bf16[16,8,8,128]{3,2,1,0:T(8,128)(2,1)S(1)}, u32[]{:S(2)}, u32[]{:S(2)}) collective-permute-start(bf16[16,8,8,128]{3,2,1,0:T(8,128)(2,1)S(1)} %slice_bitcast_fusion), channel_id=1, source_target_pairs={{0,1},{1,0},{2,3},{3,2},{4,5},{5,4},{6,7},{7,6},{8,9},{9,8},{10,11... | collective-permute-start | bytes 786440 | tf_op jit(solution)/shard_map/ppermute | solution.py:27
  32.3 1.0 copy-start.4
  33.3 1.0 copy-start.5
  34.3 0.9 copy-start.8
  35.2 25.5 %copy-start.6 = (bf16[1024,128]{1,0:T(8,128)(2,1)S(1)}, bf16[1024,128]{1,0:T(8,128)(2,1)}, u32[]{:S(2)}) copy-start(bf16[1024,128]{1,0:T(8,128)(2,1)} %final_ref.1) | copy-start | bytes 786436
  60.5 6.1 %collective-permute-start.1 = (bf16[128,2304]{1,0:T(8,128)(2,1)S(1)}, bf16[128,2304]{1,0:T(8,128)(2,1)S(1)}, u32[]{:S(2)}, u32[]{:S(2)}) collective-permute-start(bf16[128,2304]{1,0:T(8,128)(2,1)S(1)} %bitcast.9), channel_id=1, source_target_pairs={{0,1},{1,0},{2,3},{3,2},{4,5},{5,4},{6,7},{7,6},{8,9},{9,8},{10,11... | collective-permute-start | bytes 1769480 | tf_op jit(solution)/shard_map/ppermute | solution.py:27
  60.6 5.9 %copy-start.3 = (bf16[8,128,128]{2,1,0:T(8,128)(2,1)S(1)}, bf16[8,128,128]{2,1,0:T(8,128)(2,1)}, u32[]{:S(2)}) copy-start(bf16[8,128,128]{2,1,0:T(8,128)(2,1)} %refs_5_.1) | copy-start | bytes 786436
  61.4 2.0 %copy-start = (bf16[4096,512]{1,0:T(8,128)(2,1)}, bf16[4096,512]{1,0:T(8,128)(2,1)S(1)}, u32[]{:S(2)}) copy-start(bf16[4096,512]{1,0:T(8,128)(2,1)S(1)} %spread_weight.1.refs_1_.refs_6_) | copy-start | bytes 12582916
  63.3 2.2 %copy-start.1 = (bf16[4096,512]{1,0:T(8,128)(2,1)S(1)}, bf16[4096,512]{1,0:T(8,128)(2,1)}, u32[]{:S(2)}) copy-start(bf16[4096,512]{1,0:T(8,128)(2,1)} %copy-done) | copy-start | bytes 12582916
  65.5 2.2 %copy-start.2 = (bf16[4096,512]{1,0:T(8,128)(2,1)S(1)}, bf16[4096,512]{1,0:T(8,128)(2,1)}, u32[]{:S(2)}) copy-start(bf16[4096,512]{1,0:T(8,128)(2,1)} %copy-done) | copy-start | bytes 12582916
  67.7 44.7 %copy-start.7 = (bf16[2,128,128]{2,1,0:T(8,128)(2,1)S(1)}, bf16[2,128,128]{2,1,0:T(8,128)(2,1)}, u32[]{:S(2)}) copy-start(bf16[2,128,128]{2,1,0:T(8,128)(2,1)} %exit_ref.3) | copy-start | bytes 196612
